TPU v7x, 32 devices: a whole 2x2x4 slice. The times are simulated.
32 devices in a mesh: dp: 8 (over y, x, core), tensor: 4 (over z).
Axes of the slice: x: 2, y: 2, z: 4, core: 2. Of those that a mesh axis runs over, the one named last changes fastest.
Arguments:
- latent_in: bfloat16 [16, 1024, 1408], P('dp', 'tensor'), may hold values from -6 to 6
- skip_in: bfloat16 [16, 1024, 1408], P('dp', 'tensor'), may hold values from -6 to 6
- text_emb: bfloat16 [16, 256, 1408], P('dp'), may hold values from -6 to 6
- text_length: int32 [16], P('dp'), may hold values from 64 to 256
- time_emb: bfloat16 [16, 1408], P('dp'), may hold values from -6 to 6
- grid_pos: int32 [16, 1024, 2], P('dp'), may hold values from 0 to 31
- skip_gain: bfloat16 [2816], replicated, may hold values from 0.5 to 1.5
- skip_beta: bfloat16 [2816], replicated, may hold values from -2 to 2
- skip_weight: bfloat16 [2816, 1408], P(None, 'tensor'), may hold values from -0.109375 to 0.109375
- skip_bias: bfloat16 [1408], P('tensor'), may hold values from -2 to 2
- ada_weight: bfloat16 [1408, 1408], P(None, 'tensor'), may hold values from -0.15625 to 0.15625
- ada_bias: bfloat16 [1408], P('tensor'), may hold values from -2 to 2
- query_key_value_weight: bfloat16 [3, 1408, 1408], P(None, None, 'tensor'), may hold values from -0.15625 to 0.15625
- qk_gain: bfloat16 [2, 88], replicated, may hold values from 0.5 to 1.5
- attention_output_weight: bfloat16 [1408, 1408], P('tensor'), may hold values from -3 to 3
- out_bias: bfloat16 [1408], replicated, may hold values from -2 to 2
- norm2_gain: bfloat16 [1408], replicated, may hold values from 0.5 to 1.5
- norm2_beta: bfloat16 [1408], replicated, may hold values from -2 to 2
- crossed_query_weight: bfloat16 [1408, 1408], P(None, 'tensor'), may hold values from -0.15625 to 0.15625
- cross_kv_weight: bfloat16 [2, 1408, 1408], P(None, None, 'tensor'), may hold values from -0.15625 to 0.15625
- cross_qk_gain: bfloat16 [2, 88], replicated, may hold values from 0.5 to 1.5
- crossed_output_weight: bfloat16 [1408, 1408], P('tensor'), may hold values from -1.5 to 1.5
- cross_out_bias: bfloat16 [1408], replicated, may hold values from -2 to 2
- norm3_gain: bfloat16 [1408], replicated, may hold values from 0.5 to 1.5
- norm3_beta: bfloat16 [1408], replicated, may hold values from -2 to 2
- up_projection_weight: bfloat16 [1408, 6144], P(None, 'tensor'), may hold values from -0.15625 to 0.15625
- up_bias: bfloat16 [6144], P('tensor'), may hold values from -2 to 2
- down_projection_weight: bfloat16 [6144, 1408], P('tensor'), may hold values from -0.078125 to 0.078125
- down_bias: bfloat16 [1408], replicated, may hold values from -2 to 2
- out_grad: bfloat16 [16, 1024, 1408], P('dp', 'tensor'), may hold values from -6 to 6
Outputs:
- output: bfloat16 [16, 1024, 1408], P('dp', 'tensor')
- stats: float32 [16, 5, 1024], P('dp', None, 'tensor')
- latent_grad: float32 [16, 1024, 1408], P('dp', 'tensor')
- skip_grad: float32 [16, 1024, 1408], P('dp', 'tensor')
- text_grad: float32 [16, 256, 1408], P('dp')
- time_grad: float32 [16, 1408], P('dp')
- skip_gain_grad: float32 [2816], replicated
- skip_beta_grad: float32 [2816], replicated
- skip_weight_grad: float32 [2816, 1408], P(None, 'tensor')
- skip_bias_grad: float32 [1408], P('tensor')
- ada_weight_grad: float32 [1408, 1408], P(None, 'tensor')
- ada_bias_grad: float32 [1408], P('tensor')
- qkv_weight_grad: float32 [3, 1408, 1408], P(None, None, 'tensor')
- qk_gain_grad: float32 [2, 88], replicated
- out_weight_grad: float32 [1408, 1408], P('tensor')
- out_bias_grad: float32 [1408], replicated
- norm2_gain_grad: float32 [1408], replicated
- norm2_beta_grad: float32 [1408], replicated
- cross_query_weight_grad: float32 [1408, 1408], P(None, 'tensor')
- cross_kv_weight_grad: float32 [2, 1408, 1408], P(None, None, 'tensor')
- cross_qk_gain_grad: float32 [2, 88], replicated
- cross_out_weight_grad: float32 [1408, 1408], P('tensor')
- cross_out_bias_grad: float32 [1408], replicated
- norm3_gain_grad: float32 [1408], replicated
- norm3_beta_grad: float32 [1408], replicated
- up_projection_gradient: float32 [1408, 6144], P(None, 'tensor')
- up_bias_grad: float32 [6144], P('tensor')
- down_weight_grad: float32 [6144, 1408], P('tensor')
- down_bias_grad: float32 [1408], replicated
All inputs are finite; a program needn't handle non-finite values.
Results may differ from a plain program's by a relative error of at most 0.033.
Values may be sent and summed in bfloat16 or wider, within the bound.
No kernel may reach another device: no remote copies, remote signals or barrier semaphores. Data moves between devices by JAX's collectives and lax.ppermute only.
A program may use at most 320 MiB of HBM per device.

v0:
```python
from functools import partial

import jax
import jax.numpy as jnp
from jax import lax
from jax.sharding import PartitionSpec as P

HD = 88


EPSILON = 1e-06
ROPE_BASE = 10000.0
PRECISE = lax.Precision.HIGHEST


def layer_norm(values):
    center = values - jnp.mean(values, -1, keepdims=True)
    return center * lax.rsqrt(jnp.mean(center * center, -1, keepdims=True) + EPSILON)


def rope_tables(grid_pos):
    quarter = HD // 4
    frequency = ROPE_BASE ** (-jnp.arange(quarter, dtype=jnp.float32) / quarter)
    row_angle = grid_pos[..., 0:1].astype(jnp.float32) * frequency
    col_angle = grid_pos[..., 1:2].astype(jnp.float32) * frequency
    angles = jnp.concatenate([row_angle, row_angle, col_angle, col_angle], -1)
    return (jnp.cos(angles)[..., None, :], jnp.sin(angles)[..., None, :])


def rotate(values, cosines, sine_table):
    quarter = HD // 4
    first = values[..., :quarter]
    second = values[..., quarter : 2 * quarter]
    third = values[..., 2 * quarter : 3 * quarter]
    fourth = values[..., 3 * quarter :]
    turned = jnp.concatenate([-second, first, -fourth, third], -1)
    return values * cosines + turned * sine_table


def gather_tokens(values):
    return lax.all_gather(values, "tensor", axis=1, tiled=True)


def reduce_tokens(values):
    return lax.psum_scatter(
        values.astype(jnp.bfloat16), "tensor", scatter_dimension=1, tiled=True
    ).astype(jnp.float32)


def attend_forward(query_in, keys_in, values_in, key_bias):
    sequences, length, head_count, head_size = query_in.shape
    block_rows = min(512, length)
    query_blocks = jnp.moveaxis(
        query_in.reshape(sequences, length // block_rows, block_rows, head_count, head_size), 1, 0
    )

    def one_block(portion):
        scores = jnp.einsum(
            "sqhd,skhd->shqk", portion, keys_in, preferred_element_type=jnp.float32
        ) * HD ** (-0.5)
        scores = scores + key_bias[:, None, None, :]
        highest = jnp.max(scores, -1, keepdims=True)
        powers = jnp.exp(scores - highest)
        totals = jnp.sum(powers, -1, keepdims=True)
        weights = (powers / totals).astype(jnp.bfloat16)
        result = jnp.einsum(
            "shqk,skhd->sqhd", weights, values_in, preferred_element_type=jnp.float32
        )
        return (result, (highest + jnp.log(totals))[..., 0])

    results, logsum = lax.map(one_block, query_blocks)
    return (jnp.moveaxis(results, 0, 1).reshape(sequences, length, head_count * head_size), logsum)


def attend_backward(query_in, keys_in, values_in, key_bias, logsum, grad_mixed, result):
    sequences, length, head_count, head_size = query_in.shape
    block_rows = min(512, length)
    grad_heads = grad_mixed.reshape(sequences, length, head_count, head_size)
    delta = jnp.sum(
        grad_heads.astype(jnp.float32) * result.reshape(sequences, length, head_count, head_size),
        -1,
    )

    def cut_rows(array):
        return jnp.moveaxis(
            array.reshape((sequences, length // block_rows, block_rows) + array.shape[2:]), 1, 0
        )

    def one_block(running, item):
        keys_grad, values_grad = running
        portion, lse_part, grad_part, delta_part = item
        scores = jnp.einsum(
            "sqhd,skhd->shqk", portion, keys_in, preferred_element_type=jnp.float32
        ) * HD ** (-0.5)
        scores = scores + key_bias[:, None, None, :]
        weights = jnp.exp(scores - lse_part[..., None])
        values_grad = values_grad + jnp.einsum(
            "shqk,sqhd->skhd",
            weights.astype(jnp.bfloat16),
            grad_part,
            preferred_element_type=jnp.float32,
        )
        weight_grad = jnp.einsum(
            "sqhd,skhd->shqk", grad_part, values_in, preferred_element_type=jnp.float32
        )
        score_grad = (weights * (weight_grad - jnp.swapaxes(delta_part, 1, 2)[..., None])).astype(
            jnp.bfloat16
        )
        query_grad = jnp.einsum(
            "shqk,skhd->sqhd", score_grad, keys_in, preferred_element_type=jnp.float32
        ) * HD ** (-0.5)
        keys_grad = keys_grad + jnp.einsum(
            "shqk,sqhd->skhd", score_grad, portion, preferred_element_type=jnp.float32
        ) * HD ** (-0.5)
        return ((keys_grad, values_grad), query_grad)

    zero_keys = jnp.zeros(keys_in.shape, jnp.float32)
    (keys_grad, values_grad), query_grad = lax.scan(
        one_block,
        (zero_keys, zero_keys),
        (cut_rows(query_in), logsum, cut_rows(grad_heads), cut_rows(delta)),
    )
    query_grad = jnp.moveaxis(query_grad, 0, 1).reshape(query_in.shape)
    return (query_grad, keys_grad, values_grad)


def affine_norm(values, gain, beta):
    return layer_norm(values) * gain + beta


def local(
    latent_in,
    skip_in,
    text_emb,
    text_length,
    time_emb,
    grid_pos,
    skip_gain,
    skip_beta,
    skip_weight,
    skip_bias,
    ada_weight,
    ada_bias,
    query_key_value_weight,
    qk_gain,
    attention_output_weight,
    out_bias,
    norm2_gain,
    norm2_beta,
    crossed_query_weight,
    cross_kv_weight,
    cross_qk_gain,
    crossed_output_weight,
    cross_out_bias,
    norm3_gain,
    norm3_beta,
    up_projection_weight,
    up_bias,
    down_projection_weight,
    down_bias,
    out_grad,
):
    tensor_count = lax.axis_size("tensor")
    tensor_rank = lax.axis_index("tensor")
    sequences, local_len, model_width = latent_in.shape
    full_len = local_len * tensor_count
    col_width = ada_weight.shape[1]
    head_cols = query_key_value_weight.shape[2]
    local_heads = head_cols // HD
    cosines, sine_table = rope_tables(grid_pos)
    key_bias = jnp.where(
        jnp.arange(text_emb.shape[1])[None, :] < text_length[:, None], 0.0, -1e30
    ).astype(jnp.float32)
    self_bias = jnp.zeros((sequences, full_len), jnp.float32)
    skip_gain_f = skip_gain.astype(jnp.float32)
    skip_beta_f = skip_beta.astype(jnp.float32)
    norm2_gain_f = norm2_gain.astype(jnp.float32)
    norm2_beta_f = norm2_beta.astype(jnp.float32)
    norm3_gain_f = norm3_gain.astype(jnp.float32)
    norm3_beta_f = norm3_beta.astype(jnp.float32)
    qk_gain_f = qk_gain.astype(jnp.float32)
    cross_gain_f = cross_qk_gain.astype(jnp.float32)

    def first_norm(stream_in, shift_in):
        return layer_norm(stream_in) + shift_in[:, None, :]

    def qk_prep(raw, gain):
        return rotate(
            layer_norm(raw.reshape(sequences, full_len, local_heads, HD)) * gain,
            cosines,
            sine_table,
        )

    def head_norm(raw, gain):
        return layer_norm(raw.reshape(raw.shape[0], raw.shape[1], local_heads, HD)) * gain

    joined = jnp.concatenate([latent_in.astype(jnp.float32), skip_in.astype(jnp.float32)], -1)
    skip_normed = affine_norm(joined, skip_gain_f, skip_beta_f).astype(jnp.bfloat16)
    skip_all = gather_tokens(skip_normed)
    skip_cols = jnp.einsum(
        "slc,ce->sle", skip_all, skip_weight, preferred_element_type=jnp.float32
    ) + skip_bias.astype(jnp.float32)
    stream = lax.all_to_all(
        skip_cols.astype(jnp.bfloat16), "tensor", split_axis=1, concat_axis=2, tiled=True
    ).astype(skip_cols.dtype)
    condition = jax.nn.silu(time_emb.astype(jnp.float32))
    ada_weight_f = ada_weight.astype(jnp.float32)
    shift_part = jnp.dot(condition, ada_weight_f, precision=PRECISE) + ada_bias.astype(jnp.float32)
    shift_vec = lax.all_gather(shift_part, "tensor", axis=1, tiled=True)
    attn_in = first_norm(stream, shift_vec).astype(jnp.bfloat16)
    attention_gathered = gather_tokens(attn_in)
    projected = jnp.einsum(
        "mxp,jpc->jmxc",
        attention_gathered,
        query_key_value_weight,
        preferred_element_type=jnp.float32,
    )
    query_self = qk_prep(projected[0], qk_gain_f[0]).astype(jnp.bfloat16)
    keys_self = qk_prep(projected[1], qk_gain_f[1]).astype(jnp.bfloat16)
    values_self = projected[2].reshape(sequences, full_len, local_heads, HD).astype(jnp.bfloat16)
    attn_result, attn_logsum = attend_forward(query_self, keys_self, values_self, self_bias)
    attention_combined = attn_result.astype(jnp.bfloat16)
    branch_one = reduce_tokens(
        jnp.einsum(
            "jpe,ec->jpc",
            attention_combined,
            attention_output_weight,
            preferred_element_type=jnp.float32,
        )
    ) + out_bias.astype(jnp.float32)
    stream_two = stream + branch_one
    cross_in = affine_norm(stream_two, norm2_gain_f, norm2_beta_f).astype(jnp.bfloat16)
    crossed_gathered = gather_tokens(cross_in)
    query_raw = jnp.einsum(
        "pik,kx->pix", crossed_gathered, crossed_query_weight, preferred_element_type=jnp.float32
    )
    text_proj = jnp.einsum(
        "std,kdh->ksth", text_emb, cross_kv_weight, preferred_element_type=jnp.float32
    )
    cross_query = head_norm(query_raw, cross_gain_f[0]).astype(jnp.bfloat16)
    cross_keys = head_norm(text_proj[0], cross_gain_f[1]).astype(jnp.bfloat16)
    cross_values = (
        text_proj[1].reshape(sequences, text_proj.shape[2], local_heads, HD).astype(jnp.bfloat16)
    )
    cross_result, cross_logsum = attend_forward(cross_query, cross_keys, cross_values, key_bias)
    crossed_combined = cross_result.astype(jnp.bfloat16)
    branch_two = reduce_tokens(
        jnp.einsum(
            "jpe,ec->jpc",
            crossed_combined,
            crossed_output_weight,
            preferred_element_type=jnp.float32,
        )
    ) + cross_out_bias.astype(jnp.float32)
    stream_three = stream_two + branch_two
    mlp_in = affine_norm(stream_three, norm3_gain_f, norm3_beta_f).astype(jnp.bfloat16)
    gelu_fn = partial(jax.nn.gelu, approximate=True)
    perceptron_gathered = gather_tokens(mlp_in)
    hidden_pre = jnp.einsum(
        "ctk,kr->ctr", perceptron_gathered, up_projection_weight, preferred_element_type=jnp.float32
    ) + up_bias.astype(jnp.float32)
    hidden_state = gelu_fn(hidden_pre).astype(jnp.bfloat16)
    branch_three = reduce_tokens(
        jnp.einsum(
            "jgy,yv->jgv", hidden_state, down_projection_weight, preferred_element_type=jnp.float32
        )
    ) + down_bias.astype(jnp.float32)
    output = stream_three + branch_three
    stats = jnp.stack(
        [
            jnp.sqrt(jnp.mean(stream_term * stream_term, -1) + EPSILON)
            for stream_term in (stream, branch_one, branch_two, branch_three, output)
        ],
        1,
    )
    grad_out = out_grad.astype(jnp.float32)
    down_bias_part = jnp.sum(grad_out, axis=(0, 1))
    _, gelu_back = jax.vjp(gelu_fn, hidden_pre)
    gradient_gathered = gather_tokens(out_grad)
    hidden_grad = jnp.einsum(
        "bcq,eq->bce", gradient_gathered, down_projection_weight, preferred_element_type=jnp.float32
    )
    down_weight_grad = jnp.einsum(
        "mho,mhj->oj", hidden_state, gradient_gathered, preferred_element_type=jnp.float32
    )
    pre_grad = gelu_back(hidden_grad)[0]
    up_bias_grad = jnp.sum(pre_grad, axis=(0, 1))
    prenorm_reduced = pre_grad.astype(jnp.bfloat16)
    up_projection_gradient = jnp.einsum(
        "boy,bot->yt", perceptron_gathered, prenorm_reduced, preferred_element_type=jnp.float32
    )
    norm3_grad_in = reduce_tokens(
        jnp.einsum(
            "tke,ve->tkv", prenorm_reduced, up_projection_weight, preferred_element_type=jnp.float32
        )
    )
    _, norm3_back = jax.vjp(affine_norm, stream_three, norm3_gain_f, norm3_beta_f)
    from_three, gain3_part, beta3_part = norm3_back(norm3_grad_in)
    grad_three = grad_out + from_three
    cross_bias_part = jnp.sum(grad_three, axis=(0, 1))
    gradient_third_gathered = gather_tokens(grad_three.astype(jnp.bfloat16))
    cross_out_weight_grad = jnp.einsum(
        "kwy,kwn->yn", crossed_combined, gradient_third_gathered, preferred_element_type=jnp.float32
    )
    cross_mixed_grad = jnp.einsum(
        "ofz,iz->ofi",
        gradient_third_gathered,
        crossed_output_weight,
        preferred_element_type=jnp.float32,
    ).astype(jnp.bfloat16)
    cq_grad, ck_grad, cv_grad = attend_backward(
        cross_query,
        cross_keys,
        cross_values,
        key_bias,
        cross_logsum,
        cross_mixed_grad,
        cross_result,
    )
    _, cq_back = jax.vjp(head_norm, query_raw, cross_gain_f[0])
    query_raw_grad, cq_gain_part = cq_back(cq_grad)
    _, ck_back = jax.vjp(head_norm, text_proj[0], cross_gain_f[1])
    keys_raw_grad, ck_gain_part = ck_back(ck_grad)
    cross_gain_part = jnp.stack([cq_gain_part, ck_gain_part])
    query_reduced = query_raw_grad.astype(jnp.bfloat16)
    cross_query_weight_grad = jnp.einsum(
        "yfw,yfb->wb", crossed_gathered, query_reduced, preferred_element_type=jnp.float32
    )
    text_grads = jnp.stack(
        [keys_raw_grad, cv_grad.reshape(sequences, cv_grad.shape[1], head_cols)]
    ).astype(jnp.bfloat16)
    cross_kv_weight_grad = jnp.einsum(
        "std,ksth->kdh", text_emb, text_grads, preferred_element_type=jnp.float32
    )
    text_part = jnp.einsum(
        "ksth,kdh->std", text_grads, cross_kv_weight, preferred_element_type=jnp.float32
    )
    norm2_grad_in = reduce_tokens(
        jnp.einsum(
            "rjc,vc->rjv", query_reduced, crossed_query_weight, preferred_element_type=jnp.float32
        )
    )
    _, norm2_back = jax.vjp(affine_norm, stream_two, norm2_gain_f, norm2_beta_f)
    from_two, gain2_part, beta2_part = norm2_back(norm2_grad_in)
    grad_two = grad_three + from_two
    out_bias_part = jnp.sum(grad_two, axis=(0, 1))
    gradient_second_gathered = gather_tokens(grad_two.astype(jnp.bfloat16))
    out_weight_grad = jnp.einsum(
        "kwy,kwn->yn",
        attention_combined,
        gradient_second_gathered,
        preferred_element_type=jnp.float32,
    )
    attn_mixed_grad = jnp.einsum(
        "ofz,iz->ofi",
        gradient_second_gathered,
        attention_output_weight,
        preferred_element_type=jnp.float32,
    ).astype(jnp.bfloat16)
    sq_grad, sk_grad, sv_grad = attend_backward(
        query_self, keys_self, values_self, self_bias, attn_logsum, attn_mixed_grad, attn_result
    )
    _, sq_back = jax.vjp(qk_prep, projected[0], qk_gain_f[0])
    q_raw_grad, sq_gain_part = sq_back(sq_grad)
    _, sk_back = jax.vjp(qk_prep, projected[1], qk_gain_f[1])
    k_raw_grad, sk_gain_part = sk_back(sk_grad)
    self_gain_part = jnp.stack([sq_gain_part, sk_gain_part])
    projection_gradient = jnp.stack(
        [q_raw_grad, k_raw_grad, sv_grad.reshape(sequences, full_len, head_cols)]
    ).astype(jnp.bfloat16)
    qkv_weight_grad = jnp.einsum(
        "yze,myzi->mei", attention_gathered, projection_gradient, preferred_element_type=jnp.float32
    )
    first_grad_in = reduce_tokens(
        jnp.einsum(
            "apwf,acf->pwc",
            projection_gradient,
            query_key_value_weight,
            preferred_element_type=jnp.float32,
        )
    )
    _, first_back = jax.vjp(first_norm, stream, shift_vec)
    from_one, shift_part_grad = first_back(first_grad_in)
    grad_one = grad_two + from_one
    (
        shift_grad,
        down_bias_sum,
        gain3_sum,
        beta3_sum,
        cross_bias_sum,
        gain2_sum,
        beta2_sum,
        cross_gain_sum,
        out_bias_sum,
        self_gain_sum,
    ) = (
        lax.psum(shift_part_grad.astype(jnp.bfloat16), "tensor").astype(jnp.float32),
        lax.psum(down_bias_part.astype(jnp.bfloat16), "tensor").astype(jnp.float32),
        lax.psum(gain3_part.astype(jnp.bfloat16), "tensor").astype(jnp.float32),
        lax.psum(beta3_part.astype(jnp.bfloat16), "tensor").astype(jnp.float32),
        lax.psum(cross_bias_part.astype(jnp.bfloat16), "tensor").astype(jnp.float32),
        lax.psum(gain2_part.astype(jnp.bfloat16), "tensor").astype(jnp.float32),
        lax.psum(beta2_part.astype(jnp.bfloat16), "tensor").astype(jnp.float32),
        lax.psum(cross_gain_part.astype(jnp.bfloat16), "tensor").astype(jnp.float32),
        lax.psum(out_bias_part.astype(jnp.bfloat16), "tensor").astype(jnp.float32),
        lax.psum(self_gain_part.astype(jnp.bfloat16), "tensor").astype(jnp.float32),
    )
    shift_cols = lax.dynamic_slice_in_dim(shift_grad, tensor_rank * col_width, col_width, 1)
    ada_bias_grad = jnp.sum(shift_cols, axis=0)
    ada_weight_grad = jnp.dot(condition.T, shift_cols, precision=PRECISE)
    condition_grad = jnp.dot(shift_cols, ada_weight_f.T, precision=PRECISE)
    _, silu_back = jax.vjp(jax.nn.silu, time_emb.astype(jnp.float32))
    time_part = silu_back(condition_grad)[0]
    skip_grad_cols = lax.all_to_all(
        grad_one.astype(jnp.bfloat16), "tensor", split_axis=2, concat_axis=1, tiled=True
    ).astype(grad_one.dtype)
    skip_bias_grad = jnp.sum(skip_grad_cols, axis=(0, 1))
    skip_low = skip_grad_cols.astype(jnp.bfloat16)
    skip_weight_grad = jnp.einsum(
        "slc,sle->ce", skip_all, skip_low, preferred_element_type=jnp.float32
    )
    joined_grad_in = reduce_tokens(
        jnp.einsum("sle,ce->slc", skip_low, skip_weight, preferred_element_type=jnp.float32)
    )
    _, skip_norm_back = jax.vjp(affine_norm, joined, skip_gain_f, skip_beta_f)
    joined_grad, skip_gain_part, skip_beta_part = skip_norm_back(joined_grad_in)
    latent_grad = joined_grad[..., :model_width]
    skip_grad = joined_grad[..., model_width:]
    text_grad, time_grad, skip_gain_sum, skip_beta_sum = (
        lax.psum(text_part.astype(jnp.bfloat16), "tensor").astype(jnp.float32),
        lax.psum(time_part.astype(jnp.bfloat16), "tensor").astype(jnp.float32),
        lax.psum(skip_gain_part.astype(jnp.bfloat16), "tensor").astype(jnp.float32),
        lax.psum(skip_beta_part.astype(jnp.bfloat16), "tensor").astype(jnp.float32),
    )
    weight_sums = (
        lax.psum(skip_gain_sum.astype(jnp.bfloat16), "dp").astype(jnp.float32),
        lax.psum(skip_beta_sum.astype(jnp.bfloat16), "dp").astype(jnp.float32),
        lax.psum(skip_weight_grad.astype(jnp.bfloat16), "dp").astype(jnp.float32),
        lax.psum(skip_bias_grad.astype(jnp.bfloat16), "dp").astype(jnp.float32),
        lax.psum(ada_weight_grad.astype(jnp.bfloat16), "dp").astype(jnp.float32),
        lax.psum(ada_bias_grad.astype(jnp.bfloat16), "dp").astype(jnp.float32),
        lax.psum(qkv_weight_grad.astype(jnp.bfloat16), "dp").astype(jnp.float32),
        lax.psum(self_gain_sum.astype(jnp.bfloat16), "dp").astype(jnp.float32),
        lax.psum(out_weight_grad.astype(jnp.bfloat16), "dp").astype(jnp.float32),
        lax.psum(out_bias_sum.astype(jnp.bfloat16), "dp").astype(jnp.float32),
        lax.psum(gain2_sum.astype(jnp.bfloat16), "dp").astype(jnp.float32),
        lax.psum(beta2_sum.astype(jnp.bfloat16), "dp").astype(jnp.float32),
        lax.psum(cross_query_weight_grad.astype(jnp.bfloat16), "dp").astype(jnp.float32),
        lax.psum(cross_kv_weight_grad.astype(jnp.bfloat16), "dp").astype(jnp.float32),
        lax.psum(cross_gain_sum.astype(jnp.bfloat16), "dp").astype(jnp.float32),
        lax.psum(cross_out_weight_grad.astype(jnp.bfloat16), "dp").astype(jnp.float32),
        lax.psum(cross_bias_sum.astype(jnp.bfloat16), "dp").astype(jnp.float32),
        lax.psum(gain3_sum.astype(jnp.bfloat16), "dp").astype(jnp.float32),
        lax.psum(beta3_sum.astype(jnp.bfloat16), "dp").astype(jnp.float32),
        lax.psum(up_projection_gradient.astype(jnp.bfloat16), "dp").astype(jnp.float32),
        lax.psum(up_bias_grad.astype(jnp.bfloat16), "dp").astype(jnp.float32),
        lax.psum(down_weight_grad.astype(jnp.bfloat16), "dp").astype(jnp.float32),
        lax.psum(down_bias_sum.astype(jnp.bfloat16), "dp").astype(jnp.float32),
    )
    return (
        output.astype(jnp.bfloat16),
        stats,
        latent_grad,
        skip_grad,
        text_grad,
        time_grad,
    ) + tuple(weight_sums)


def solution(mesh):
    in_specs = (
        P("dp", "tensor", None),
        P("dp", "tensor", None),
        P("dp", None, None),
        P("dp"),
        P("dp", None),
        P("dp", None, None),
        P(),
        P(),
        P(None, "tensor"),
        P("tensor"),
        P(None, "tensor"),
        P("tensor"),
        P(None, None, "tensor"),
        P(),
        P("tensor", None),
        P(),
        P(),
        P(),
        P(None, "tensor"),
        P(None, None, "tensor"),
        P(),
        P("tensor", None),
        P(),
        P(),
        P(),
        P(None, "tensor"),
        P("tensor"),
        P("tensor", None),
        P(),
        P("dp", "tensor", None),
    )
    out_specs = (
        P("dp", "tensor", None),
        P("dp", None, "tensor"),
        P("dp", "tensor", None),
        P("dp", "tensor", None),
        P("dp", None, None),
        P("dp", None),
        P(),
        P(),
        P(None, "tensor"),
        P("tensor"),
        P(None, "tensor"),
        P("tensor"),
        P(None, None, "tensor"),
        P(),
        P("tensor", None),
        P(),
        P(),
        P(),
        P(None, "tensor"),
        P(None, None, "tensor"),
        P(),
        P("tensor", None),
        P(),
        P(),
        P(),
        P(None, "tensor"),
        P("tensor"),
        P("tensor", None),
        P(),
    )
    return jax.shard_map(local, mesh=mesh, in_specs=in_specs, out_specs=out_specs, check_vma=False)
```

profile of v0, /device:TPU:0, one launch (start us, length us, event | category | flops | bytes accessed | tf_op | source)
XLA Modules:
  0.0 2595.4 jit_solution(8212341249898907865)
XLA Ops:
  16.8 203.3 %all-gather.9.cloned.1.call-done = bf16[2,1024,2816]{2,1,0:T(8,128)(2,1)} async-done(((bf16[2,256,2816]{2,1,0:T(8,128)(2,1)}), bf16[2,1024,2816]{2,1,0:T(8,128)(2,1)}) %all-gather.9.cloned.1.call-update) | async-done | bytes 11534352 | tf_op jit(solution)/shard_map/all_gather | solution.py:41
  220.0 10.2 add_convert_fusion.7
  230.2 4.9 copy.214
  241.7 40.6 %all-gather = f32[4,352,2]{1,2,0:T(2,128)S(1)} all-gather(f32[1,352,2]{1,2,0:T(2,128)S(1)} %fusion.155), channel_id=1, replica_groups=mesh['dp'=8,'tensor'=4] {'tensor'}, dimensions={0}, use_global_device_ids=true | all-gather | bytes 14080 | tf_op jit(solution)/shard_map/all_gather | solution.py:209
  309.3 10.9 fusion.191
  320.3 91.2 %all-gather.11.cloned.1.call-done = bf16[2,1024,1408]{2,1,0:T(8,128)(2,1)} async-done(((bf16[2,256,1408]{2,1,0:T(8,128)(2,1)}), bf16[2,1024,1408]{2,1,0:T(8,128)(2,1)}) %all-gather.11.cloned.1.call-update) | async-done | bytes 5767184 | tf_op jit(solution)/shard_map/all_gather | solution.py:41
  411.4 9.2 fusion.103
  429.5 5.4 reshape_squeeze.16
  459.7 11.2 fusion.151
  477.4 30.3 %while.55 = (s32[]{:T(128)}, f32[2,2,512,4,88]{2,4,3,1,0:T(8,128)}, f32[2,2,4,512]{3,2,1,0:T(4,128)S(1)}, bf16[2,2,512,4,88]{2,4,3,1,0:T(8,128)(2,1)}, bf16[2,10...) while((s32[]{:T(128)}, f32[2,2,512,4,88]{2,4,3,1,0:T(8,128)}, ...), condition=%wide.region_12.13_spmd, body=%wide.region_9.0_spmd.sunk | while | flops 1514139648 | bytes 84345008 | solution.py:71
  485.5 5.6 fusion.278
  500.5 5.6 fusion.278
  517.0 7.5 convolution_convert_fusion.5
  525.2 100.0 %reduce-scatter.8.cloned.1.call-done = bf16[2,256,1408]{2,1,0:T(8,128)(2,1)} async-done(((bf16[2,1024,1408]{2,1,0:T(8,128)(2,1)}), bf16[2,256,1408]{2,1,0:T(8,128)(2,1)}) %reduce-scatter.8.cloned.1.call-update) | async-done | bytes 1441808 | tf_op jit(solution)/shard_map/reduce_scatter | solution.py:45
  642.6 97.3 %all-gather.13.cloned.1.call-done = bf16[2,1024,1408]{2,1,0:T(8,128)(2,1)} async-done(((bf16[2,256,1408]{2,1,0:T(8,128)(2,1)}), bf16[2,1024,1408]{2,1,0:T(8,128)(2,1)}) %all-gather.13.cloned.1.call-update) | async-done | bytes 5767184 | tf_op jit(solution)/shard_map/all_gather | solution.py:41
  739.9 6.9 fusion.159
  746.8 5.3 reshape.644
  761.0 14.0 while.56
  784.6 7.5 convolution_convert_fusion.4
  792.8 100.0 %reduce-scatter.10.cloned.1.call-done = bf16[2,256,1408]{2,1,0:T(8,128)(2,1)} async-done(((bf16[2,1024,1408]{2,1,0:T(8,128)(2,1)}), bf16[2,256,1408]{2,1,0:T(8,128)(2,1)}) %reduce-scatter.10.cloned.1.call-update) | async-done | bytes 1441808 | tf_op jit(solution)/shard_map/reduce_scatter | solution.py:45
  900.4 106.5 %all-gather.15.cloned.1.call-done = bf16[2,1024,1408]{2,1,0:T(8,128)(2,1)} async-done(((bf16[2,256,1408]{2,1,0:T(8,128)(2,1)}), bf16[2,1024,1408]{2,1,0:T(8,128)(2,1)}) %all-gather.15.cloned.1.call-update) | async-done | bytes 5767184 | tf_op jit(solution)/shard_map/all_gather | solution.py:41
  1007.0 15.9 fusion.91
  1022.8 90.7 %all-gather.17.cloned.1.call-done = bf16[2,1024,1408]{2,1,0:T(8,128)(2,1)} async-done(((bf16[2,256,1408]{2,1,0:T(8,128)(2,1)}), bf16[2,1024,1408]{2,1,0:T(8,128)(2,1)}) %all-gather.17.cloned.1.call-update) | async-done | bytes 5767184 | tf_op jit(solution)/shard_map/all_gather | solution.py:41
  1113.6 22.5 fusion.202
  1138.8 14.0 convolution_convert_fusion.1
  1152.9 17.2 convolution_convert_fusion.2
  1170.8 82.8 %reduce-scatter.14.cloned.1.call-done = bf16[2,256,1408]{2,1,0:T(8,128)(2,1)} async-done(((bf16[2,1024,1408]{2,1,0:T(8,128)(2,1)}), bf16[2,256,1408]{2,1,0:T(8,128)(2,1)}) %reduce-scatter.14.cloned.1.call-update) | async-done | bytes 1441808 | tf_op jit(solution)/shard_map/reduce_scatter | solution.py:45
  1256.4 102.8 %reduce-scatter.12.cloned.1.call-done = bf16[2,256,1408]{2,1,0:T(8,128)(2,1)} async-done(((bf16[2,1024,1408]{2,1,0:T(8,128)(2,1)}), bf16[2,256,1408]{2,1,0:T(8,128)(2,1)}) %reduce-scatter.12.cloned.1.call-update) | async-done | bytes 1441808 | tf_op jit(solution)/shard_map/reduce_scatter | solution.py:45
  1359.2 5.6 fusion.114
  1369.6 107.2 %all-gather.19.cloned.1.call-done = bf16[2,1024,1408]{2,1,0:T(8,128)(2,1)} async-done(((bf16[2,256,1408]{2,1,0:T(8,128)(2,1)}), bf16[2,1024,1408]{2,1,0:T(8,128)(2,1)}) %all-gather.19.cloned.1.call-update) | async-done | bytes 5767184 | tf_op jit(solution)/shard_map/all_gather | solution.py:41
  1476.8 6.4 convolution_convert_fusion.8
  1483.2 5.1 reshape_reshape.8
  1494.7 19.2 while.57
  1513.9 5.6 copy.233
  1519.5 5.4 reshape.646
  1534.7 5.2 convolution_convert_fusion.3
  1540.0 100.6 %reduce-scatter.16.cloned.1.call-done = bf16[2,256,1408]{2,1,0:T(8,128)(2,1)} async-done(((bf16[2,1024,1408]{2,1,0:T(8,128)(2,1)}), bf16[2,256,1408]{2,1,0:T(8,128)(2,1)}) %reduce-scatter.16.cloned.1.call-update) | async-done | bytes 1441808 | tf_op jit(solution)/shard_map/reduce_scatter | solution.py:45
  1650.8 107.3 %all-gather.21.cloned.1.call-done = bf16[2,1024,1408]{2,1,0:T(8,128)(2,1)} async-done(((bf16[2,256,1408]{2,1,0:T(8,128)(2,1)}), bf16[2,1024,1408]{2,1,0:T(8,128)(2,1)}) %all-gather.21.cloned.1.call-update) | async-done | bytes 5767184 | tf_op jit(solution)/shard_map/all_gather | solution.py:41
  1758.1 6.5 convolution_convert_fusion.7
  1775.6 61.0 %while.58 = (s32[]{:T(128)}, f32[2,1024,4,88]{1,3,2,0:T(8,128)}, f32[2,1024,4,88]{1,3,2,0:T(8,128)}, f32[2,2,512,4,88]{2,4,3,1,0:T(8,128)}, bf16[2,2,512,4,88]{2...) while((s32[]{:T(128)}, f32[2,1024,4,88]{1,3,2,0:T(8,128)}, ...), condition=%wide.region_46.47_spmd.clone, body=%wide.region_45.46_spmd.clone.sunk | while | flops 3728506880 | bytes 197509424 | solution.py:118
  1779.8 5.7 copy-done.1
  1785.5 5.5 bitcast_add_fusion.5
  1791.1 9.0 multiply_convert_fusion.10
  1809.9 5.7 copy-done.1
  1815.7 6.0 bitcast_add_fusion.5
  1821.7 9.0 multiply_convert_fusion.10
  1848.4 5.4 multiply_reduce_fusion.6
  1861.5 10.1 bitcast_convert_fusion
  1871.7 14.6 bitcast_convert_fusion.2
  1886.4 18.2 bitcast_convert_fusion.1
  1911.1 6.5 fusion.133
  1917.7 6.0 fusion.134
  1923.7 48.7 %reduce-scatter.18.cloned.1.call-done = bf16[2,256,1408]{2,1,0:T(8,128)(2,1)} async-done(((bf16[2,1024,1408]{2,1,0:T(8,128)(2,1)}), bf16[2,256,1408]{2,1,0:T(8,128)(2,1)}) %reduce-scatter.18.cloned.1.call-update) | async-done | bytes 1441808 | tf_op jit(solution)/shard_map/reduce_scatter | solution.py:45
  1988.5 11.6 fusion.100
  2000.2 6.0 fusion.132
  2007.8 25.9 psum.260
  2035.7 19.0 all-to-all-done.1
  2057.6 9.7 fusion.93
  2067.4 11.5 convolution_convert_fusion
  2088.9 11.7 reduce_sum.654
  2100.6 223.1 %all-reduce.16.cloned.1.call-done = (bf16[2816,352]{0,1:T(8,128)(2,1)}, bf16[1408,352]{0,1:T(8,128)(2,1)}, bf16[3,1408,352]{1,2,0:T(8,128)(2,1)}, bf16[352,1408]...) async-done(((bf16[2816,352]{0,1:T(8,128)(2,1)}, ...) | async-done | bytes 19554320 | tf_op jit(solution)/shard_map/psum | solution.py:438
  2349.6 171.4 %reduce-scatter.20.cloned.1.call-done = bf16[2,256,2816]{2,1,0:T(8,128)(2,1)} async-done(((bf16[2,1024,2816]{2,1,0:T(8,128)(2,1)}), bf16[2,256,2816]{2,1,0:T(8,128)(2,1)}) %reduce-scatter.20.cloned.1.call-update) | async-done | bytes 2883600 | tf_op jit(solution)/shard_map/reduce_scatter | solution.py:45
  2537.6 19.2 all-reduce.10
  2557.4 22.9 all-reduce.8
  (695 shorter events, 365.5 us)
Async XLA Ops:
  7.2 404.2 %copy-start = (bf16[3,1408,352]{1,2,0:T(8,128)(2,1)S(1)}, bf16[3,1408,352]{1,2,0:T(8,128)(2,1)}, u32[]{:S(2)}) copy-start(bf16[3,1408,352]{1,2,0:T(8,128)(2,1)} %param.50) | copy-start | bytes 8921092
  7.2 212.8 %all-gather.9.cloned.1.call-start = ((), (), s32[]{:S(2)}) async-start(), calls=%async_computation.9 | async-start | bytes 14417920 | tf_op jit(solution)/shard_map/all_gather | solution.py:41
  230.2 9.3 copy-start.170
  230.2 9.3 copy-start.125
  235.2 47.2 %all-to-all-start = ((bf16[2,1024,352]{2,0,1:T(2,128)(2,1)}), bf16[2,1024,352]{2,0,1:T(2,128)(2,1)}, u32[]{:S(2)}, u32[]{:S(2)}) async-start(bf16[2,1024,352]{2,0,1:T(2,128)(2,1)} %copy.214), calls=%async_computation | async-start | bytes 3145728 | tf_op jit(solution)/shard_map/all_to_all | solution.py:203
  239.5 171.9 %all-gather.11.cloned.1.call-start = ((), (), s32[]{:S(2)}) async-start(), calls=%async_computation.10 | async-start | bytes 7208960 | tf_op jit(solution)/shard_map/all_gather | solution.py:41
  295.0 6.3 copy-start.116
  304.7 320.5 %reduce-scatter.8.cloned.1.call-start = ((), (), s32[]{:S(2)}) async-start(), calls=%async_computation.11 | async-start | bytes 7208960 | tf_op jit(solution)/shard_map/reduce_scatter | solution.py:45
  320.3 137.2 %copy-start.133 = (f32[88]{0:T(128)}, f32[88]{0:T(128)S(1)}, u32[]{:S(2)}) copy-start(f32[88]{0:T(128)S(1)} %get-tuple-element.569) | copy-start | bytes 1060
  320.3 152.2 %copy-start.135 = (f32[88]{0:T(128)}, f32[88]{0:T(128)S(1)}, u32[]{:S(2)}) copy-start(f32[88]{0:T(128)S(1)} %get-tuple-element.568) | copy-start | bytes 1060
  427.2 12.9 copy-start.71
  429.4 10.5 copy-start.104
  437.0 35.4 %copy-start.69 = (f32[2,1024,4]{1,2,0:T(4,128)}, f32[2,1024,4]{1,2,0:T(4,128)S(1)}, u32[]{:S(2)}) copy-start(f32[2,1024,4]{1,2,0:T(4,128)S(1)} %broadcast_multiply_fusion.7) | copy-start | bytes 98308
  440.0 32.5 %copy-start.84 = (f32[2,1024,4]{1,2,0:T(4,128)}, f32[2,1024,4]{1,2,0:T(4,128)S(1)}, u32[]{:S(2)}) copy-start(f32[2,1024,4]{1,2,0:T(4,128)S(1)} %fusion.167) | copy-start | bytes 98308
  459.6 12.8 copy-start.56
  459.6 12.8 copy-start.58
  524.5 215.4 %all-gather.13.cloned.1.call-start = ((), (), s32[]{:S(2)}) async-start(), calls=%async_computation.12 | async-start | bytes 7208960 | tf_op jit(solution)/shard_map/all_gather | solution.py:41
  525.2 104.8 %copy-start.110 = (f32[1408]{0:T(1024)}, f32[1408]{0:T(1024)S(1)}, u32[]{:S(2)}) copy-start(f32[1408]{0:T(1024)S(1)} %convert_element_type.423) | copy-start | bytes 16900
  632.6 260.3 %reduce-scatter.10.cloned.1.call-start = ((), (), s32[]{:S(2)}) async-start(), calls=%async_computation.13 | async-start | bytes 7208960 | tf_op jit(solution)/shard_map/reduce_scatter | solution.py:45
  640.1 106.7 %copy-start.149 = (f32[88]{0:T(128)}, f32[88]{0:T(128)S(1)}, u32[]{:S(2)}) copy-start(f32[88]{0:T(128)S(1)} %get-tuple-element.566) | copy-start | bytes 1060
  640.1 117.1 %copy-start.147 = (f32[88]{0:T(128)}, f32[88]{0:T(128)S(1)}, u32[]{:S(2)}) copy-start(f32[88]{0:T(128)S(1)} %get-tuple-element.567) | copy-start | bytes 1060
  792.2 214.8 %all-gather.15.cloned.1.call-start = ((), (), s32[]{:S(2)}) async-start(), calls=%async_computation.14 | async-start | bytes 7208960 | tf_op jit(solution)/shard_map/all_gather | solution.py:41
  899.6 214.0 %all-gather.17.cloned.1.call-start = ((), (), s32[]{:S(2)}) async-start(), calls=%async_computation.16 | async-start | bytes 7208960 | tf_op jit(solution)/shard_map/all_gather | solution.py:41
  900.3 353.2 %reduce-scatter.14.cloned.1.call-start = ((), (), s32[]{:S(2)}) async-start(), calls=%async_computation.17 | async-start | bytes 7208960 | tf_op jit(solution)/shard_map/reduce_scatter | solution.py:45
  900.4 252.4 %copy-start.153 = (f32[1536]{0:T(1024)}, f32[1536]{0:T(1024)S(1)}, u32[]{:S(2)}) copy-start(f32[1536]{0:T(1024)S(1)} %convert_element_type.438) | copy-start | bytes 18436
  1152.8 206.4 %reduce-scatter.12.cloned.1.call-start = ((), (), s32[]{:S(2)}) async-start(), calls=%async_computation.15 | async-start | bytes 7208960 | tf_op jit(solution)/shard_map/reduce_scatter | solution.py:45
  1170.1 306.7 %all-gather.19.cloned.1.call-start = ((), (), s32[]{:S(2)}) async-start(), calls=%async_computation.18 | async-start | bytes 7208960 | tf_op jit(solution)/shard_map/all_gather | solution.py:41
  1369.4 271.2 %reduce-scatter.16.cloned.1.call-start = ((), (), s32[]{:S(2)}) async-start(), calls=%async_computation.19 | async-start | bytes 7208960 | tf_op jit(solution)/shard_map/reduce_scatter | solution.py:45
  1539.9 100.7 %copy-start.111 = (f32[1408]{0:T(1024)S(1)}, f32[1408]{0:T(1024)}, u32[]{:S(2)}) copy-start(f32[1408]{0:T(1024)} %copy-done.110) | copy-start | bytes 16900
  1539.9 100.7 %copy-start.115 = (f32[2,256]{1,0:T(2,128)S(1)}, f32[2,256]{1,0:T(2,128)}, u32[]{:S(2)}) copy-start(f32[2,256]{1,0:T(2,128)} %copy-done.114) | copy-start | bytes 6148
  1539.9 103.7 %copy-start.142 = (f32[2,256]{1,0:T(2,128)S(1)}, f32[2,256]{1,0:T(2,128)}, u32[]{:S(2)}) copy-start(f32[2,256]{1,0:T(2,128)} %copy-done.141) | copy-start | bytes 6148
  1539.9 103.7 %copy-start.128 = (f32[2,256]{1,0:T(2,128)S(1)}, f32[2,256]{1,0:T(2,128)}, u32[]{:S(2)}) copy-start(f32[2,256]{1,0:T(2,128)} %copy-done.127) | copy-start | bytes 6148
  1539.9 218.2 %all-gather.21.cloned.1.call-start = ((), (), s32[]{:S(2)}) async-start(), calls=%async_computation.20 | async-start | bytes 7208960 | tf_op jit(solution)/shard_map/all_gather | solution.py:41
  1650.7 321.6 %reduce-scatter.18.cloned.1.call-start = ((), (), s32[]{:S(2)}) async-start(), calls=%async_computation.21 | async-start | bytes 7208960 | tf_op jit(solution)/shard_map/reduce_scatter | solution.py:45
  1791.1 9.1 copy-start.3
  1791.1 9.1 copy-start.11
  1821.7 9.1 copy-start.3
  1821.7 9.1 copy-start.11
  1871.6 210.7 %all-reduce.14.cloned.1.call-start = ((), (), s32[]{:S(2)}) async-start(), calls=%async_computation.23 | async-start | bytes 2883584 | tf_op jit(solution)/shard_map/psum | solution.py:430
  1871.7 14.6 copy-start.154
  1886.3 18.3 copy-start.36
  1886.3 18.4 copy-start.27
  1886.3 18.4 copy-start.33
  1886.3 18.4 copy-start.99
  1886.3 18.4 copy-start.150
  1886.3 18.6 copy-start.119
  1886.3 18.6 copy-start.113
  1911.1 6.6 copy-start.77
  1917.7 54.7 %copy-start.117 = (f32[2,256]{1,0:T(2,128)S(1)}, f32[2,256]{1,0:T(2,128)}, u32[]{:S(2)}) copy-start(f32[2,256]{1,0:T(2,128)} %copy-done.116) | copy-start | bytes 6148
  1923.7 51.6 %copy-start.140 = (f32[2,256]{1,0:T(2,128)S(1)}, f32[2,256]{1,0:T(2,128)}, u32[]{:S(2)}) copy-start(f32[2,256]{1,0:T(2,128)} %copy-done.139) | copy-start | bytes 6148
  1923.7 51.6 %copy-start.130 = (f32[2,256]{1,0:T(2,128)S(1)}, f32[2,256]{1,0:T(2,128)}, u32[]{:S(2)}) copy-start(f32[2,256]{1,0:T(2,128)} %copy-done.129) | copy-start | bytes 6148
  1984.1 70.6 %all-to-all-start.1 = ((bf16[2,256,1408]{1,0,2:T(2,128)(2,1)}), bf16[2,256,1408]{1,0,2:T(2,128)(2,1)}, u32[]{:S(2)}, u32[]{:S(2)}) async-start(bf16[2,256,1408]{1,0,2:T(2,128)(2,1)} %copy.242), calls=%async_computation.7 | async-start | bytes 2883584 | tf_op jit(solution)/shard_map/all_to_all | solution.py:414
  1988.5 335.3 %all-reduce.16.cloned.1.call-start = ((), (), s32[]{:S(2)}) async-start(), calls=%async_computation.24 | async-start | bytes 39108608 | tf_op jit(solution)/shard_map/psum | solution.py:438
  1988.5 11.7 copy-start.73
  2000.2 33.5 %copy-start.126 = (bf16[2,1408]{1,0:T(2,128)(2,1)S(1)}, bf16[2,1408]{1,0:T(2,128)(2,1)}, u32[]{:S(2)}) copy-start(bf16[2,1408]{1,0:T(2,128)(2,1)} %param.42) | copy-start | bytes 16900
  2067.3 453.6 %reduce-scatter.20.cloned.1.call-start = ((), (), s32[]{:S(2)}) async-start(), calls=%async_computation.22 | async-start | bytes 14417920 | tf_op jit(solution)/shard_map/reduce_scatter | solution.py:45
  2332.0 8.8 slice-start.2
  2337.4 8.1 slice-start
  2345.5 175.4 %copy-start.97 = (f32[2816]{0:T(1024)S(1)}, f32[2816]{0:T(1024)}, u32[]{:S(2)}) copy-start(f32[2816]{0:T(1024)} %copy-done.96) | copy-start | bytes 33796
  2345.5 175.4 %copy-start.121 = (f32[2,256]{1,0:T(2,128)S(1)}, f32[2,256]{1,0:T(2,128)}, u32[]{:S(2)}) copy-start(f32[2,256]{1,0:T(2,128)} %copy-done.120) | copy-start | bytes 6148
  2349.6 175.6 %copy-start.138 = (f32[2,256]{1,0:T(2,128)S(1)}, f32[2,256]{1,0:T(2,128)}, u32[]{:S(2)}) copy-start(f32[2,256]{1,0:T(2,128)} %copy-done.137) | copy-start | bytes 6148
  2349.6 175.7 %copy-start.132 = (f32[2,256]{1,0:T(2,128)S(1)}, f32[2,256]{1,0:T(2,128)}, u32[]{:S(2)}) copy-start(f32[2,256]{1,0:T(2,128)} %copy-done.131) | copy-start | bytes 6148
  2521.0 6.1 copy-start.28
  2535.1 22.3 copy-start.168
  (157 other events, 390.3 us)
Sparse Core Ops, SparseCore 0:
  16.2 203.7 all-gather.8
  304.9 106.5 all-gather.10
  524.6 100.5 reduce-scatter.7
  632.7 107.2 all-gather.12
  792.3 100.5 reduce-scatter.9
  899.7 107.2 all-gather.14
  1008.5 104.9 all-gather.16
  1152.9 100.5 reduce-scatter.13
  1256.4 102.7 reduce-scatter.11
  1369.6 107.1 all-gather.18
  1540.0 100.5 reduce-scatter.15
  1650.9 107.2 all-gather.20
  1871.8 100.5 reduce-scatter.17
  1975.2 87.1 all-reduce.13
  2070.1 253.6 all-reduce.15
  2326.0 194.9 reduce-scatter.19
where the time goes:
time: 2610 us; the launch traced here: 2600 us
  waiting for transfers between devices  1750 us (67%)
  matrix products  326 us (12%)
  other arithmetic  214 us (8%)
  local copies, waits for them, and re-layouts  166 us (6%)
  blocking collectives  109 us (4%)
    all_gather x7, waiting for transfers between devices, gather_tokens(): return lax.all_gather(values, 'tensor', axis=1, tiled=True)  804 us
    reduce_scatter x7, waiting for transfers between devices, reduce_tokens(): lax.psum_scatter(values.astype(jnp.bfloat16), 'tensor', scatter_dimension...  706 us
    psum x1, waiting for transfers between devices, local(): lax.psum(skip_weight_grad.astype(jnp.bfloat16), 'dp').astype(jnp.float32)  223 us
  transfers between devices with their start and end apart: 18, of which 16 were waited for; matrix products, arithmetic and copies ran while one was open for 8% of the time, Pallas kernels for 0%

commit v1 on v0

--- a/solution.py
+++ b/solution.py
@@ -3,6 +3,7 @@
 import jax
 import jax.numpy as jnp
 from jax import lax
+from jax.sharding import Mesh
 from jax.sharding import PartitionSpec as P
 
 HD = 88
@@ -128,7 +129,7 @@
     return layer_norm(values) * gain + beta
 
 
-def local(
+def tensor_local(
     latent_in,
     skip_in,
     text_emb,
@@ -467,14 +468,535 @@
     ) + tuple(weight_sums)
 
 
-def solution(mesh):
+def ring_pairs(size, step):
+    return [(rank, (rank + step) % size) for rank in range(size)]
+
+
+def swap_cores(values):
+    return lax.ppermute(values, "core", [(0, 1), (1, 0)])
+
+
+def from_later(values, step, size):
+    return lax.ppermute(values, "tensor", ring_pairs(size, -step))
+
+
+def from_earlier(values, step, size):
+    return lax.ppermute(values, "tensor", ring_pairs(size, step))
+
+
+def spread_pairs(size, turn):
+    pairs = []
+    for core in range(2):
+        for rank in range(size):
+            piece = (rank + turn) % size
+            pairs.append((core * size + rank, (piece % 2) * size + 2 * core + piece // 2))
+    return pairs
+
+
+def pick(array, index):
+    return lax.dynamic_index_in_dim(array, index, 0, keepdims=False)
+
+
+def rolled(array, start):
+    return lax.dynamic_slice_in_dim(jnp.concatenate([array, array], 0), start, array.shape[0], 0)
+
+
+def dot_tt(left, right):
+    return lax.dot_general(left, right, (((1,), (1,)), ((), ())), preferred_element_type=jnp.float32)
+
+
+def dot_nn(left, right):
+    return lax.dot_general(left, right, (((1,), (0,)), ((), ())), preferred_element_type=jnp.float32)
+
+
+def dot_tn(left, right):
+    return lax.dot_general(left, right, (((0,), (0,)), ((), ())), preferred_element_type=jnp.float32)
+
+
+def chip_local(
+    latent_in,
+    skip_in,
+    text_emb,
+    text_length,
+    time_emb,
+    grid_pos,
+    skip_gain,
+    skip_beta,
+    skip_weight,
+    skip_bias,
+    ada_weight,
+    ada_bias,
+    query_key_value_weight,
+    qk_gain,
+    attention_output_weight,
+    out_bias,
+    norm2_gain,
+    norm2_beta,
+    crossed_query_weight,
+    cross_kv_weight,
+    cross_qk_gain,
+    crossed_output_weight,
+    cross_out_bias,
+    norm3_gain,
+    norm3_beta,
+    up_projection_weight,
+    up_bias,
+    down_projection_weight,
+    down_bias,
+    out_grad,
+):
+    f32 = jnp.float32
+    low = jnp.bfloat16
+    size = lax.axis_size("tensor")
+    chips = lax.axis_size("chip")
+    rank = lax.axis_index("tensor")
+    core = lax.axis_index("core")
+    chip = lax.axis_index("chip")
+    sequences, local_len, width = latent_in.shape
+    piece_len = local_len // 2
+    own_len = size * piece_len
+    shard = ada_weight.shape[1]
+    half = shard // 2
+    heads = size * half // HD
+    ff_half = up_bias.shape[0] // 2
+    ff_part = ff_half // chips
+    at_home = core == rank // sequences
+
+    def spread(values):
+        return jnp.stack(
+            [
+                lax.ppermute(
+                    pick(values, (rank + turn) % size), ("core", "tensor"), spread_pairs(size, turn)
+                )
+                for turn in range(size)
+            ]
+        )
+
+    def collect(values):
+        parts = [
+            lax.ppermute(
+                values[turn],
+                ("core", "tensor"),
+                [(target, source) for source, target in spread_pairs(size, turn)],
+            )
+            for turn in range(size)
+        ]
+        return rolled(jnp.stack(parts), (size - rank) % size)
+
+    def of_sequence(values):
+        mine = pick(values, rank % sequences)
+        return jnp.where(at_home, mine, swap_cores(mine))
+
+    def both(values):
+        return jnp.concatenate([values, swap_cores(values)], 0)
+
+    def halve(values):
+        return values[:own_len] + swap_cores(values[own_len:].astype(low)).astype(f32)
+
+    def gather_rows(own):
+        mine = pick(own, chip)
+        later = jnp.stack([from_later(mine, step, size) for step in range(1, size)])
+        rest = lax.all_gather(later, "chip", axis=0, tiled=False)
+        return jnp.concatenate([own[:, None], rest], 1)
+
+    def reduce_rows(partial_sums):
+        rows = partial_sums.shape[2]
+        parts = lax.psum_scatter(
+            partial_sums.reshape(chips * size * rows, width), "chip", scatter_dimension=0, tiled=True
+        ).reshape(size, rows, width)
+        total = parts[0].astype(f32)
+        for step in range(1, size):
+            total = total + from_earlier(parts[step], step, size).astype(f32)
+        own = lax.all_gather(total.astype(low), "chip", axis=0, tiled=True)
+        own = own.reshape(chips, rows, width)
+        other = swap_cores(own)
+        return jnp.where(core == 0, own, other), jnp.where(core == 0, other, own)
+
+    def half_cols(weight):
+        return lax.dynamic_slice_in_dim(weight, core * half, half, 1).T
+
+    def half_rows(weight):
+        return lax.dynamic_slice_in_dim(weight, core * half, half, 0)
+
+    skip_half = lax.dynamic_slice_in_dim(skip_weight, core * width, width, 0).T
+    skip_part = shard // chips
+    skip_mine = pick(skip_half.reshape(chips, skip_part, width), chip)
+    skip_rel = jnp.stack([skip_mine] + [from_later(skip_mine, step, size) for step in range(1, size)])
+    skip_abs = rolled(skip_rel, (size - rank) % size)
+    skip_own_w = (
+        lax.all_gather(skip_abs, "chip", axis=0, tiled=False)
+        .transpose(1, 0, 2, 3)
+        .reshape(width, width)
+    )
+    skip_other_w = swap_cores(skip_own_w)
+
+    self_own = jnp.stack(
+        [half_cols(query_key_value_weight[i]) for i in range(3)]
+        + [half_rows(attention_output_weight)]
+    )
+    self_full = gather_rows(self_own).reshape(4, size * half, width)
+    cross_own = jnp.stack(
+        [half_cols(crossed_query_weight), half_cols(cross_kv_weight[0]), half_cols(cross_kv_weight[1])]
+        + [half_rows(crossed_output_weight)]
+    )
+    cross_full = gather_rows(cross_own).reshape(4, size * half, width)
+    up_own = lax.dynamic_slice_in_dim(up_projection_weight, core * ff_half, ff_half, 1).T
+    up_full = gather_rows(up_own.reshape(chips, ff_part, width)).reshape(size * ff_half, width)
+    down_own = lax.dynamic_slice_in_dim(down_projection_weight, core * ff_half, ff_half, 0)
+    down_full = gather_rows(down_own.reshape(chips, ff_part, width)).reshape(size * ff_half, width)
+
+    condition = jax.nn.silu(time_emb.astype(f32))
+    ada_weight_f = ada_weight.astype(f32)
+    shift_part = jnp.dot(condition, ada_weight_f, precision=PRECISE) + ada_bias.astype(f32)
+    small = jnp.concatenate([shift_part, skip_bias.astype(f32)[None]], 0)
+    small_all = rolled(
+        jnp.stack([small] + [from_later(small, step, size) for step in range(1, size)]),
+        (size - rank) % size,
+    )
+    small_all = small_all.transpose(1, 0, 2).reshape(sequences + 1, width)
+    skip_bias_f = small_all[sequences]
+    shift_length = of_sequence(
+        jnp.concatenate([small_all[:sequences], text_length.astype(f32)[:, None]], 1)
+    )
+    shift_vec = shift_length[:width]
+    own_length = shift_length[width]
+    up_bias_own = lax.dynamic_slice_in_dim(up_bias, core * ff_half, ff_half, 0)
+    up_bias_f = (
+        jnp.stack([up_bias_own] + [from_later(up_bias_own, step, size) for step in range(1, size)])
+        .reshape(size, chips, ff_part)
+        .transpose(1, 0, 2)
+        .reshape(size * ff_half)
+        .astype(f32)
+    )
+    text_own = of_sequence(text_emb)
+    positions = of_sequence(grid_pos)
+    text_size = text_own.shape[0]
+    key_bias = jnp.where(jnp.arange(text_size)[None, :] < own_length, 0.0, -1e30).astype(f32)
+
+    by_piece = positions.reshape(2 * size, piece_len, 2)
+
+    def piece_index(of_core, turn):
+        source = (2 * (rank % 2) + of_core - turn) % size
+        return source * 2 + of_core
+
+    ordered = jnp.concatenate(
+        [pick(by_piece, piece_index(of_core, turn)) for of_core in (core, 1 - core) for turn in range(size)],
+        0,
+    )
+    cosines, sine_table = rope_tables(ordered)
+
+    skip_gain_f = skip_gain.astype(f32)
+    skip_beta_f = skip_beta.astype(f32)
+    norm2_gain_f = norm2_gain.astype(f32)
+    norm2_beta_f = norm2_beta.astype(f32)
+    norm3_gain_f = norm3_gain.astype(f32)
+    norm3_beta_f = norm3_beta.astype(f32)
+    qk_gain_f = qk_gain.astype(f32)
+    cross_gain_f = cross_qk_gain.astype(f32)
+
+    def first_norm(stream_in, shift_in):
+        return layer_norm(stream_in) + shift_in[None, :]
+
+    def qk_prep(raw, gain):
+        return rotate(layer_norm(raw.reshape(raw.shape[0], heads, HD)) * gain, cosines, sine_table)
+
+    def head_norm(raw, gain):
+        return layer_norm(raw.reshape(raw.shape[0], heads, HD)) * gain
+
+    latent_f = latent_in.reshape(own_len, width).astype(f32)
+    skip_f = skip_in.reshape(own_len, width).astype(f32)
+    joined_size = 2 * width
+    center = (jnp.sum(latent_f, -1, keepdims=True) + jnp.sum(skip_f, -1, keepdims=True)) / joined_size
+    latent_c = latent_f - center
+    skip_c = skip_f - center
+    spread_sq = jnp.sum(latent_c * latent_c, -1, keepdims=True) + jnp.sum(
+        skip_c * skip_c, -1, keepdims=True
+    )
+    inverse = lax.rsqrt(spread_sq / joined_size + EPSILON)
+    normed = jnp.stack(
+        [
+            (latent_c * inverse * skip_gain_f[:width] + skip_beta_f[:width]).astype(low),
+            (skip_c * inverse * skip_gain_f[width:] + skip_beta_f[width:]).astype(low),
+        ]
+    )
+    normed_own = pick(normed, core)
+    normed_other = pick(normed, 1 - core)
+    stream_home = (
+        dot_tt(normed_own, skip_own_w) + dot_tt(normed_other, skip_other_w) + skip_bias_f
+    ).astype(low)
+    stream = spread(stream_home.reshape(size, piece_len, width)).reshape(own_len, width).astype(f32)
+    grad_low = spread(out_grad.reshape(size, piece_len, width)).reshape(own_len, width)
+
+    attn_in = both(first_norm(stream, shift_vec).astype(low))
+    projected = [dot_tt(attn_in, self_full[i]) for i in range(3)]
+    query_self = qk_prep(projected[0], qk_gain_f[0]).astype(low)[None]
+    keys_self = qk_prep(projected[1], qk_gain_f[1]).astype(low)[None]
+    values_self = projected[2].reshape(1, 2 * own_len, heads, HD).astype(low)
+    self_bias = jnp.zeros((1, 2 * own_len), f32)
+    attn_result, attn_logsum = attend_forward(query_self, keys_self, values_self, self_bias)
+    attention_combined = attn_result[0].astype(low)
+    branch_one = halve(dot_nn(attention_combined, self_full[3])) + out_bias.astype(f32)
+    stream_two = stream + branch_one
+    cross_in = both(affine_norm(stream_two, norm2_gain_f, norm2_beta_f).astype(low))
+    query_raw = dot_tt(cross_in, cross_full[0])
+    keys_raw = dot_tt(text_own, cross_full[1])
+    values_raw = dot_tt(text_own, cross_full[2])
+    cross_query = head_norm(query_raw, cross_gain_f[0]).astype(low)[None]
+    cross_keys = head_norm(keys_raw, cross_gain_f[1]).astype(low)[None]
+    cross_values = values_raw.reshape(1, text_size, heads, HD).astype(low)
+    cross_result, cross_logsum = attend_forward(cross_query, cross_keys, cross_values, key_bias)
+    crossed_combined = cross_result[0].astype(low)
+    branch_two = halve(dot_nn(crossed_combined, cross_full[3])) + cross_out_bias.astype(f32)
+    stream_three = stream_two + branch_two
+    mlp_in = both(affine_norm(stream_three, norm3_gain_f, norm3_beta_f).astype(low))
+    gelu_fn = partial(jax.nn.gelu, approximate=True)
+    hidden_pre = dot_tt(mlp_in, up_full) + up_bias_f
+    hidden_state, gelu_back = jax.vjp(gelu_fn, hidden_pre)
+    hidden_state = hidden_state.astype(low)
+    branch_three = halve(dot_nn(hidden_state, down_full)) + down_bias.astype(f32)
+    output = stream_three + branch_three
+    stats = jnp.stack(
+        [
+            jnp.sqrt(jnp.mean(term * term, -1) + EPSILON)
+            for term in (stream, branch_one, branch_two, branch_three, output)
+        ]
+    )
+    output_home = collect(output.astype(low).reshape(size, piece_len, width)).reshape(latent_in.shape)
+    stats_home = (
+        collect(stats.reshape(5, size, piece_len).transpose(1, 0, 2))
+        .reshape(sequences, 2, 5, piece_len)
+        .transpose(0, 2, 1, 3)
+        .reshape(sequences, 5, local_len)
+    )
+
+    grad_out = grad_low.astype(f32)
+    down_bias_part = jnp.sum(grad_out, axis=0)
+    grad_all = both(grad_low)
+    down_grad = dot_tn(hidden_state, grad_all).astype(low)
+    hidden_grad = dot_tt(grad_all, down_full)
+    pre_grad = gelu_back(hidden_grad)[0]
+    up_bias_part = jnp.sum(pre_grad, axis=0)
+    pre_low = pre_grad.astype(low)
+    norm3_grad_in = halve(dot_nn(pre_low, up_full))
+    up_grad = dot_tn(pre_low, mlp_in).astype(low)
+    _, norm3_back = jax.vjp(affine_norm, stream_three, norm3_gain_f, norm3_beta_f)
+    from_three, gain3_part, beta3_part = norm3_back(norm3_grad_in)
+    grad_three = grad_out + from_three
+    cross_bias_part = jnp.sum(grad_three, axis=0)
+    three_all = both(grad_three.astype(low))
+    cross_out_grad = dot_tn(crossed_combined, three_all).astype(low)
+    cross_mixed_grad = dot_tt(three_all, cross_full[3]).astype(low)[None]
+    cq_grad, ck_grad, cv_grad = attend_backward(
+        cross_query, cross_keys, cross_values, key_bias, cross_logsum, cross_mixed_grad, cross_result
+    )
+    _, cq_back = jax.vjp(head_norm, query_raw, cross_gain_f[0])
+    query_raw_grad, cq_gain_part = cq_back(cq_grad[0])
+    _, ck_back = jax.vjp(head_norm, keys_raw, cross_gain_f[1])
+    keys_raw_grad, ck_gain_part = ck_back(ck_grad[0])
+    cross_gain_part = jnp.concatenate([cq_gain_part, ck_gain_part])
+    query_low = query_raw_grad.astype(low)
+    keys_low = keys_raw_grad.astype(low)
+    values_low = cv_grad.reshape(text_size, size * half).astype(low)
+    norm2_grad_in = halve(dot_nn(query_low, cross_full[0]))
+    cross_grads = jnp.stack(
+        [
+            dot_tn(query_low, cross_in).astype(low),
+            dot_tn(keys_low, text_own).astype(low),
+            dot_tn(values_low, text_own).astype(low),
+            cross_out_grad,
+        ]
+    )
+    text_part = dot_nn(keys_low, cross_full[1]) + dot_nn(values_low, cross_full[2])
+    _, norm2_back = jax.vjp(affine_norm, stream_two, norm2_gain_f, norm2_beta_f)
+    from_two, gain2_part, beta2_part = norm2_back(norm2_grad_in)
+    grad_two = grad_three + from_two
+    out_bias_part = jnp.sum(grad_two, axis=0)
+    two_all = both(grad_two.astype(low))
+    out_weight_part = dot_tn(attention_combined, two_all).astype(low)
+    attn_mixed_grad = dot_tt(two_all, self_full[3]).astype(low)[None]
+    sq_grad, sk_grad, sv_grad = attend_backward(
+        query_self, keys_self, values_self, self_bias, attn_logsum, attn_mixed_grad, attn_result
+    )
+    _, sq_back = jax.vjp(qk_prep, projected[0], qk_gain_f[0])
+    q_raw_grad, sq_gain_part = sq_back(sq_grad[0])
+    _, sk_back = jax.vjp(qk_prep, projected[1], qk_gain_f[1])
+    k_raw_grad, sk_gain_part = sk_back(sk_grad[0])
+    self_gain_part = jnp.concatenate([sq_gain_part, sk_gain_part])
+    proj_grads = [
+        q_raw_grad.astype(low),
+        k_raw_grad.astype(low),
+        sv_grad.reshape(2 * own_len, size * half).astype(low),
+    ]
+    first_grad_in = halve(
+        dot_nn(proj_grads[0], self_full[0])
+        + dot_nn(proj_grads[1], self_full[1])
+        + dot_nn(proj_grads[2], self_full[2])
+    )
+    self_grads = jnp.stack(
+        [dot_tn(grad, attn_in).astype(low) for grad in proj_grads] + [out_weight_part]
+    )
+    _, first_back = jax.vjp(first_norm, stream, shift_vec)
+    from_one, shift_own_grad = first_back(first_grad_in)
+    grad_one = (grad_two + from_one).astype(low)
+
+    home_grad = collect(grad_one.reshape(size, piece_len, width)).reshape(own_len, width)
+    skip_bias_part = jnp.sum(home_grad.astype(f32), axis=0)
+    skip_own_grad = dot_tn(home_grad, normed_own)
+    skip_other_grad = dot_tn(home_grad, normed_other).astype(low)
+    skip_sum = (skip_own_grad + swap_cores(skip_other_grad).astype(f32)).astype(low)
+    own_in = dot_nn(home_grad, skip_own_w)
+    other_in = dot_nn(home_grad, skip_other_w)
+    latent_in_grad = jnp.where(core == 0, own_in, other_in)
+    skip_in_grad = jnp.where(core == 0, other_in, own_in)
+    latent_ln = latent_c * inverse
+    skip_ln = skip_c * inverse
+    skip_gain_part = jnp.concatenate(
+        [jnp.sum(latent_in_grad * latent_ln, 0), jnp.sum(skip_in_grad * skip_ln, 0)]
+    )
+    skip_beta_part = jnp.concatenate([jnp.sum(latent_in_grad, 0), jnp.sum(skip_in_grad, 0)])
+    latent_h = latent_in_grad * skip_gain_f[:width]
+    skip_h = skip_in_grad * skip_gain_f[width:]
+    mean_h = (jnp.sum(latent_h, -1, keepdims=True) + jnp.sum(skip_h, -1, keepdims=True)) / joined_size
+    mean_hl = (
+        jnp.sum(latent_h * latent_ln, -1, keepdims=True)
+        + jnp.sum(skip_h * skip_ln, -1, keepdims=True)
+    ) / joined_size
+    latent_grad = (inverse * (latent_h - mean_h - latent_ln * mean_hl)).reshape(latent_in.shape)
+    skip_grad = (inverse * (skip_h - mean_h - skip_ln * mean_hl)).reshape(latent_in.shape)
+
+    shift_own = shift_own_grad + swap_cores(shift_own_grad)
+    shift_all = lax.all_gather(shift_own, ("chip", "tensor"), axis=0, tiled=False)
+    condition_all = jax.nn.silu(
+        lax.all_gather(time_emb, ("chip", "core"), axis=0, tiled=True).astype(f32)
+    )
+    shift_cols = lax.dynamic_slice_in_dim(shift_all, rank * shard, shard, 1)
+    ada_bias_grad = jnp.sum(shift_cols, axis=0)
+    ada_weight_grad = jnp.dot(condition_all.T, shift_cols, precision=PRECISE)
+    shift_mine = lax.dynamic_slice_in_dim(
+        shift_cols, (chip * 2 + core) * sequences, sequences, 0
+    )
+    condition_grad = lax.psum(jnp.dot(shift_mine, ada_weight_f.T, precision=PRECISE), "tensor")
+    _, silu_back = jax.vjp(jax.nn.silu, time_emb.astype(f32))
+    time_grad = silu_back(condition_grad)[0]
+
+    text_half = text_size // 2
+    text_rows = lax.dynamic_slice_in_dim(text_part, core * text_half, text_half, 0)
+    text_away = lax.dynamic_slice_in_dim(text_part, (1 - core) * text_half, text_half, 0).astype(low)
+    text_rows = (text_rows + swap_cores(text_away).astype(f32)).astype(low)
+    text_pieces = []
+    for turn in range(size):
+        pairs = [
+            (c * size + r, (r // 2) * size + (2 * (r % 2) + c + turn) % size)
+            for c in range(2)
+            for r in range(size)
+        ]
+        text_pieces.append(lax.ppermute(text_rows, ("core", "tensor"), pairs))
+    text_stack = jnp.stack(text_pieces)
+    text_grad = (
+        jnp.stack([pick(text_stack, (rank - k) % size) for k in range(size)])
+        .reshape(sequences, text_size, width)
+        .astype(f32)
+    )
+
+    up_bias_rel = up_bias_part.reshape(chips, size, ff_part).transpose(1, 0, 2).reshape(size, ff_half)
+    up_bias_abs = rolled(up_bias_rel, (size - rank) % size)
+    up_bias_vec = jnp.stack(
+        [jnp.where(core == 0, up_bias_abs, 0.0), jnp.where(core == 1, up_bias_abs, 0.0)], 1
+    ).reshape(2 * size * ff_half)
+    vectors = [
+        skip_gain_part,
+        skip_beta_part,
+        skip_bias_part,
+        self_gain_part,
+        out_bias_part,
+        gain2_part,
+        beta2_part,
+        cross_gain_part,
+        cross_bias_part,
+        gain3_part,
+        beta3_part,
+        up_bias_vec,
+        down_bias_part,
+    ]
+    lengths = [vector.shape[0] for vector in vectors]
+    summed = lax.psum(jnp.concatenate(vectors), ("chip", "core", "tensor"))
+    sums = []
+    at = 0
+    for length in lengths:
+        sums.append(summed[at : at + length])
+        at += length
+
+    def own_cols(vector, count):
+        return lax.dynamic_slice_in_dim(vector, rank * count, count, 0)
+
+    down0, down1 = reduce_rows(down_grad.reshape(chips, size, ff_part, width))
+    down_weight_grad = jnp.concatenate(
+        [down0.reshape(ff_half, width), down1.reshape(ff_half, width)], 0
+    ).astype(f32)
+    up0, up1 = reduce_rows(up_grad.reshape(chips, size, ff_part, width))
+    up_weight_grad = jnp.concatenate(
+        [up0.reshape(ff_half, width).T, up1.reshape(ff_half, width).T], 1
+    ).astype(f32)
+    cross0, cross1 = reduce_rows(cross_grads.reshape(4, size, half, width))
+
+    def cols_of(first, second):
+        return jnp.concatenate([first.T, second.T], 1).astype(f32)
+
+    def rows_of(first, second):
+        return jnp.concatenate([first, second], 0).astype(f32)
+
+    cross_query_weight_grad = cols_of(cross0[0], cross1[0])
+    cross_kv_weight_grad = jnp.stack([cols_of(cross0[i], cross1[i]) for i in (1, 2)])
+    cross_out_weight_grad = rows_of(cross0[3], cross1[3])
+    self0, self1 = reduce_rows(self_grads.reshape(4, size, half, width))
+    qkv_weight_grad = jnp.stack([cols_of(self0[i], self1[i]) for i in range(3)])
+    out_weight_grad = rows_of(self0[3], self1[3])
+    skip_rel_grad = rolled(skip_sum.reshape(size, chips, skip_part, width), rank).transpose(1, 0, 2, 3)
+    skip0, skip1 = reduce_rows(skip_rel_grad)
+    skip_weight_grad = jnp.concatenate(
+        [skip0.reshape(shard, width).T, skip1.reshape(shard, width).T], 0
+    ).astype(f32)
+    return (
+        output_home,
+        stats_home,
+        latent_grad,
+        skip_grad,
+        text_grad,
+        time_grad,
+        sums[0],
+        sums[1],
+        skip_weight_grad,
+        own_cols(sums[2], shard),
+        ada_weight_grad,
+        ada_bias_grad,
+        qkv_weight_grad,
+        sums[3].reshape(2, HD),
+        out_weight_grad,
+        sums[4],
+        sums[5],
+        sums[6],
+        cross_query_weight_grad,
+        cross_kv_weight_grad,
+        sums[7].reshape(2, HD),
+        cross_out_weight_grad,
+        sums[8],
+        sums[9],
+        sums[10],
+        up_weight_grad,
+        own_cols(sums[11], 2 * ff_half),
+        down_weight_grad,
+        sums[12],
+    )
+
+
+def specs(dp):
     in_specs = (
-        P("dp", "tensor", None),
-        P("dp", "tensor", None),
-        P("dp", None, None),
-        P("dp"),
-        P("dp", None),
-        P("dp", None, None),
+        P(dp, "tensor", None),
+        P(dp, "tensor", None),
+        P(dp, None, None),
+        P(dp),
+        P(dp, None),
+        P(dp, None, None),
         P(),
         P(),
         P(None, "tensor"),
@@ -498,15 +1020,15 @@
         P("tensor"),
         P("tensor", None),
         P(),
-        P("dp", "tensor", None),
+        P(dp, "tensor", None),
     )
     out_specs = (
-        P("dp", "tensor", None),
-        P("dp", None, "tensor"),
-        P("dp", "tensor", None),
-        P("dp", "tensor", None),
-        P("dp", None, None),
-        P("dp", None),
+        P(dp, "tensor", None),
+        P(dp, None, "tensor"),
+        P(dp, "tensor", None),
+        P(dp, "tensor", None),
+        P(dp, None, None),
+        P(dp, None),
         P(),
         P(),
         P(None, "tensor"),
@@ -531,4 +1053,18 @@
         P("tensor", None),
         P(),
     )
-    return jax.shard_map(local, mesh=mesh, in_specs=in_specs, out_specs=out_specs, check_vma=False)
+    return in_specs, out_specs
+
+
+def solution(mesh):
+    dp_size, size = mesh.shape["dp"], mesh.shape["tensor"]
+    if dp_size == 8 and size == 4:
+        grid = Mesh(mesh.devices.reshape(dp_size // 2, 2, size), ("chip", "core", "tensor"))
+        in_specs, out_specs = specs(("chip", "core"))
+        return jax.shard_map(
+            chip_local, mesh=grid, in_specs=in_specs, out_specs=out_specs, check_vma=False
+        )
+    in_specs, out_specs = specs("dp")
+    return jax.shard_map(
+        tensor_local, mesh=mesh, in_specs=in_specs, out_specs=out_specs, check_vma=False
+    )

time: 2610 us -> 1500 us (0.57)
  waiting for transfers between devices: 1750 us -> 288 us
  starting transfers between devices: 10.3 us -> 275 us
  local copies, waits for them, and re-layouts: 166 us -> 301 us
  other arithmetic: 214 us -> 186 us
  blocking collectives: 109 us -> 81 us
    all_gather x7 -> x9, waiting for transfers between devices: 804 us -> 14.7 us  [the longest x4 14.7 us: reduce_rows(): own = lax.all_gather(total.astype(low), 'chip', axis=0, tiled=True)]
    reduce_scatter x7 -> x5, waiting for transfers between devices: 706 us -> 0.05 us  [reduce_rows(): lax.psum_scatter(partial_sums.reshape(chips * size * rows, width), 'chip'...]
    ppermute x0 -> x84, starting transfers between devices: none -> 274 us  [the longest x21 91.3 us: from_later(): return lax.ppermute(values, 'tensor', ring_pairs(size, -step))]
    ppermute x0 -> x84, waiting for transfers between devices: none -> 273 us  [the longest x15 115 us: from_earlier(): return lax.ppermute(values, 'tensor', ring_pairs(size, step))]
    psum x2 -> x1, waiting for transfers between devices: 223 us -> 0.01 us  [chip_local(): summed = lax.psum(jnp.concatenate(vectors), ('chip', 'core', 'tensor'))]
    dynamic_update_slice x0 -> x8, local copies, waits for them, and re-layouts: none -> 121 us  [attend_forward(): results, logsum = lax.map(one_block, query_blocks)]
    psum x3 -> x1, blocking collectives: 68 us -> 16 us  [chip_local(): lax.psum(jnp.dot(shift_mine, ada_weight_f.T, precision=PRECISE), 'tensor')]
    unnamed x329 -> x481, local copies, waits for them, and re-layouts: 32.6 us -> 64.9 us
  transfers between devices with their start and end apart: 18 -> 99, of which waited for: 16 -> 30; matrix products, arithmetic and copies ran while one was open for 8% -> 47% of each run, Pallas kernels for 0% -> 0%
where the time goes in v1:
time: 1500 us; the launch traced here: 1480 us
  matrix products  325 us (22%)
  local copies, waits for them, and re-layouts  301 us (20%)
  waiting for transfers between devices  288 us (19%)
  starting transfers between devices  275 us (18%)
  other arithmetic  186 us (12%)
  blocking collectives  81 us (5%)
  between operations  18.4 us (1%)
    dynamic_update_slice x8, local copies, waits for them, and re-layouts, attend_forward(): results, logsum = lax.map(one_block, query_blocks)  121 us
    ppermute x15, waiting for transfers between devices, from_earlier(): return lax.ppermute(values, 'tensor', ring_pairs(size, step))  115 us
    ppermute x21, starting transfers between devices, from_later(): return lax.ppermute(values, 'tensor', ring_pairs(size, -step))  91.3 us
    dot_general x12, matrix products, dot_tt(): lax.dot_general(left, right, (((1,), (1,)), ((), ())), preferred_element_...  80.2 us
    dot_general x12, matrix products, dot_tn(): lax.dot_general(left, right, (((0,), (0,)), ((), ())), preferred_element_...  68.3 us
    ppermute x21, waiting for transfers between devices, from_later(): return lax.ppermute(values, 'tensor', ring_pairs(size, -step))  68.3 us
    dot_general x12, matrix products, dot_nn(): lax.dot_general(left, right, (((1,), (0,)), ((), ())), preferred_element_...  64.9 us
    unnamed x481, local copies, waits for them, and re-layouts  64.9 us
  transfers between devices with their start and end apart: 99, of which 30 were waited for; matrix products, arithmetic and copies ran while one was open for 47% of the time, Pallas kernels for 0%

profile of v1, /device:TPU:0, one launch (start us, length us, event | category | flops | bytes accessed | tf_op | source)
XLA Modules:
  0.0 1476.8 jit_solution(1155517312640112960)
XLA Ops:
  22.7 13.9 collective-permute-done.1
  54.2 11.1 collective-permute-done.15
  65.3 19.3 %collective-permute-done.14 = bf16[176,1408]{1,0:T(8,128)(2,1)S(1)} collective-permute-done((bf16[176,1408]{1,0:T(8,128)(2,1)S(1)}, bf16[176,1408]{1,0:T(8,128)(2,1)S(1)}, u32[]{:S(2)}, u32[]{:S(2)}) %collective-permute-start.14) | collective-permute-done | bytes 495648 | tf_op jit(solution)/shard_map/ppermute | solution.py:480
  87.0 11.9 collective-permute-start.4
  120.1 19.4 %collective-permute-start.6 = (f32[3,352]{1,0:T(4,128)S(1)}, f32[3,352]{1,0:T(4,128)S(1)}, u32[]{:S(2)}, u32[]{:S(2)}) collective-permute-start(f32[3,352]{1,0:T(4,128)S(1)} %pad_maximum_fusion.40), channel_id=1, source_target_pairs={{0,1},{1,2},{2,3},{3,0},{4,5},{5,6},{6,7},{7,4},{8,9},{9,10},{10,1... | collective-permute-start | bytes 12680 | tf_op jit(solution)/shard_map/ppermute | solution.py:480
  164.4 10.5 collective-permute-start.10
  190.3 6.5 collective-permute-start.25
  205.3 23.4 %collective-permute-start.12 = (bf16[512,1408]{1,0:T(8,128)(2,1)}, bf16[512,1408]{1,0:T(8,128)(2,1)}, u32[]{:S(2)}, u32[]{:S(2)}) collective-permute-start(bf16[512,1408]{1,0:T(8,128)(2,1)} %fusion.132), channel_id=1, source_target_pairs={{0,4},{4,0},{1,5},{5,1},{2,6},{6,2},{3,7},{7,3},{8,12},{12,8},{9,1... | collective-permute-start | bytes 4325384 | tf_op jit(solution)/shard_map/ppermute | solution.py:476
  230.8 22.2 %collective-permute-start.32 = (bf16[192,1408]{1,0:T(8,128)(2,1)}, bf16[192,1408]{1,0:T(8,128)(2,1)}, u32[]{:S(2)}, u32[]{:S(2)}) collective-permute-start(bf16[192,1408]{1,0:T(8,128)(2,1)} %dynamic-slice_bitcast_fusion.5), channel_id=1, source_target_pairs={{0,2},{1,3},{2,0},{3,1},{4,6},{5,7},{6,4},{7,5},{8,10},{9,11},{10,... | collective-permute-start | bytes 1622024 | tf_op jit(solution)/shard_map/ppermute | solution.py:480
  253.1 18.5 %collective-permute-done.26 = bf16[192,1408]{1,0:T(8,128)(2,1)S(1)} collective-permute-done((bf16[192,1408]{1,0:T(8,128)(2,1)}, bf16[192,1408]{1,0:T(8,128)(2,1)S(1)}, u32[]{:S(2)}, u32[]{:S(2)}) %collective-permute-start.26) | collective-permute-done | bytes 540704 | tf_op jit(solution)/shard_map/ppermute | solution.py:480
  306.8 26.2 %while.55 = (s32[]{:T(128)}, f32[2,1,512,8,88]{2,4,3,1,0:T(8,128)}, f32[2,1,8,512]{3,2,1,0:T(8,128)S(1)}, bf16[2,1,512,8,88]{2,4,3,1,0:T(8,128)(2,1)S(1)}, bf16[...) while((s32[]{:T(128)}, f32[2,1,512,8,88]{2,4,3,1,0:T(8,128)}, ...), condition=%wide.region_13.14_spmd, body=%wide.region_10.13_spmd.sunk | while | flops 1514139648 | bytes 84345008 | solution.py:72
  379.4 14.8 while.56
  402.4 8.2 collective-permute-start.30
  427.7 15.2 %collective-permute-done.45 = bf16[128,1408]{1,0:T(8,128)(2,1)} collective-permute-done((bf16[128,1408]{1,0:T(8,128)(2,1)}, bf16[128,1408]{1,0:T(8,128)(2,1)}, u32[]{:S(2)}, u32[]{:S(2)}) %collective-permute-start.45) | collective-permute-done | bytes 360480 | tf_op jit(solution)/shard_map/ppermute | solution.py:568
  446.3 7.8 pad_maximum_fusion
  454.1 7.8 pad_maximum_fusion.1
  461.8 16.0 %fusion.154 = f32[1024,3072]{1,0:T(8,128)} fusion(bf16[3072,1408]{1,0:T(8,128)(2,1)} %bitcast.895, bf16[512,1408]{1,0:T(8,128)(2,1)} %collective-permute-done.24, bf16[512,1408]{1,0:T(8,128)(2,1)} %add_convert_fusion.4), kind=kOutput, calls=%fused_computation.306 | convolution fusion | flops 8864137216 | bytes 24117248 | tf_op jit(solution)/shard_map/dot_general | solution.py:505
  477.9 24.4 %fusion.264 = (f32[3072]{0:T(1024)}, bf16[1024,3072]{1,0:T(8,128)(2,1)}) fusion(f32[1024,3072]{1,0:T(8,128)} %fusion.154, f32[3072]{0:T(1024)S(1)} %reshape.1515, bf16[3072,1408]{1,0:T(8,128)(2,1)} %bitcast.893, bf16[512,1408]{1,0:T(8,128)(2,1)} %collective-permute-done.47, bf16[512,1408]{1,0:T(8,128)(2,1)} %bitcast.151), kind=kOutput, calls=%fused_computation.627 | convolution fusion | flops 8933340160 | bytes 30433280 | tf_op jit(solution)/shard_map/dot_general | solution.py:505
  502.2 15.5 %convolution_convert_fusion.1 = bf16[3072,1408]{1,0:T(8,128)(2,1)} fusion(bf16[1024,3072]{1,0:T(8,128)(2,1)} %get-tuple-element.829, bf16[512,1408]{1,0:T(8,128)(2,1)} %collective-permute-done.24, bf16[512,1408]{1,0:T(8,128)(2,1)} %add_convert_fusion.4), kind=kOutput, calls=%fused_computation.113 | convolution fusion | flops 8868462592 | bytes 17825792 | tf_op jit(solution)/shard_map/dot_general | solution.py:513
  517.8 13.0 fusion.96
  535.1 17.4 %fusion.235 = f32[1024,1408]{1,0:T(8,128)S(1)} fusion(bf16[3072,1408]{1,0:T(8,128)(2,1)} %bitcast.894, f32[1024,3072]{1,0:T(8,128)} %fusion.154, f32[3072]{0:T(1024)S(1)} %reshape.1515), kind=kOutput, calls=%fused_computation.600 | convolution fusion | flops 8889827328 | bytes 27013120 | tf_op jit(solution)/shard_map/dot_general | solution.py:509
  556.3 15.3 %convolution_convert_fusion = bf16[3072,1408]{1,0:T(8,128)(2,1)} fusion(bf16[512,1408]{1,0:T(8,128)(2,1)} %collective-permute-done.47, bf16[512,1408]{1,0:T(8,128)(2,1)} %bitcast.151, f32[1024,3072]{1,0:T(8,128)S(1)} %bitcast.1004, f32[3072]{0:T(1024)S(1)} %reshape.1515), kind=kOutput, calls=%fused_computation.112 | convolution fusion | flops 8899919872 | bytes 24129536 | tf_op jit(solution)/shard_map/dot_general | solution.py:513
  572.3 6.4 multiply_reduce_fusion.1
  599.1 86.3 %while.57 = (s32[]{:T(128)}, f32[1,256,8,88]{1,3,2,0:T(8,128)}, f32[1,256,8,88]{1,3,2,0:T(8,128)}, f32[2,1,512,8,88]{2,0,4,3,1:T(2,128)}, bf16[2,1,512,8,88]{2,4...) while((s32[]{:T(128)}, f32[1,256,8,88]{1,3,2,0:T(8,128)}, ...), condition=%wide.region_35.36_spmd.clone, body=%wide.region_34.35_spmd.clone.sunk | while | flops 934494976 | bytes 74083720 | solution.py:119
  613.2 28.9 %dynamic_update_slice.38 = f32[2,1,512,8,88]{2,0,4,3,1:T(2,128)} dynamic-update-slice(f32[2,1,512,8,88]{2,0,4,3,1:T(2,128)} %get-tuple-element.1115, f32[1,1,512,8,88]{2,0,4,3,1:T(1,128)S(1)} %copy.274, s32[]{:T(128)S(6)} %copy.343, s32[]{:T(128)} %constant.390.clone.1..sunk, s32[]{:T(128)} %constant.390.clone.1..sunk, s32[]{:T(128)} %constant.390.clone.1..sunk, s32[]{:T(128)} %constant.390.clone.1..sunk) | dynamic-update-slice | bytes 2883588 | tf_op jit(solution)/shard_map/while/body/jit(dynamic_update_index_in_dim)/dynamic_update_slice | solution.py:72
  656.5 28.8 %dynamic_update_slice.38 = f32[2,1,512,8,88]{2,0,4,3,1:T(2,128)} dynamic-update-slice(f32[2,1,512,8,88]{2,0,4,3,1:T(2,128)} %get-tuple-element.1115, f32[1,1,512,8,88]{2,0,4,3,1:T(1,128)S(1)} %copy.274, s32[]{:T(128)S(6)} %copy.343, s32[]{:T(128)} %constant.390.clone.1..sunk, s32[]{:T(128)} %constant.390.clone.1..sunk, s32[]{:T(128)} %constant.390.clone.1..sunk, s32[]{:T(128)} %constant.390.clone.1..sunk) | dynamic-update-slice | bytes 2883588 | tf_op jit(solution)/shard_map/while/body/jit(dynamic_update_index_in_dim)/dynamic_update_slice | solution.py:72
  742.9 142.9 %while.58 = (s32[]{:T(128)}, f32[1,1024,8,88]{1,3,2,0:T(8,128)}, f32[1,1024,8,88]{1,3,2,0:T(8,128)}, f32[2,1,512,8,88]{2,0,4,3,1:T(2,128)}, bf16[2,1,512,8,88]{2...) while((s32[]{:T(128)}, f32[1,1024,8,88]{1,3,2,0:T(8,128)}, ...), condition=%wide.region_42.43_spmd.clone, body=%wide.region_41.42_spmd.clone.sunk | while | flops 3728506880 | bytes 247316752 | solution.py:119
  747.1 6.2 copy-done.2
  753.3 8.8 multiply_convert_fusion.10
  762.1 7.2 bitcast_add_fusion.6
  777.4 6.2 multiply_bitcast_fusion.2
  785.1 28.8 %dynamic_update_slice.39 = f32[2,1,512,8,88]{2,0,4,3,1:T(2,128)} dynamic-update-slice(f32[2,1,512,8,88]{2,0,4,3,1:T(2,128)} %get-tuple-element.1153, f32[1,1,512,8,88]{2,0,4,3,1:T(1,128)S(1)} %copy.275, s32[]{:T(128)S(6)} %copy.355, s32[]{:T(128)} %constant.390.clone.1..sunk.1, s32[]{:T(128)} %constant.390.clone.1..sunk.1, s32[]{:T(128)} %constant.390.clone.1..sunk.1, s32[]{:T(128)} %constant.390.clone.1..sunk.1) | dynamic-update-slice | bytes 2883588 | tf_op jit(solution)/shard_map/while/body/jit(dynamic_update_index_in_dim)/dynamic_update_slice | solution.py:72
  823.7 8.8 multiply_convert_fusion.10
  832.6 7.8 bitcast_add_fusion.6
  843.2 6.1 bitcast_add_fusion.7
  849.3 6.2 multiply_bitcast_fusion.2
  857.0 28.7 %dynamic_update_slice.39 = f32[2,1,512,8,88]{2,0,4,3,1:T(2,128)} dynamic-update-slice(f32[2,1,512,8,88]{2,0,4,3,1:T(2,128)} %get-tuple-element.1153, f32[1,1,512,8,88]{2,0,4,3,1:T(1,128)S(1)} %copy.275, s32[]{:T(128)S(6)} %copy.355, s32[]{:T(128)} %constant.390.clone.1..sunk.1, s32[]{:T(128)} %constant.390.clone.1..sunk.1, s32[]{:T(128)} %constant.390.clone.1..sunk.1, s32[]{:T(128)} %constant.390.clone.1..sunk.1) | dynamic-update-slice | bytes 2883588 | tf_op jit(solution)/shard_map/while/body/jit(dynamic_update_index_in_dim)/dynamic_update_slice | solution.py:72
  885.7 5.8 squeeze_reshape_transpose.9
  927.2 11.5 collective-permute-start.54
  947.6 7.7 collective-permute-done.55
  967.6 7.1 collective-permute-start.63
  974.7 6.8 collective-permute-done.63
  991.5 6.3 fusion.270
  1005.7 10.5 multiply_reduce_fusion.7
  1017.8 32.6 %collective-permute-done.77 = bf16[192,1408]{1,0:T(8,128)(2,1)} collective-permute-done((bf16[192,1408]{1,0:T(8,128)(2,1)}, bf16[192,1408]{1,0:T(8,128)(2,1)}, u32[]{:S(2)}, u32[]{:S(2)}) %collective-permute-start.77) | collective-permute-done | bytes 540704 | tf_op jit(solution)/shard_map/ppermute | solution.py:484
  1075.4 9.1 all-gather.7
  1104.2 15.0 %collective-permute-done.40 = f32[5,128]{1,0:T(8,128)S(1)} collective-permute-done((f32[5,128]{1,0:T(8,128)S(1)}, f32[5,128]{1,0:T(8,128)S(1)}, u32[]{:S(2)}, u32[]{:S(2)}) %collective-permute-start.40) | collective-permute-done | bytes 2592 | tf_op jit(solution)/shard_map/ppermute | solution.py:577
  1119.2 10.3 collective-permute-start.41
  1157.4 6.8 collective-permute-done.60
  1164.2 7.3 collective-permute-done.59
  1172.0 13.3 collective-permute-start.62
  1187.2 39.1 %all-gather.6 = f32[16,1,1408]{2,1,0:T(1,128)S(1)} all-gather(f32[1,1,1408]{2,1,0:T(1,128)S(1)} %reshape.1525), channel_id=7, replica_groups=mesh['chip'=4,'core'=2,'tensor'=4] {'chip','tensor'}, dimensions={0}, use_global_device_ids=true | all-gather | bytes 95744 | tf_op jit(solution)/shard_map/all_gather | solution.py:868
  1226.9 16.0 %psum.14 = f32[2,1408]{1,0:T(2,128)S(1)} all-reduce(f32[2,1408]{1,0:T(2,128)S(1)} %fusion.202), channel_id=1, replica_groups=mesh['chip'=4,'core'=2,'tensor'=4] {'tensor'}, use_global_device_ids=true, to_apply=%region_56.57 | all-reduce | flops 2816 | bytes 22528 | tf_op jit(solution)/shard_map/psum | solution.py:878
  1244.5 10.9 collective-permute-start.82
  1257.4 7.2 collective-permute-done.82
  1264.6 17.8 %collective-permute-done.81 = bf16[192,1408]{1,0:T(8,128)(2,1)S(1)} collective-permute-done((bf16[192,1408]{1,0:T(8,128)(2,1)S(1)}, bf16[192,1408]{1,0:T(8,128)(2,1)S(1)}, u32[]{:S(2)}, u32[]{:S(2)}) %collective-permute-start.81) | collective-permute-done | bytes 540704 | tf_op jit(solution)/shard_map/ppermute | solution.py:484
  1302.6 7.6 collective-permute-done.74
  1310.2 23.6 %collective-permute-start.64 = (bf16[88,1408]{1,0:T(8,128)(2,1)S(1)}, bf16[88,1408]{1,0:T(8,128)(2,1)S(1)}, u32[]{:S(2)}, u32[]{:S(2)}) collective-permute-start(bf16[88,1408]{1,0:T(8,128)(2,1)S(1)} %get-tuple-element.763), channel_id=1, source_target_pairs={{0,1},{1,2},{2,3},{3,0},{4,5},{5,6},{6,7},{7,4},{8,9},{9,10},{10,1... | collective-permute-start | bytes 743432 | tf_op jit(solution)/shard_map/ppermute | solution.py:484
  1333.8 8.9 collective-permute-done.73
  1349.0 16.8 %all_gather.66 = bf16[352,1408]{1,0:T(8,128)(2,1)S(1)} all-gather(bf16[88,1408]{1,0:T(8,128)(2,1)S(1)} %add_convert_fusion.12), channel_id=1, replica_groups=mesh['chip'=4,'core'=2,'tensor'=4] {'chip'}, dimensions={0}, use_global_device_ids=true | all-gather | bytes 1239040 | tf_op jit(solution)/shard_map/all_gather | solution.py:610
  1380.8 9.9 collective-permute-done.70
  1390.7 28.0 %collective-permute-done.69 = bf16[176,1408]{1,0:T(8,128)(2,1)S(1)} collective-permute-done((bf16[176,1408]{1,0:T(8,128)(2,1)}, bf16[176,1408]{1,0:T(8,128)(2,1)S(1)}, u32[]{:S(2)}, u32[]{:S(2)}) %collective-permute-start.69) | collective-permute-done | bytes 495648 | tf_op jit(solution)/shard_map/ppermute | solution.py:484
  1427.1 9.3 copy.162
  1442.4 14.7 all-gather.18.cloned.1.call-done
  (1070 shorter events, 620.9 us)
Async XLA Ops:
  7.2 140.2 %all-gather.26.cloned.1.call-start = ((), (), s32[]{:S(2)}) async-start(), calls=%async_computation.15 | async-start | bytes 4956160 | tf_op jit(solution)/shard_map/all_gather | solution.py:627
  15.6 21.1 %collective-permute-start.1 = (bf16[88,1408]{1,0:T(8,128)(2,1)S(1)}, bf16[88,1408]{1,0:T(8,128)(2,1)S(1)}, u32[]{:S(2)}, u32[]{:S(2)}) collective-permute-start(bf16[88,1408]{1,0:T(8,128)(2,1)S(1)} %get-tuple-element.766), channel_id=1, source_target_pairs={{0,2},{1,3},{2,0},{3,1},{4,6},{5,7},{6,4},{7,5},{8,10},{9,11},{10,... | collective-permute-start | bytes 743432 | tf_op jit(solution)/shard_map/ppermute | solution.py:480
  15.6 21.8 %collective-permute-start.2 = (bf16[88,1408]{1,0:T(8,128)(2,1)S(1)}, bf16[88,1408]{1,0:T(8,128)(2,1)S(1)}, u32[]{:S(2)}, u32[]{:S(2)}) collective-permute-start(bf16[88,1408]{1,0:T(8,128)(2,1)S(1)} %get-tuple-element.766), channel_id=1, source_target_pairs={{0,1},{1,2},{2,3},{3,0},{4,5},{5,6},{6,7},{7,4},{8,9},{9,10},{10,1... | collective-permute-start | bytes 743432 | tf_op jit(solution)/shard_map/ppermute | solution.py:480
  45.9 227.7 %all-gather.28.cloned.1.call-start = ((), (), s32[]{:S(2)}) async-start(), calls=%async_computation.16 | async-start | bytes 7434240 | tf_op jit(solution)/shard_map/all_gather | solution.py:599
  49.4 35.3 %collective-permute-start.14 = (bf16[176,1408]{1,0:T(8,128)(2,1)S(1)}, bf16[176,1408]{1,0:T(8,128)(2,1)S(1)}, u32[]{:S(2)}, u32[]{:S(2)}) collective-permute-start(bf16[176,1408]{1,0:T(8,128)(2,1)S(1)} %dynamic-slice_bitcast_fusion.12), channel_id=1, source_target_pairs={{0,2},{1,3},{2,0},{3,1},{4,6},{5,7},{6,4},{7,5},{8,10},{9,11},{10,... | collective-permute-start | bytes 1486856 | tf_op jit(solution)/shard_map/ppermute | solution.py:480
  51.4 33.3 %collective-permute-start.13 = (bf16[176,1408]{1,0:T(8,128)(2,1)S(1)}, bf16[176,1408]{1,0:T(8,128)(2,1)S(1)}, u32[]{:S(2)}, u32[]{:S(2)}) collective-permute-start(bf16[176,1408]{1,0:T(8,128)(2,1)S(1)} %dynamic-slice_bitcast_fusion.12), channel_id=1, source_target_pairs={{0,3},{1,0},{2,1},{3,2},{4,7},{5,4},{6,5},{7,6},{8,11},{9,8},{10,9... | collective-permute-start | bytes 1486856 | tf_op jit(solution)/shard_map/ppermute | solution.py:480
  86.0 275.1 %all-gather.30.cloned.1.call-start = ((), (), s32[]{:S(2)}) async-start(), calls=%async_computation.17 | async-start | bytes 7434240 | tf_op jit(solution)/shard_map/all_gather | solution.py:599
  87.0 66.9 %collective-permute-start.4 = (f32[3,352]{1,0:T(4,128)S(1)}, f32[3,352]{1,0:T(4,128)S(1)}, u32[]{:S(2)}, u32[]{:S(2)}) collective-permute-start(f32[3,352]{1,0:T(4,128)S(1)} %pad_maximum_fusion.40), channel_id=1, source_target_pairs={{0,3},{1,0},{2,1},{3,2},{4,7},{5,4},{6,5},{7,6},{8,11},{9,8},{10,9... | collective-permute-start | bytes 12680 | tf_op jit(solution)/shard_map/ppermute | solution.py:480
  98.9 55.0 %collective-permute-start.5 = (f32[3,352]{1,0:T(4,128)S(1)}, f32[3,352]{1,0:T(4,128)S(1)}, u32[]{:S(2)}, u32[]{:S(2)}) collective-permute-start(f32[3,352]{1,0:T(4,128)S(1)} %pad_maximum_fusion.40), channel_id=1, source_target_pairs={{0,2},{1,3},{2,0},{3,1},{4,6},{5,7},{6,4},{7,5},{8,10},{9,11},{10,... | collective-permute-start | bytes 12680 | tf_op jit(solution)/shard_map/ppermute | solution.py:480
  103.7 35.9 %collective-permute-start.20 = (bf16[176,1408]{1,0:T(8,128)(2,1)S(1)}, bf16[176,1408]{1,0:T(8,128)(2,1)}, u32[]{:S(2)}, u32[]{:S(2)}) collective-permute-start(bf16[176,1408]{1,0:T(8,128)(2,1)S(1)} %dynamic-slice_bitcast_fusion.7), channel_id=1, source_target_pairs={{0,2},{1,3},{2,0},{3,1},{4,6},{5,7},{6,4},{7,5},{8,10},{9,11},{10,... | collective-permute-start | bytes 1486856 | tf_op jit(solution)/shard_map/ppermute | solution.py:480
  106.0 33.5 %collective-permute-start.19 = (bf16[176,1408]{1,0:T(8,128)(2,1)S(1)}, bf16[176,1408]{1,0:T(8,128)(2,1)}, u32[]{:S(2)}, u32[]{:S(2)}) collective-permute-start(bf16[176,1408]{1,0:T(8,128)(2,1)S(1)} %dynamic-slice_bitcast_fusion.7), channel_id=1, source_target_pairs={{0,3},{1,0},{2,1},{3,2},{4,7},{5,4},{6,5},{7,6},{8,11},{9,8},{10,9... | collective-permute-start | bytes 1486856 | tf_op jit(solution)/shard_map/ppermute | solution.py:480
  120.1 33.9 %collective-permute-start.6 = (f32[3,352]{1,0:T(4,128)S(1)}, f32[3,352]{1,0:T(4,128)S(1)}, u32[]{:S(2)}, u32[]{:S(2)}) collective-permute-start(f32[3,352]{1,0:T(4,128)S(1)} %pad_maximum_fusion.40), channel_id=1, source_target_pairs={{0,1},{1,2},{2,3},{3,0},{4,5},{5,6},{6,7},{7,4},{8,9},{9,10},{10,1... | collective-permute-start | bytes 12680 | tf_op jit(solution)/shard_map/ppermute | solution.py:480
  142.2 304.1 %all-gather.32.cloned.1.call-start = ((), (), s32[]{:S(2)}) async-start(), calls=%async_computation.18 | async-start | bytes 8110080 | tf_op jit(solution)/shard_map/all_gather | solution.py:599
  154.2 26.0 %collective-permute-start.11 = (f32[1409]{0:T(1024)S(1)}, f32[1409]{0:T(1024)S(1)}, u32[]{:S(2)}, u32[]{:S(2)}) collective-permute-start(f32[1409]{0:T(1024)S(1)} %fusion.201), channel_id=1, source_target_pairs={{0,4},{4,0},{1,5},{5,1},{2,6},{6,2},{3,7},{7,3},{8,12},{12,8},{9,1... | collective-permute-start | bytes 16916 | tf_op jit(solution)/shard_map/ppermute | solution.py:476
  164.4 22.3 %collective-permute-start.10 = (bf16[128,1408]{1,0:T(8,128)(2,1)S(1)}, bf16[128,1408]{1,0:T(8,128)(2,1)S(1)}, u32[]{:S(2)}, u32[]{:S(2)}) collective-permute-start(bf16[128,1408]{1,0:T(8,128)(2,1)S(1)} %get-tuple-element.760), channel_id=1, source_target_pairs={{0,5},{1,0},{2,4},{3,1},{4,7},{5,2},{6,6},{7,3},{8,13},{9,8},{10,1... | collective-permute-start | bytes 1081352 | tf_op jit(solution)/shard_map/ppermute | solution.py:568
  175.2 27.0 %collective-permute-start.8 = (bf16[128,1408]{1,0:T(8,128)(2,1)S(1)}, bf16[128,1408]{1,0:T(8,128)(2,1)S(1)}, u32[]{:S(2)}, u32[]{:S(2)}) collective-permute-start(bf16[128,1408]{1,0:T(8,128)(2,1)S(1)} %get-tuple-element.762), channel_id=1, source_target_pairs={{0,4},{1,1},{2,5},{3,0},{4,6},{5,3},{6,7},{7,2},{8,12},{9,9},{10,1... | collective-permute-start | bytes 1081352 | tf_op jit(solution)/shard_map/ppermute | solution.py:568
  179.6 22.7 %collective-permute-start.7 = (bf16[128,1408]{1,0:T(8,128)(2,1)S(1)}, bf16[128,1408]{1,0:T(8,128)(2,1)S(1)}, u32[]{:S(2)}, u32[]{:S(2)}) collective-permute-start(bf16[128,1408]{1,0:T(8,128)(2,1)S(1)} %get-tuple-element.759), channel_id=1, source_target_pairs={{0,0},{1,4},{2,1},{3,5},{4,2},{5,6},{6,3},{7,7},{8,8},{9,12},{10,9... | collective-permute-start | bytes 1081352 | tf_op jit(solution)/shard_map/ppermute | solution.py:568
  180.3 50.6 %collective-permute-start.27 = (bf16[192,1408]{1,0:T(8,128)(2,1)}, bf16[192,1408]{1,0:T(8,128)(2,1)S(1)}, u32[]{:S(2)}, u32[]{:S(2)}) collective-permute-start(bf16[192,1408]{1,0:T(8,128)(2,1)} %dynamic-slice_bitcast_fusion.6), channel_id=1, source_target_pairs={{0,1},{1,2},{2,3},{3,0},{4,5},{5,6},{6,7},{7,4},{8,9},{9,10},{10,1... | collective-permute-start | bytes 1622024 | tf_op jit(solution)/shard_map/ppermute | solution.py:480
  186.6 84.9 %collective-permute-start.26 = (bf16[192,1408]{1,0:T(8,128)(2,1)}, bf16[192,1408]{1,0:T(8,128)(2,1)S(1)}, u32[]{:S(2)}, u32[]{:S(2)}) collective-permute-start(bf16[192,1408]{1,0:T(8,128)(2,1)} %dynamic-slice_bitcast_fusion.6), channel_id=1, source_target_pairs={{0,2},{1,3},{2,0},{3,1},{4,6},{5,7},{6,4},{7,5},{8,10},{9,11},{10,... | collective-permute-start | bytes 1622024 | tf_op jit(solution)/shard_map/ppermute | solution.py:480
  190.3 81.3 %collective-permute-start.25 = (bf16[192,1408]{1,0:T(8,128)(2,1)}, bf16[192,1408]{1,0:T(8,128)(2,1)S(1)}, u32[]{:S(2)}, u32[]{:S(2)}) collective-permute-start(bf16[192,1408]{1,0:T(8,128)(2,1)} %dynamic-slice_bitcast_fusion.6), channel_id=1, source_target_pairs={{0,3},{1,0},{2,1},{3,2},{4,7},{5,4},{6,5},{7,6},{8,11},{9,8},{10,9... | collective-permute-start | bytes 1622024 | tf_op jit(solution)/shard_map/ppermute | solution.py:480
  202.2 148.0 %collective-permute-start.33 = (bf16[192,1408]{1,0:T(8,128)(2,1)}, bf16[192,1408]{1,0:T(8,128)(2,1)}, u32[]{:S(2)}, u32[]{:S(2)}) collective-permute-start(bf16[192,1408]{1,0:T(8,128)(2,1)} %dynamic-slice_bitcast_fusion.5), channel_id=1, source_target_pairs={{0,1},{1,2},{2,3},{3,0},{4,5},{5,6},{6,7},{7,4},{8,9},{9,10},{10,1... | collective-permute-start | bytes 1622024 | tf_op jit(solution)/shard_map/ppermute | solution.py:480
  205.3 72.7 %collective-permute-start.12 = (bf16[512,1408]{1,0:T(8,128)(2,1)}, bf16[512,1408]{1,0:T(8,128)(2,1)}, u32[]{:S(2)}, u32[]{:S(2)}) collective-permute-start(bf16[512,1408]{1,0:T(8,128)(2,1)} %fusion.132), channel_id=1, source_target_pairs={{0,4},{4,0},{1,5},{5,1},{2,6},{6,2},{3,7},{7,3},{8,12},{12,8},{9,1... | collective-permute-start | bytes 4325384 | tf_op jit(solution)/shard_map/ppermute | solution.py:476
  230.8 119.4 %collective-permute-start.32 = (bf16[192,1408]{1,0:T(8,128)(2,1)}, bf16[192,1408]{1,0:T(8,128)(2,1)}, u32[]{:S(2)}, u32[]{:S(2)}) collective-permute-start(bf16[192,1408]{1,0:T(8,128)(2,1)} %dynamic-slice_bitcast_fusion.5), channel_id=1, source_target_pairs={{0,2},{1,3},{2,0},{3,1},{4,6},{5,7},{6,4},{7,5},{8,10},{9,11},{10,... | collective-permute-start | bytes 1622024 | tf_op jit(solution)/shard_map/ppermute | solution.py:480
  271.6 78.7 %collective-permute-start.31 = (bf16[192,1408]{1,0:T(8,128)(2,1)}, bf16[192,1408]{1,0:T(8,128)(2,1)}, u32[]{:S(2)}, u32[]{:S(2)}) collective-permute-start(bf16[192,1408]{1,0:T(8,128)(2,1)} %dynamic-slice_bitcast_fusion.5), channel_id=1, source_target_pairs={{0,3},{1,0},{2,1},{3,2},{4,7},{5,4},{6,5},{7,6},{8,11},{9,8},{10,9... | collective-permute-start | bytes 1622024 | tf_op jit(solution)/shard_map/ppermute | solution.py:480
  273.0 181.1 %all-gather.34.cloned.1.call-start = ((), (), s32[]{:S(2)}) async-start(), calls=%async_computation.19 | async-start | bytes 8110080 | tf_op jit(solution)/shard_map/all_gather | solution.py:599
  353.2 644.6 %reduce-scatter.12.cloned.1.call-start = ((), (), s32[]{:S(2)}) async-start(), calls=%async_computation.11 | async-start | bytes 10813440 | tf_op jit(solution)/shard_map/reduce_scatter | solution.py:604
  416.0 26.9 %collective-permute-start.45 = (bf16[128,1408]{1,0:T(8,128)(2,1)}, bf16[128,1408]{1,0:T(8,128)(2,1)}, u32[]{:S(2)}, u32[]{:S(2)}) collective-permute-start(bf16[128,1408]{1,0:T(8,128)(2,1)} %get-tuple-element.753), channel_id=1, source_target_pairs={{0,1},{1,5},{2,0},{3,4},{4,3},{5,7},{6,2},{7,6},{8,9},{9,13},{10,8... | collective-permute-start | bytes 1081352 | tf_op jit(solution)/shard_map/ppermute | solution.py:568
  419.9 23.1 %collective-permute-start.44 = (bf16[128,1408]{1,0:T(8,128)(2,1)}, bf16[128,1408]{1,0:T(8,128)(2,1)}, u32[]{:S(2)}, u32[]{:S(2)}) collective-permute-start(bf16[128,1408]{1,0:T(8,128)(2,1)} %get-tuple-element.754), channel_id=1, source_target_pairs={{0,4},{1,1},{2,5},{3,0},{4,6},{5,3},{6,7},{7,2},{8,12},{9,9},{10,1... | collective-permute-start | bytes 1081352 | tf_op jit(solution)/shard_map/ppermute | solution.py:568
  421.9 21.1 %collective-permute-start.43 = (bf16[128,1408]{1,0:T(8,128)(2,1)S(1)}, bf16[128,1408]{1,0:T(8,128)(2,1)}, u32[]{:S(2)}, u32[]{:S(2)}) collective-permute-start(bf16[128,1408]{1,0:T(8,128)(2,1)S(1)} %get-tuple-element.751), channel_id=1, source_target_pairs={{0,0},{1,4},{2,1},{3,5},{4,2},{5,6},{6,3},{7,7},{8,8},{9,12},{10,9... | collective-permute-start | bytes 1081352 | tf_op jit(solution)/shard_map/ppermute | solution.py:568
  424.9 36.9 %collective-permute-start.24 = (bf16[512,1408]{1,0:T(8,128)(2,1)}, bf16[512,1408]{1,0:T(8,128)(2,1)}, u32[]{:S(2)}, u32[]{:S(2)}) collective-permute-start(bf16[512,1408]{1,0:T(8,128)(2,1)} %add_convert_fusion.4), channel_id=1, source_target_pairs={{0,4},{4,0},{1,5},{5,1},{2,6},{6,2},{3,7},{7,3},{8,12},{12,8},{9,1... | collective-permute-start | bytes 4325384 | tf_op jit(solution)/shard_map/ppermute | solution.py:476
  446.2 31.7 %collective-permute-start.47 = (bf16[512,1408]{1,0:T(8,128)(2,1)}, bf16[512,1408]{1,0:T(8,128)(2,1)}, u32[]{:S(2)}, u32[]{:S(2)}) collective-permute-start(bf16[512,1408]{1,0:T(8,128)(2,1)} %bitcast.151), channel_id=1, source_target_pairs={{0,4},{4,0},{1,5},{5,1},{2,6},{6,2},{3,7},{7,3},{8,12},{12,8},{9,1... | collective-permute-start | bytes 4325384 | tf_op jit(solution)/shard_map/ppermute | solution.py:476
  517.8 725.1 %reduce-scatter.14.cloned.1.call-start = ((), (), s32[]{:S(2)}) async-start(), calls=%async_computation.13 | async-start | bytes 10813440 | tf_op jit(solution)/shard_map/reduce_scatter | solution.py:604
  534.7 37.6 %collective-permute-start.48 = (bf16[512,1408]{1,0:T(8,128)(2,1)}, bf16[512,1408]{1,0:T(8,128)(2,1)}, u32[]{:S(2)}, u32[]{:S(2)}) collective-permute-start(bf16[512,1408]{1,0:T(8,128)(2,1)} %slice.722), channel_id=1, source_target_pairs={{0,4},{4,0},{1,5},{5,1},{2,6},{6,2},{3,7},{7,3},{8,12},{12,8},{9,1... | collective-permute-start | bytes 4325384 | tf_op jit(solution)/shard_map/ppermute | solution.py:476
  571.6 716.1 %reduce-scatter.10.cloned.1.call-start = ((), (), s32[]{:S(2)}) async-start(), calls=%async_computation.9 | async-start | bytes 9912320 | tf_op jit(solution)/shard_map/reduce_scatter | solution.py:604
  725.7 573.9 %reduce-scatter.6.cloned.1.call-start = ((), (), s32[]{:S(2)}) async-start(), calls=%async_computation.6 | async-start | bytes 4956160 | tf_op jit(solution)/shard_map/reduce_scatter | solution.py:604
  927.2 20.4 %collective-permute-start.54 = (bf16[128,1408]{1,0:T(8,128)(2,1)S(1)}, bf16[128,1408]{1,0:T(8,128)(2,1)S(1)}, u32[]{:S(2)}, u32[]{:S(2)}) collective-permute-start(bf16[128,1408]{1,0:T(8,128)(2,1)S(1)} %get-tuple-element.749), channel_id=1, source_target_pairs={{4,0},{1,1},{5,2},{0,3},{6,4},{3,5},{7,6},{2,7},{12,8},{9,9},{13,1... | collective-permute-start | bytes 1081352 | tf_op jit(solution)/shard_map/ppermute | solution.py:577
  938.7 22.0 %collective-permute-start.56 = (bf16[128,1408]{1,0:T(8,128)(2,1)S(1)}, bf16[128,1408]{1,0:T(8,128)(2,1)S(1)}, u32[]{:S(2)}, u32[]{:S(2)}) collective-permute-start(bf16[128,1408]{1,0:T(8,128)(2,1)S(1)} %get-tuple-element.747), channel_id=1, source_target_pairs={{5,0},{0,1},{4,2},{1,3},{7,4},{2,5},{6,6},{3,7},{13,8},{8,9},{12,1... | collective-permute-start | bytes 1081352 | tf_op jit(solution)/shard_map/ppermute | solution.py:577
  990.5 375.2 %all-reduce.10.cloned.1.call-start = ((), (), s32[]{:S(2)}) async-start(), calls=%async_computation.5 | async-start | bytes 188416 | tf_op jit(solution)/shard_map/psum | solution.py:922
  1004.4 46.1 %collective-permute-start.77 = (bf16[192,1408]{1,0:T(8,128)(2,1)}, bf16[192,1408]{1,0:T(8,128)(2,1)}, u32[]{:S(2)}, u32[]{:S(2)}) collective-permute-start(bf16[192,1408]{1,0:T(8,128)(2,1)} %get-tuple-element.712), channel_id=1, source_target_pairs={{0,2},{1,3},{2,0},{3,1},{4,6},{5,7},{6,4},{7,5},{8,10},{9,11},{10,... | collective-permute-start | bytes 1622024 | tf_op jit(solution)/shard_map/ppermute | solution.py:484
  1004.5 46.0 %collective-permute-start.76 = (bf16[192,1408]{1,0:T(8,128)(2,1)S(1)}, bf16[192,1408]{1,0:T(8,128)(2,1)}, u32[]{:S(2)}, u32[]{:S(2)}) collective-permute-start(bf16[192,1408]{1,0:T(8,128)(2,1)S(1)} %get-tuple-element.710), channel_id=1, source_target_pairs={{0,1},{1,2},{2,3},{3,0},{4,5},{5,6},{6,7},{7,4},{8,9},{9,10},{10,1... | collective-permute-start | bytes 1622024 | tf_op jit(solution)/shard_map/ppermute | solution.py:484
  1017.8 350.9 %all-gather.22.cloned.1.call-start = ((), (), s32[]{:S(2)}) async-start(), calls=%async_computation.12 | async-start | bytes 2703360 | tf_op jit(solution)/shard_map/all_gather | solution.py:610
  1053.1 320.4 %reduce-scatter.8.cloned.1.call-start = ((), (), s32[]{:S(2)}) async-start(), calls=%async_computation.7 | async-start | bytes 9912320 | tf_op jit(solution)/shard_map/reduce_scatter | solution.py:604
  1074.7 306.0 %all-gather.24.cloned.1.call-start = ((), (), s32[]{:S(2)}) async-start(), calls=%async_computation.14 | async-start | bytes 2703360 | tf_op jit(solution)/shard_map/all_gather | solution.py:610
  1087.8 48.7 %collective-permute-start.35 = (bf16[128,1408]{1,0:T(8,128)(2,1)}, bf16[128,1408]{1,0:T(8,128)(2,1)}, u32[]{:S(2)}, u32[]{:S(2)}) collective-permute-start(bf16[128,1408]{1,0:T(8,128)(2,1)} %get-tuple-element.758), channel_id=1, source_target_pairs={{0,0},{4,1},{1,2},{5,3},{2,4},{6,5},{3,6},{7,7},{8,8},{12,9},{9,10... | collective-permute-start | bytes 1081352 | tf_op jit(solution)/shard_map/ppermute | solution.py:577
  1092.3 45.3 %collective-permute-start.36 = (bf16[128,1408]{1,0:T(8,128)(2,1)}, bf16[128,1408]{1,0:T(8,128)(2,1)}, u32[]{:S(2)}, u32[]{:S(2)}) collective-permute-start(bf16[128,1408]{1,0:T(8,128)(2,1)} %get-tuple-element.757), channel_id=1, source_target_pairs={{4,0},{1,1},{5,2},{0,3},{6,4},{3,5},{7,6},{2,7},{12,8},{9,9},{13,1... | collective-permute-start | bytes 1081352 | tf_op jit(solution)/shard_map/ppermute | solution.py:577
  1097.6 41.1 %collective-permute-start.37 = (bf16[128,1408]{1,0:T(8,128)(2,1)}, bf16[128,1408]{1,0:T(8,128)(2,1)}, u32[]{:S(2)}, u32[]{:S(2)}) collective-permute-start(bf16[128,1408]{1,0:T(8,128)(2,1)} %get-tuple-element.756), channel_id=1, source_target_pairs={{1,0},{5,1},{0,2},{4,3},{3,4},{7,5},{2,6},{6,7},{9,8},{13,9},{8,10... | collective-permute-start | bytes 1081352 | tf_op jit(solution)/shard_map/ppermute | solution.py:577
  1097.6 42.1 %collective-permute-start.38 = (bf16[128,1408]{1,0:T(8,128)(2,1)}, bf16[128,1408]{1,0:T(8,128)(2,1)}, u32[]{:S(2)}, u32[]{:S(2)}) collective-permute-start(bf16[128,1408]{1,0:T(8,128)(2,1)} %get-tuple-element.755), channel_id=1, source_target_pairs={{5,0},{0,1},{4,2},{1,3},{7,4},{2,5},{6,6},{3,7},{13,8},{8,9},{12,1... | collective-permute-start | bytes 1081352 | tf_op jit(solution)/shard_map/ppermute | solution.py:577
  1152.5 18.9 %collective-permute-start.59 = (bf16[128,1408]{1,0:T(8,128)(2,1)S(1)}, bf16[128,1408]{1,0:T(8,128)(2,1)S(1)}, u32[]{:S(2)}, u32[]{:S(2)}) collective-permute-start(bf16[128,1408]{1,0:T(8,128)(2,1)S(1)} %add_convert_fusion.10), channel_id=1, source_target_pairs={{0,1},{1,3},{2,5},{3,7},{4,2},{5,0},{6,6},{7,4},{8,9},{9,11},{10,1... | collective-permute-start | bytes 1081352 | tf_op jit(solution)/shard_map/ppermute | solution.py:893
  1244.5 20.1 %collective-permute-start.82 = (bf16[192,1408]{1,0:T(8,128)(2,1)S(1)}, bf16[192,1408]{1,0:T(8,128)(2,1)S(1)}, u32[]{:S(2)}, u32[]{:S(2)}) collective-permute-start(bf16[192,1408]{1,0:T(8,128)(2,1)S(1)} %get-tuple-element.708), channel_id=1, source_target_pairs={{0,3},{1,0},{2,1},{3,2},{4,7},{5,4},{6,5},{7,6},{8,11},{9,8},{10,9... | collective-permute-start | bytes 1622024 | tf_op jit(solution)/shard_map/ppermute | solution.py:484
  1255.4 27.0 %collective-permute-start.81 = (bf16[192,1408]{1,0:T(8,128)(2,1)S(1)}, bf16[192,1408]{1,0:T(8,128)(2,1)S(1)}, u32[]{:S(2)}, u32[]{:S(2)}) collective-permute-start(bf16[192,1408]{1,0:T(8,128)(2,1)S(1)} %get-tuple-element.709), channel_id=1, source_target_pairs={{0,2},{1,3},{2,0},{3,1},{4,6},{5,7},{6,4},{7,5},{8,10},{9,11},{10,... | collective-permute-start | bytes 1622024 | tf_op jit(solution)/shard_map/ppermute | solution.py:484
  1255.4 27.0 %collective-permute-start.80 = (bf16[192,1408]{1,0:T(8,128)(2,1)S(1)}, bf16[192,1408]{1,0:T(8,128)(2,1)S(1)}, u32[]{:S(2)}, u32[]{:S(2)}) collective-permute-start(bf16[192,1408]{1,0:T(8,128)(2,1)S(1)} %get-tuple-element.707), channel_id=1, source_target_pairs={{0,1},{1,2},{2,3},{3,0},{4,5},{5,6},{6,7},{7,4},{8,9},{9,10},{10,1... | collective-permute-start | bytes 1622024 | tf_op jit(solution)/shard_map/ppermute | solution.py:484
  1284.6 136.4 %all-gather.20.cloned.1.call-start = ((), (), s32[]{:S(2)}) async-start(), calls=%async_computation.10 | async-start | bytes 2478080 | tf_op jit(solution)/shard_map/all_gather | solution.py:610
  1290.4 19.8 %collective-permute-start.74 = (bf16[176,1408]{1,0:T(8,128)(2,1)}, bf16[176,1408]{1,0:T(8,128)(2,1)S(1)}, u32[]{:S(2)}, u32[]{:S(2)}) collective-permute-start(bf16[176,1408]{1,0:T(8,128)(2,1)} %get-tuple-element.722), channel_id=1, source_target_pairs={{0,3},{1,0},{2,1},{3,2},{4,7},{5,4},{6,5},{7,6},{8,11},{9,8},{10,9... | collective-permute-start | bytes 1486856 | tf_op jit(solution)/shard_map/ppermute | solution.py:484
  1290.4 52.3 %collective-permute-start.73 = (bf16[176,1408]{1,0:T(8,128)(2,1)}, bf16[176,1408]{1,0:T(8,128)(2,1)}, u32[]{:S(2)}, u32[]{:S(2)}) collective-permute-start(bf16[176,1408]{1,0:T(8,128)(2,1)} %get-tuple-element.723), channel_id=1, source_target_pairs={{0,2},{1,3},{2,0},{3,1},{4,6},{5,7},{6,4},{7,5},{8,10},{9,11},{10,... | collective-permute-start | bytes 1486856 | tf_op jit(solution)/shard_map/ppermute | solution.py:484
  1292.3 50.3 %collective-permute-start.72 = (bf16[176,1408]{1,0:T(8,128)(2,1)}, bf16[176,1408]{1,0:T(8,128)(2,1)}, u32[]{:S(2)}, u32[]{:S(2)}) collective-permute-start(bf16[176,1408]{1,0:T(8,128)(2,1)} %get-tuple-element.721), channel_id=1, source_target_pairs={{0,1},{1,2},{2,3},{3,0},{4,5},{5,6},{6,7},{7,4},{8,9},{9,10},{10,1... | collective-permute-start | bytes 1486856 | tf_op jit(solution)/shard_map/ppermute | solution.py:484
  1300.8 44.3 %collective-permute-start.66 = (bf16[88,1408]{1,0:T(8,128)(2,1)S(1)}, bf16[88,1408]{1,0:T(8,128)(2,1)S(1)}, u32[]{:S(2)}, u32[]{:S(2)}) collective-permute-start(bf16[88,1408]{1,0:T(8,128)(2,1)S(1)} %get-tuple-element.764), channel_id=1, source_target_pairs={{0,3},{1,0},{2,1},{3,2},{4,7},{5,4},{6,5},{7,6},{8,11},{9,8},{10,9... | collective-permute-start | bytes 743432 | tf_op jit(solution)/shard_map/ppermute | solution.py:484
  1302.6 45.3 %collective-permute-start.65 = (bf16[88,1408]{1,0:T(8,128)(2,1)S(1)}, bf16[88,1408]{1,0:T(8,128)(2,1)S(1)}, u32[]{:S(2)}, u32[]{:S(2)}) collective-permute-start(bf16[88,1408]{1,0:T(8,128)(2,1)S(1)} %get-tuple-element.765), channel_id=1, source_target_pairs={{0,2},{1,3},{2,0},{3,1},{4,6},{5,7},{6,4},{7,5},{8,10},{9,11},{10,... | collective-permute-start | bytes 743432 | tf_op jit(solution)/shard_map/ppermute | solution.py:484
  1310.2 37.7 %collective-permute-start.64 = (bf16[88,1408]{1,0:T(8,128)(2,1)S(1)}, bf16[88,1408]{1,0:T(8,128)(2,1)S(1)}, u32[]{:S(2)}, u32[]{:S(2)}) collective-permute-start(bf16[88,1408]{1,0:T(8,128)(2,1)S(1)} %get-tuple-element.763), channel_id=1, source_target_pairs={{0,1},{1,2},{2,3},{3,0},{4,5},{5,6},{6,7},{7,4},{8,9},{9,10},{10,1... | collective-permute-start | bytes 743432 | tf_op jit(solution)/shard_map/ppermute | solution.py:484
  1345.0 112.1 %all-gather.18.cloned.1.call-start = ((), (), s32[]{:S(2)}) async-start(), calls=%async_computation.8 | async-start | bytes 2478080 | tf_op jit(solution)/shard_map/all_gather | solution.py:610
  1368.7 52.3 %collective-permute-start.79 = (bf16[4,192,1408]{2,1,0:T(8,128)(2,1)}, bf16[4,192,1408]{2,1,0:T(8,128)(2,1)}, u32[]{:S(2)}, u32[]{:S(2)}) collective-permute-start(bf16[4,192,1408]{2,1,0:T(8,128)(2,1)} %bitcast.924), channel_id=1, source_target_pairs={{0,4},{4,0},{1,5},{5,1},{2,6},{6,2},{3,7},{7,3},{8,12},{12,8},{9,1... | collective-permute-start | bytes 6488072 | tf_op jit(solution)/shard_map/ppermute | solution.py:476
  1376.2 42.5 %collective-permute-start.69 = (bf16[176,1408]{1,0:T(8,128)(2,1)}, bf16[176,1408]{1,0:T(8,128)(2,1)S(1)}, u32[]{:S(2)}, u32[]{:S(2)}) collective-permute-start(bf16[176,1408]{1,0:T(8,128)(2,1)} %get-tuple-element.734), channel_id=1, source_target_pairs={{0,2},{1,3},{2,0},{3,1},{4,6},{5,7},{6,4},{7,5},{8,10},{9,11},{10,... | collective-permute-start | bytes 1486856 | tf_op jit(solution)/shard_map/ppermute | solution.py:484
  1376.2 42.5 %collective-permute-start.68 = (bf16[176,1408]{1,0:T(8,128)(2,1)}, bf16[176,1408]{1,0:T(8,128)(2,1)}, u32[]{:S(2)}, u32[]{:S(2)}) collective-permute-start(bf16[176,1408]{1,0:T(8,128)(2,1)} %get-tuple-element.732), channel_id=1, source_target_pairs={{0,1},{1,2},{2,3},{3,0},{4,5},{5,6},{6,7},{7,4},{8,9},{9,10},{10,1... | collective-permute-start | bytes 1486856 | tf_op jit(solution)/shard_map/ppermute | solution.py:484
  1380.8 55.6 %collective-permute-start.83 = (bf16[4,192,1408]{2,1,0:T(8,128)(2,1)}, bf16[4,192,1408]{2,1,0:T(8,128)(2,1)}, u32[]{:S(2)}, u32[]{:S(2)}) collective-permute-start(bf16[4,192,1408]{2,1,0:T(8,128)(2,1)} %bitcast.926), channel_id=1, source_target_pairs={{0,4},{4,0},{1,5},{5,1},{2,6},{6,2},{3,7},{7,3},{8,12},{12,8},{9,1... | collective-permute-start | bytes 6488072 | tf_op jit(solution)/shard_map/ppermute | solution.py:476
  1420.9 36.2 %collective-permute-start.75 = (bf16[4,176,1408]{2,1,0:T(8,128)(2,1)}, bf16[4,176,1408]{2,1,0:T(8,128)(2,1)}, u32[]{:S(2)}, u32[]{:S(2)}) collective-permute-start(bf16[4,176,1408]{2,1,0:T(8,128)(2,1)} %bitcast.938), channel_id=1, source_target_pairs={{0,4},{4,0},{1,5},{5,1},{2,6},{6,2},{3,7},{7,3},{8,12},{12,8},{9,1... | collective-permute-start | bytes 5947400 | tf_op jit(solution)/shard_map/ppermute | solution.py:476
  (282 other events, 3030.2 us)
Sparse Core Ops, SparseCore 0:
  46.0 50.5 all-gather.25
  99.0 67.2 all-gather.27
  168.8 67.2 all-gather.29
  273.1 81.5 all-gather.31
  357.0 73.5 all-gather.33
  517.9 94.5 reduce-scatter.11
  616.2 88.5 reduce-scatter.13
  725.8 88.9 reduce-scatter.9
  990.7 51.8 reduce-scatter.5
  1047.9 135.8 all-reduce.9
  1186.2 38.6 all-gather.21
  1228.5 82.5 reduce-scatter.7
  1313.5 35.8 all-gather.23
  1351.7 35.6 all-gather.19
  1421.0 36.0 all-gather.17

commit v2 on v1

--- a/solution.py
+++ b/solution.py
@@ -1,8 +1,11 @@
+import functools
 from functools import partial
 
 import jax
 import jax.numpy as jnp
 from jax import lax
+from jax.experimental import pallas as pl
+from jax.experimental.pallas import tpu as pltpu
 from jax.sharding import Mesh
 from jax.sharding import PartitionSpec as P
 
@@ -468,6 +471,246 @@
     ) + tuple(weight_sums)
 
 
+LANES = 128
+LOG2E = 1.4426950408889634
+
+
+def lane_index(shape):
+    return lax.broadcasted_iota(jnp.int32, shape, 1)
+
+
+def matmul_nt(left, right):
+    return lax.dot_general(left, right, (((1,), (1,)), ((), ())), preferred_element_type=jnp.float32)
+
+
+def matmul_nn(left, right):
+    return lax.dot_general(left, right, (((1,), (0,)), ((), ())), preferred_element_type=jnp.float32)
+
+
+def matmul_tn(left, right):
+    return lax.dot_general(left, right, (((0,), (0,)), ((), ())), preferred_element_type=jnp.float32)
+
+
+def row_sums(rows, both_parts=False):
+    ones = jnp.ones((LANES, LANES), jnp.bfloat16)
+    high = rows.astype(jnp.bfloat16)
+    total = matmul_nn(high, ones)
+    if both_parts:
+        total = total + matmul_nn((rows - high.astype(jnp.float32)).astype(jnp.bfloat16), ones)
+    return total
+
+
+def norm_rows(raw):
+    center = raw - row_sums(raw, True) * (1.0 / HD)
+    center = jnp.where(lane_index(raw.shape) < HD, center, 0.0)
+    inverse = lax.rsqrt(row_sums(center * center) * (1.0 / HD) + EPSILON)
+    return center * inverse, inverse
+
+
+def norm_rows_back(grad, normed, inverse):
+    mean = row_sums(grad) * (1.0 / HD)
+    along = row_sums(grad * normed) * (1.0 / HD)
+    return jnp.where(lane_index(grad.shape) < HD, inverse * (grad - mean - normed * along), 0.0)
+
+
+def turn_rows(rows, tables):
+    quarter = HD // 4
+    return (
+        rows * tables[0]
+        + pltpu.roll(rows, LANES - quarter, 1) * tables[1]
+        + pltpu.roll(rows, quarter, 1) * tables[2]
+    )
+
+
+def turn_rows_back(grad, tables):
+    quarter = HD // 4
+    return (
+        grad * tables[0]
+        + pltpu.roll(grad * tables[1], quarter, 1)
+        + pltpu.roll(grad * tables[2], LANES - quarter, 1)
+    )
+
+
+def kept_keys(count_ref, shape):
+    return lax.broadcasted_iota(jnp.int32, shape, 0).astype(jnp.float32) < count_ref[0:1, :]
+
+
+def attention_kernel(turned, rows, *refs):
+    if turned:
+        q_ref, k_ref, v_ref, gain_ref, count_ref, table_ref, out_ref, inv_ref = refs
+    else:
+        q_ref, k_ref, v_ref, gain_ref, count_ref, out_ref, inv_ref = refs
+    low = jnp.bfloat16
+    keys = norm_rows(k_ref[...])[0] * gain_ref[1:2, :]
+    if turned:
+        keys = turn_rows(keys, (table_ref[0], table_ref[1], table_ref[2]))
+    values = v_ref[...]
+    ones = jnp.ones(values.shape, jnp.float32)
+    if not turned:
+        kept = kept_keys(count_ref, values.shape)
+        keys = jnp.where(kept, keys, 0.0)
+        values = jnp.where(kept, values, 0.0)
+        ones = jnp.where(kept, ones, 0.0)
+    keys = keys.astype(low)
+    mixed = jnp.concatenate([values.astype(low), ones.astype(low)], 1)
+    for start in range(0, q_ref.shape[0], rows):
+        part = pl.ds(start, rows)
+        query = norm_rows(q_ref[part, :])[0] * gain_ref[0:1, :]
+        if turned:
+            query = turn_rows(query, tuple(table_ref[i, part, :] for i in range(3)))
+        powers = jnp.exp2(matmul_nt(query.astype(low), keys)).astype(low)
+        sums = matmul_nn(powers, mixed)
+        inverse = 1.0 / sums[:, LANES:]
+        out_ref[part, :] = (sums[:, :LANES] * inverse).astype(low)
+        inv_ref[part, :] = inverse
+
+
+def attention_back_kernel(turned, rows, *refs):
+    if turned:
+        q_ref, k_ref, v_ref, gain_ref, count_ref, table_ref = refs[:6]
+        refs = refs[6:]
+    else:
+        q_ref, k_ref, v_ref, gain_ref, count_ref = refs[:5]
+        refs = refs[5:]
+    grad_ref, out_ref, inv_ref, dq_ref, dk_ref, dv_ref, dgain_ref, keys_acc, values_acc = refs
+    low = jnp.bfloat16
+    f32 = jnp.float32
+    key_normed, key_inverse = norm_rows(k_ref[...])
+    keys = key_normed * gain_ref[1:2, :]
+    if turned:
+        keys = turn_rows(keys, (table_ref[0], table_ref[1], table_ref[2]))
+    else:
+        kept = kept_keys(count_ref, keys.shape)
+        keys = jnp.where(kept, keys, 0.0)
+    keys = keys.astype(low)
+    lane = lane_index(k_ref.shape)
+    values = jnp.where((lane == HD) | (lane == HD + 1), 1.0, v_ref[...]).astype(low)
+    factor = HD ** (-0.5)
+    gain_total = jnp.zeros((1, LANES), f32)
+    for start in range(0, q_ref.shape[0], rows):
+        part = pl.ds(start, rows)
+        query_normed, query_inverse = norm_rows(q_ref[part, :])
+        query = query_normed * gain_ref[0:1, :]
+        if turned:
+            tables = tuple(table_ref[i, part, :] for i in range(3))
+            query = turn_rows(query, tables)
+        query = query.astype(low)
+        grad = grad_ref[part, :].astype(f32) * inv_ref[part, :]
+        delta = row_sums(grad * out_ref[part, :].astype(f32))
+        delta_high = delta.astype(low).astype(f32)
+        lane = lane_index((rows, LANES))
+        grad_low = grad.astype(low)
+        grad_more = jnp.where(
+            lane == HD, -delta_high, jnp.where(lane == HD + 1, delta_high - delta, grad)
+        ).astype(low)
+        powers = jnp.exp2(matmul_nt(keys, query))
+        score_grad = (powers * matmul_nt(values, grad_more)).astype(low)
+        values_part = matmul_nn(powers.astype(low), grad_low)
+        keys_part = matmul_nn(score_grad, query)
+        if start == 0:
+            values_acc[...] = values_part
+            keys_acc[...] = keys_part
+        else:
+            values_acc[...] += values_part
+            keys_acc[...] += keys_part
+        query_grad = matmul_tn(score_grad, keys) * factor
+        if turned:
+            query_grad = turn_rows_back(query_grad, tables)
+        gain_total = gain_total + jnp.sum(query_grad * query_normed, 0, keepdims=True)
+        dq_ref[part, :] = norm_rows_back(
+            query_grad * gain_ref[2:3, :], query_normed, query_inverse
+        ).astype(low)
+    values_grad = values_acc[...]
+    key_grad = keys_acc[...] * (1.0 / LOG2E)
+    if turned:
+        key_grad = turn_rows_back(key_grad, (table_ref[0], table_ref[1], table_ref[2]))
+    else:
+        kept = kept_keys(count_ref, key_grad.shape)
+        values_grad = jnp.where(kept, values_grad, 0.0)
+        key_grad = jnp.where(kept, key_grad, 0.0)
+    dv_ref[...] = values_grad.astype(low)
+    dk_ref[...] = norm_rows_back(key_grad * gain_ref[1:2, :], key_normed, key_inverse).astype(low)
+    dgain_ref[0, 0:1, :] = gain_total
+    dgain_ref[0, 1:2, :] = jnp.sum(key_grad * key_normed, 0, keepdims=True)
+    dgain_ref[0, 2:8, :] = jnp.zeros((6, LANES), f32)
+
+
+def attention_specs(turned, length, key_length, q_at, k_at, v_at):
+    specs = [
+        pl.BlockSpec((length, LANES), lambda h: (0, q_at + h)),
+        pl.BlockSpec((key_length, LANES), lambda h: (0, k_at + h)),
+        pl.BlockSpec((key_length, LANES), lambda h: (0, v_at + h)),
+        pl.BlockSpec((8, LANES), lambda h: (0, 0)),
+        pl.BlockSpec((8, LANES), lambda h: (0, 0)),
+    ]
+    if turned:
+        specs.append(pl.BlockSpec((3, length, LANES), lambda h: (0, 0, 0)))
+    return specs
+
+
+def attention(heads, query, keys, values, at, gains, count, tables=None, rows=256):
+    length, key_length = query.shape[0], keys.shape[0]
+    turned = tables is not None
+    operands = [query, keys, values, gains, count] + ([tables] if turned else [])
+    pairs = heads * length * key_length
+    return pl.pallas_call(
+        functools.partial(attention_kernel, turned, min(rows, length)),
+        grid=(heads,),
+        in_specs=attention_specs(turned, length, key_length, *at),
+        out_specs=[
+            pl.BlockSpec((length, LANES), lambda h: (0, h)),
+            pl.BlockSpec((length, LANES), lambda h: (0, h)),
+        ],
+        out_shape=[
+            jax.ShapeDtypeStruct((length, heads * LANES), jnp.bfloat16),
+            jax.ShapeDtypeStruct((length, heads * LANES), jnp.float32),
+        ],
+        compiler_params=pltpu.CompilerParams(
+            dimension_semantics=("arbitrary",), vmem_limit_bytes=40 * 2**20
+        ),
+        cost_estimate=pl.CostEstimate(
+            flops=4 * pairs * LANES, transcendentals=pairs, bytes_accessed=18 * heads * length * LANES
+        ),
+        name="attention_turned" if turned else "attention_plain",
+    )(*operands)
+
+
+def attention_back(
+    heads, query, keys, values, at, gains, count, grad, mixed, inverse, tables=None, rows=256
+):
+    length, key_length = query.shape[0], keys.shape[0]
+    turned = tables is not None
+    operands = [query, keys, values, gains, count] + ([tables] if turned else [])
+    pairs = heads * length * key_length
+    return pl.pallas_call(
+        functools.partial(attention_back_kernel, turned, min(rows, length)),
+        grid=(heads,),
+        in_specs=attention_specs(turned, length, key_length, *at)
+        + [pl.BlockSpec((length, LANES), lambda h: (0, h))] * 3,
+        out_specs=[
+            pl.BlockSpec((length, LANES), lambda h: (0, h)),
+            pl.BlockSpec((key_length, LANES), lambda h: (0, h)),
+            pl.BlockSpec((key_length, LANES), lambda h: (0, h)),
+            pl.BlockSpec((1, 8, LANES), lambda h: (h, 0, 0)),
+        ],
+        out_shape=[
+            jax.ShapeDtypeStruct((length, heads * LANES), jnp.bfloat16),
+            jax.ShapeDtypeStruct((key_length, heads * LANES), jnp.bfloat16),
+            jax.ShapeDtypeStruct((key_length, heads * LANES), jnp.bfloat16),
+            jax.ShapeDtypeStruct((heads, 8, LANES), jnp.float32),
+        ],
+        scratch_shapes=[
+            pltpu.VMEM((key_length, LANES), jnp.float32),
+            pltpu.VMEM((key_length, LANES), jnp.float32),
+        ],
+        compiler_params=pltpu.CompilerParams(
+            dimension_semantics=("arbitrary",), vmem_limit_bytes=40 * 2**20
+        ),
+        cost_estimate=pl.CostEstimate(
+            flops=10 * pairs * LANES, transcendentals=pairs, bytes_accessed=30 * heads * length * LANES
+        ),
+        name="attention_turned_back" if turned else "attention_plain_back",
+    )(*operands, grad, mixed, inverse)
 def ring_pairs(size, step):
     return [(rank, (rank + step) % size) for rank in range(size)]
 
@@ -499,6 +742,10 @@
 
 def rolled(array, start):
     return lax.dynamic_slice_in_dim(jnp.concatenate([array, array], 0), start, array.shape[0], 0)
+
+
+def tie(*values):
+    return lax.optimization_barrier(values)
 
 
 def dot_tt(left, right):
@@ -560,6 +807,7 @@
     heads = size * half // HD
     ff_half = up_bias.shape[0] // 2
     ff_part = ff_half // chips
+    lanes = heads * LANES
     at_home = core == rank // sequences
 
     def spread(values):
@@ -593,24 +841,54 @@
     def halve(values):
         return values[:own_len] + swap_cores(values[own_len:].astype(low)).astype(f32)
 
-    def gather_rows(own):
-        mine = pick(own, chip)
+    def quarters(owns):
+        mine = jnp.concatenate([pick(own, chip) for own in owns], 0)
         later = jnp.stack([from_later(mine, step, size) for step in range(1, size)])
-        rest = lax.all_gather(later, "chip", axis=0, tiled=False)
-        return jnp.concatenate([own[:, None], rest], 1)
-
-    def reduce_rows(partial_sums):
+        parts, at = [], 0
+        for own in owns:
+            parts.append(later[:, at : at + own.shape[1]])
+            at += own.shape[1]
+        return parts
+
+    def gather_shares(later):
+        return lax.all_gather(later, "chip", axis=0, tiled=False)
+
+    def gather_rows(own, later):
+        return jnp.concatenate([own[:, None], gather_shares(later)], 1)
+
+    def pad_heads(own, rest):
+        own = own.reshape(own.shape[0], 1, half // HD, HD, width)
+        rest = rest.reshape(own.shape[0], size - 1, half // HD, HD, width)
+        zero = jnp.zeros((), low)
+        nothing = (0, 0, 0)
+        own = lax.pad(own, zero, (nothing, (0, size - 1, 0), nothing, (0, LANES - HD, 0), nothing))
+        rest = lax.pad(rest, zero, (nothing, (1, 0, 0), nothing, (0, LANES - HD, 0), nothing))
+        return (own + rest).reshape(-1, lanes, width)
+
+    def trim_heads(rows):
+        return rows.reshape(heads, LANES, width)[:, :HD].reshape(size, half, width)
+
+    def by_core(own):
+        other = swap_cores(own)
+        return jnp.where(core == 0, own, other), jnp.where(core == 0, other, own)
+
+    def scatter_rows(partial_sums):
         rows = partial_sums.shape[2]
-        parts = lax.psum_scatter(
+        return lax.psum_scatter(
             partial_sums.reshape(chips * size * rows, width), "chip", scatter_dimension=0, tiled=True
         ).reshape(size, rows, width)
-        total = parts[0].astype(f32)
-        for step in range(1, size):
-            total = total + from_earlier(parts[step], step, size).astype(f32)
-        own = lax.all_gather(total.astype(low), "chip", axis=0, tiled=True)
-        own = own.reshape(chips, rows, width)
-        other = swap_cores(own)
-        return jnp.where(core == 0, own, other), jnp.where(core == 0, other, own)
+
+    def send_line(parts):
+        return [from_earlier(parts[step], step, size) for step in range(1, size)]
+
+    def add_line(own, arrived):
+        total = own.astype(f32)
+        for part in arrived:
+            total = total + part.astype(f32)
+        return total.astype(low)
+
+    def share_rows(total):
+        return lax.all_gather(total, "chip", axis=0, tiled=True)
 
     def half_cols(weight):
         return lax.dynamic_slice_in_dim(weight, core * half, half, 1).T
@@ -620,60 +898,79 @@
 
     skip_half = lax.dynamic_slice_in_dim(skip_weight, core * width, width, 0).T
     skip_part = shard // chips
+    (skip_later,) = quarters([skip_half.reshape(chips, skip_part, width)])
     skip_mine = pick(skip_half.reshape(chips, skip_part, width), chip)
-    skip_rel = jnp.stack([skip_mine] + [from_later(skip_mine, step, size) for step in range(1, size)])
-    skip_abs = rolled(skip_rel, (size - rank) % size)
-    skip_own_w = (
-        lax.all_gather(skip_abs, "chip", axis=0, tiled=False)
-        .transpose(1, 0, 2, 3)
-        .reshape(width, width)
-    )
-    skip_other_w = swap_cores(skip_own_w)
+    skip_abs = rolled(jnp.concatenate([skip_mine[None], skip_later], 0), (size - rank) % size)
+    skip_own_w = gather_shares(skip_abs).transpose(1, 0, 2, 3).reshape(width, width)
 
     self_own = jnp.stack(
         [half_cols(query_key_value_weight[i]) for i in range(3)]
         + [half_rows(attention_output_weight)]
     )
-    self_full = gather_rows(self_own).reshape(4, size * half, width)
     cross_own = jnp.stack(
         [half_cols(crossed_query_weight), half_cols(cross_kv_weight[0]), half_cols(cross_kv_weight[1])]
         + [half_rows(crossed_output_weight)]
     )
-    cross_full = gather_rows(cross_own).reshape(4, size * half, width)
     up_own = lax.dynamic_slice_in_dim(up_projection_weight, core * ff_half, ff_half, 1).T
-    up_full = gather_rows(up_own.reshape(chips, ff_part, width)).reshape(size * ff_half, width)
+    up_own = up_own.reshape(chips, ff_part, width)
     down_own = lax.dynamic_slice_in_dim(down_projection_weight, core * ff_half, ff_half, 0)
-    down_full = gather_rows(down_own.reshape(chips, ff_part, width)).reshape(size * ff_half, width)
-
+    down_own = down_own.reshape(chips, ff_part, width)
+    skip_other_w = swap_cores(skip_own_w)
     condition = jax.nn.silu(time_emb.astype(f32))
     ada_weight_f = ada_weight.astype(f32)
     shift_part = jnp.dot(condition, ada_weight_f, precision=PRECISE) + ada_bias.astype(f32)
-    small = jnp.concatenate([shift_part, skip_bias.astype(f32)[None]], 0)
-    small_all = rolled(
-        jnp.stack([small] + [from_later(small, step, size) for step in range(1, size)]),
-        (size - rank) % size,
-    )
-    small_all = small_all.transpose(1, 0, 2).reshape(sequences + 1, width)
-    skip_bias_f = small_all[sequences]
-    shift_length = of_sequence(
-        jnp.concatenate([small_all[:sequences], text_length.astype(f32)[:, None]], 1)
-    )
-    shift_vec = shift_length[:width]
-    own_length = shift_length[width]
+    shift_part = shift_part.reshape(sequences * shard)
+    shift_high = shift_part.astype(low)
+    shift_low = (shift_part - shift_high.astype(f32)).astype(low)
     up_bias_own = lax.dynamic_slice_in_dim(up_bias, core * ff_half, ff_half, 0)
+    small = jnp.concatenate([shift_high, shift_low, skip_bias, up_bias_own])
+    small_size = small.shape[0]
+    small_rows = 8 * -(-small_size // (8 * width))
+    small = jnp.pad(small, (0, small_rows * width - small_size)).reshape(1, small_rows, width)
+    small = jnp.broadcast_to(small, (chips, small_rows, width))
+    self_later, small_later = quarters([self_own, small])
+    (cross_later,) = quarters([cross_own])
+    up_later, down_later = quarters([up_own, down_own])
+    self_full = pad_heads(self_own, gather_shares(self_later))
+    cross_full = pad_heads(cross_own, gather_shares(cross_later))
+
+    small_rel = jnp.concatenate([small[:1], small_later], 0).reshape(size, -1)[:, :small_size].astype(f32)
+    shift_size = sequences * shard
     up_bias_f = (
-        jnp.stack([up_bias_own] + [from_later(up_bias_own, step, size) for step in range(1, size)])
+        small_rel[:, 2 * shift_size + shard :]
         .reshape(size, chips, ff_part)
         .transpose(1, 0, 2)
         .reshape(size * ff_half)
-        .astype(f32)
-    )
+    )
+    small_rel = jnp.concatenate(
+        [
+            small_rel[:, :shift_size] + small_rel[:, shift_size : 2 * shift_size],
+            small_rel[:, 2 * shift_size : 2 * shift_size + shard],
+        ],
+        1,
+    )
+    small_abs = rolled(small_rel, (size - rank) % size)
+    small_abs = small_abs.reshape(size, sequences + 1, shard).transpose(1, 0, 2)
+    small_abs = small_abs.reshape(sequences + 1, width)
+    skip_bias_f = small_abs[sequences]
+    full_len = grid_pos.shape[1]
+    of_mine = of_sequence(
+        jnp.concatenate(
+            [
+                small_abs[:sequences],
+                text_length.astype(f32)[:, None],
+                grid_pos.astype(f32).transpose(0, 2, 1).reshape(sequences, 2 * full_len),
+            ],
+            1,
+        )
+    )
+    shift_vec = of_mine[:width]
+    key_count = jnp.broadcast_to(of_mine[width], (8, LANES))
+    positions = of_mine[width + 1 :].reshape(2, 2 * size, piece_len)
     text_own = of_sequence(text_emb)
-    positions = of_sequence(grid_pos)
     text_size = text_own.shape[0]
-    key_bias = jnp.where(jnp.arange(text_size)[None, :] < own_length, 0.0, -1e30).astype(f32)
-
-    by_piece = positions.reshape(2 * size, piece_len, 2)
+
+    by_piece = positions.transpose(1, 0, 2)
 
     def piece_index(of_core, turn):
         source = (2 * (rank % 2) + of_core - turn) % size
@@ -681,9 +978,26 @@
 
     ordered = jnp.concatenate(
         [pick(by_piece, piece_index(of_core, turn)) for of_core in (core, 1 - core) for turn in range(size)],
-        0,
-    )
-    cosines, sine_table = rope_tables(ordered)
+        1,
+    )
+    lane = jnp.arange(LANES)
+    quarter = lane // (HD // 4)
+    frequency = ROPE_BASE ** (-(lane % (HD // 4)).astype(f32) / (HD // 4))
+    angles = ordered[0][:, None] * jnp.where(quarter < 2, frequency, 0.0)[None, :]
+    angles = angles + ordered[1][:, None] * jnp.where(quarter < 2, 0.0, frequency)[None, :]
+    real_lane = lane < HD
+    sines = jnp.sin(angles)
+    tables = jnp.stack(
+        [
+            jnp.where(real_lane, jnp.cos(angles), 0.0),
+            jnp.where(real_lane & (quarter % 2 == 0), -sines, 0.0),
+            jnp.where(real_lane & (quarter % 2 == 1), sines, 0.0),
+        ]
+    )
+
+    def kernel_gains(gains):
+        rows = jnp.stack([gains[0] * (HD ** (-0.5) * LOG2E), gains[1], gains[0]])
+        return jnp.pad(rows, ((0, 5), (0, LANES - HD)))
 
     skip_gain_f = skip_gain.astype(f32)
     skip_beta_f = skip_beta.astype(f32)
@@ -691,17 +1005,12 @@
     norm2_beta_f = norm2_beta.astype(f32)
     norm3_gain_f = norm3_gain.astype(f32)
     norm3_beta_f = norm3_beta.astype(f32)
-    qk_gain_f = qk_gain.astype(f32)
-    cross_gain_f = cross_qk_gain.astype(f32)
 
     def first_norm(stream_in, shift_in):
         return layer_norm(stream_in) + shift_in[None, :]
 
-    def qk_prep(raw, gain):
-        return rotate(layer_norm(raw.reshape(raw.shape[0], heads, HD)) * gain, cosines, sine_table)
-
-    def head_norm(raw, gain):
-        return layer_norm(raw.reshape(raw.shape[0], heads, HD)) * gain
+    self_gains = kernel_gains(qk_gain.astype(f32))
+    cross_gains = kernel_gains(cross_qk_gain.astype(f32))
 
     latent_f = latent_in.reshape(own_len, width).astype(f32)
     skip_f = skip_in.reshape(own_len, width).astype(f32)
@@ -724,28 +1033,24 @@
     stream_home = (
         dot_tt(normed_own, skip_own_w) + dot_tt(normed_other, skip_other_w) + skip_bias_f
     ).astype(low)
-    stream = spread(stream_home.reshape(size, piece_len, width)).reshape(own_len, width).astype(f32)
-    grad_low = spread(out_grad.reshape(size, piece_len, width)).reshape(own_len, width)
+    stream_low = spread(stream_home.reshape(size, piece_len, width)).reshape(own_len, width)
+    stream = stream_low.astype(f32)
 
     attn_in = both(first_norm(stream, shift_vec).astype(low))
-    projected = [dot_tt(attn_in, self_full[i]) for i in range(3)]
-    query_self = qk_prep(projected[0], qk_gain_f[0]).astype(low)[None]
-    keys_self = qk_prep(projected[1], qk_gain_f[1]).astype(low)[None]
-    values_self = projected[2].reshape(1, 2 * own_len, heads, HD).astype(low)
-    self_bias = jnp.zeros((1, 2 * own_len), f32)
-    attn_result, attn_logsum = attend_forward(query_self, keys_self, values_self, self_bias)
-    attention_combined = attn_result[0].astype(low)
+    projected = dot_tt(attn_in, self_full[:3].reshape(3 * lanes, width))
+    projected, grad_home = tie(projected, out_grad)
+    grad_low = spread(grad_home.reshape(size, piece_len, width)).reshape(own_len, width)
+    self_inputs = (heads, projected, projected, projected, (0, heads, 2 * heads), self_gains, key_count)
+    attention_combined, self_inverse = attention(*self_inputs, tables, rows=2 * own_len)
+    up_full = gather_rows(up_own, up_later).reshape(size * ff_half, width)
+    down_full = gather_rows(down_own, down_later).reshape(size * ff_half, width)
     branch_one = halve(dot_nn(attention_combined, self_full[3])) + out_bias.astype(f32)
     stream_two = stream + branch_one
     cross_in = both(affine_norm(stream_two, norm2_gain_f, norm2_beta_f).astype(low))
     query_raw = dot_tt(cross_in, cross_full[0])
-    keys_raw = dot_tt(text_own, cross_full[1])
-    values_raw = dot_tt(text_own, cross_full[2])
-    cross_query = head_norm(query_raw, cross_gain_f[0]).astype(low)[None]
-    cross_keys = head_norm(keys_raw, cross_gain_f[1]).astype(low)[None]
-    cross_values = values_raw.reshape(1, text_size, heads, HD).astype(low)
-    cross_result, cross_logsum = attend_forward(cross_query, cross_keys, cross_values, key_bias)
-    crossed_combined = cross_result[0].astype(low)
+    text_raw = dot_tt(text_own, cross_full[1:3].reshape(2 * lanes, width))
+    cross_inputs = (heads, query_raw, text_raw, text_raw, (0, 0, heads), cross_gains, key_count)
+    crossed_combined, cross_inverse = attention(*cross_inputs, rows=2 * own_len)
     branch_two = halve(dot_nn(crossed_combined, cross_full[3])) + cross_out_bias.astype(f32)
     stream_three = stream_two + branch_two
     mlp_in = both(affine_norm(stream_three, norm3_gain_f, norm3_beta_f).astype(low))
@@ -761,83 +1066,82 @@
             for term in (stream, branch_one, branch_two, branch_three, output)
         ]
     )
-    output_home = collect(output.astype(low).reshape(size, piece_len, width)).reshape(latent_in.shape)
+    stat_rows = stats.reshape(5, size, piece_len).transpose(1, 0, 2).reshape(size, 1, 5 * piece_len)
+    stat_rows = jnp.pad(stat_rows.astype(low), ((0, 0), (0, 7), (0, width - 5 * piece_len)))
+    home = collect(jnp.concatenate([output.astype(low).reshape(size, piece_len, width), stat_rows], 1))
+    output_home = home[:, :piece_len].reshape(latent_in.shape)
     stats_home = (
-        collect(stats.reshape(5, size, piece_len).transpose(1, 0, 2))
+        home[:, piece_len, : 5 * piece_len]
         .reshape(sequences, 2, 5, piece_len)
         .transpose(0, 2, 1, 3)
         .reshape(sequences, 5, local_len)
+        .astype(f32)
     )
 
     grad_out = grad_low.astype(f32)
     down_bias_part = jnp.sum(grad_out, axis=0)
     grad_all = both(grad_low)
     down_grad = dot_tn(hidden_state, grad_all).astype(low)
+    grad_all, down_grad = tie(grad_all, down_grad)
+    down_parts = scatter_rows(down_grad.reshape(chips, size, ff_part, width))
     hidden_grad = dot_tt(grad_all, down_full)
     pre_grad = gelu_back(hidden_grad)[0]
     up_bias_part = jnp.sum(pre_grad, axis=0)
     pre_low = pre_grad.astype(low)
+    up_grad = dot_tn(pre_low, mlp_in).astype(low)
+    pre_low, up_grad = tie(pre_low, up_grad)
+    up_parts = scatter_rows(up_grad.reshape(chips, size, ff_part, width))
     norm3_grad_in = halve(dot_nn(pre_low, up_full))
-    up_grad = dot_tn(pre_low, mlp_in).astype(low)
     _, norm3_back = jax.vjp(affine_norm, stream_three, norm3_gain_f, norm3_beta_f)
     from_three, gain3_part, beta3_part = norm3_back(norm3_grad_in)
     grad_three = grad_out + from_three
     cross_bias_part = jnp.sum(grad_three, axis=0)
     three_all = both(grad_three.astype(low))
-    cross_out_grad = dot_tn(crossed_combined, three_all).astype(low)
-    cross_mixed_grad = dot_tt(three_all, cross_full[3]).astype(low)[None]
-    cq_grad, ck_grad, cv_grad = attend_backward(
-        cross_query, cross_keys, cross_values, key_bias, cross_logsum, cross_mixed_grad, cross_result
-    )
-    _, cq_back = jax.vjp(head_norm, query_raw, cross_gain_f[0])
-    query_raw_grad, cq_gain_part = cq_back(cq_grad[0])
-    _, ck_back = jax.vjp(head_norm, keys_raw, cross_gain_f[1])
-    keys_raw_grad, ck_gain_part = ck_back(ck_grad[0])
-    cross_gain_part = jnp.concatenate([cq_gain_part, ck_gain_part])
-    query_low = query_raw_grad.astype(low)
-    keys_low = keys_raw_grad.astype(low)
-    values_low = cv_grad.reshape(text_size, size * half).astype(low)
+    cross_out_grad = dot_tn(crossed_combined, three_all)
+    cross_mixed_grad = dot_tt(three_all, cross_full[3]).astype(low)
+    query_low, keys_low, values_low, cross_gain_sums = attention_back(
+        *cross_inputs, cross_mixed_grad, crossed_combined, cross_inverse, rows=2 * own_len
+    )
     norm2_grad_in = halve(dot_nn(query_low, cross_full[0]))
     cross_grads = jnp.stack(
         [
-            dot_tn(query_low, cross_in).astype(low),
-            dot_tn(keys_low, text_own).astype(low),
-            dot_tn(values_low, text_own).astype(low),
-            cross_out_grad,
-        ]
-    )
+            trim_heads(grad.astype(low))
+            for grad in (
+                dot_tn(query_low, cross_in),
+                dot_tn(keys_low, text_own),
+                dot_tn(values_low, text_own),
+                cross_out_grad,
+            )
+        ],
+    )
+    cross_parts = scatter_rows(cross_grads)
     text_part = dot_nn(keys_low, cross_full[1]) + dot_nn(values_low, cross_full[2])
     _, norm2_back = jax.vjp(affine_norm, stream_two, norm2_gain_f, norm2_beta_f)
     from_two, gain2_part, beta2_part = norm2_back(norm2_grad_in)
     grad_two = grad_three + from_two
     out_bias_part = jnp.sum(grad_two, axis=0)
     two_all = both(grad_two.astype(low))
-    out_weight_part = dot_tn(attention_combined, two_all).astype(low)
-    attn_mixed_grad = dot_tt(two_all, self_full[3]).astype(low)[None]
-    sq_grad, sk_grad, sv_grad = attend_backward(
-        query_self, keys_self, values_self, self_bias, attn_logsum, attn_mixed_grad, attn_result
-    )
-    _, sq_back = jax.vjp(qk_prep, projected[0], qk_gain_f[0])
-    q_raw_grad, sq_gain_part = sq_back(sq_grad[0])
-    _, sk_back = jax.vjp(qk_prep, projected[1], qk_gain_f[1])
-    k_raw_grad, sk_gain_part = sk_back(sk_grad[0])
-    self_gain_part = jnp.concatenate([sq_gain_part, sk_gain_part])
-    proj_grads = [
-        q_raw_grad.astype(low),
-        k_raw_grad.astype(low),
-        sv_grad.reshape(2 * own_len, size * half).astype(low),
-    ]
+    out_weight_part = dot_tn(attention_combined, two_all)
+    attn_mixed_grad = dot_tt(two_all, self_full[3]).astype(low)
+    *proj_grads, self_gain_sums = attention_back(
+        *self_inputs, attn_mixed_grad, attention_combined, self_inverse, tables, rows=2 * own_len
+    )
     first_grad_in = halve(
         dot_nn(proj_grads[0], self_full[0])
         + dot_nn(proj_grads[1], self_full[1])
         + dot_nn(proj_grads[2], self_full[2])
     )
     self_grads = jnp.stack(
-        [dot_tn(grad, attn_in).astype(low) for grad in proj_grads] + [out_weight_part]
+        [trim_heads(dot_tn(grad, attn_in).astype(low)) for grad in proj_grads]
+        + [trim_heads(out_weight_part.astype(low))],
     )
     _, first_back = jax.vjp(first_norm, stream, shift_vec)
     from_one, shift_own_grad = first_back(first_grad_in)
     grad_one = (grad_two + from_one).astype(low)
+    down_sum = share_rows(add_line(down_parts[0], send_line(down_parts)))
+    up_sum = share_rows(add_line(up_parts[0], send_line(up_parts)))
+    grad_one, self_grads = tie(grad_one, self_grads)
+    self_parts = scatter_rows(self_grads)
 
     home_grad = collect(grad_one.reshape(size, piece_len, width)).reshape(own_len, width)
     skip_bias_part = jnp.sum(home_grad.astype(f32), axis=0)
@@ -865,19 +1169,12 @@
     skip_grad = (inverse * (skip_h - mean_h - skip_ln * mean_hl)).reshape(latent_in.shape)
 
     shift_own = shift_own_grad + swap_cores(shift_own_grad)
-    shift_all = lax.all_gather(shift_own, ("chip", "tensor"), axis=0, tiled=False)
-    condition_all = jax.nn.silu(
-        lax.all_gather(time_emb, ("chip", "core"), axis=0, tiled=True).astype(f32)
-    )
-    shift_cols = lax.dynamic_slice_in_dim(shift_all, rank * shard, shard, 1)
-    ada_bias_grad = jnp.sum(shift_cols, axis=0)
-    ada_weight_grad = jnp.dot(condition_all.T, shift_cols, precision=PRECISE)
-    shift_mine = lax.dynamic_slice_in_dim(
-        shift_cols, (chip * 2 + core) * sequences, sequences, 0
-    )
-    condition_grad = lax.psum(jnp.dot(shift_mine, ada_weight_f.T, precision=PRECISE), "tensor")
-    _, silu_back = jax.vjp(jax.nn.silu, time_emb.astype(f32))
-    time_grad = silu_back(condition_grad)[0]
+    shift_line = rolled(
+        jnp.stack([shift_own] + [from_later(shift_own, step, size) for step in range(1, size)]),
+        (size - rank) % size,
+    )
+    line_cols = lax.dynamic_slice_in_dim(shift_line, rank * shard, shard, 1)
+    condition_part = jnp.dot(line_cols, ada_weight_f.T, precision=PRECISE)
 
     text_half = text_size // 2
     text_rows = lax.dynamic_slice_in_dim(text_part, core * text_half, text_half, 0)
@@ -903,41 +1200,65 @@
     up_bias_vec = jnp.stack(
         [jnp.where(core == 0, up_bias_abs, 0.0), jnp.where(core == 1, up_bias_abs, 0.0)], 1
     ).reshape(2 * size * ff_half)
-    vectors = [
-        skip_gain_part,
-        skip_beta_part,
-        skip_bias_part,
-        self_gain_part,
-        out_bias_part,
-        gain2_part,
-        beta2_part,
-        cross_gain_part,
-        cross_bias_part,
-        gain3_part,
-        beta3_part,
-        up_bias_vec,
-        down_bias_part,
-    ]
-    lengths = [vector.shape[0] for vector in vectors]
-    summed = lax.psum(jnp.concatenate(vectors), ("chip", "core", "tensor"))
-    sums = []
-    at = 0
-    for length in lengths:
-        sums.append(summed[at : at + length])
-        at += length
+    gain_rows = jnp.concatenate(
+        [jnp.sum(sums[:, :2], 0)[:, :HD].reshape(2 * HD) for sums in (self_gain_sums, cross_gain_sums)]
+    )
+    last_row = 2 * size * ff_half % width
+    vector_rows = jnp.concatenate(
+        [
+            skip_gain_part,
+            skip_beta_part,
+            skip_bias_part,
+            out_bias_part,
+            gain2_part,
+            beta2_part,
+            cross_bias_part,
+            gain3_part,
+            beta3_part,
+            down_bias_part,
+            up_bias_vec,
+            gain_rows,
+            jnp.zeros((width - last_row - gain_rows.shape[0],), f32),
+        ]
+    ).reshape(-1, width)
+    first_core = core == 0
+    line_rows = jnp.stack(
+        [
+            jnp.where(first_core, condition_part, 0.0),
+            jnp.where(first_core & (rank == 0), shift_line, 0.0),
+        ]
+    )
+    chip_rows = jnp.where(
+        (jnp.arange(chips) == chip)[None, :, None, None], line_rows[:, None], 0.0
+    ).reshape(2 * chips * size, width)
+    time_rows = jnp.where(
+        (jnp.arange(2 * chips) == 2 * chip + core)[:, None, None] & (rank == 0),
+        time_emb.astype(f32)[None],
+        0.0,
+    ).reshape(2 * chips * sequences, width)
+    vectors = jnp.concatenate([chip_rows, time_rows, vector_rows], 0)
+    vector_part = 32 * -(-vectors.shape[0] // (32 * chips))
+    vectors = jnp.pad(vectors, ((0, chips * vector_part - vectors.shape[0]), (0, 0)))
+    vectors = vectors.astype(low).reshape(chips, vector_part, width)
 
     def own_cols(vector, count):
         return lax.dynamic_slice_in_dim(vector, rank * count, count, 0)
 
-    down0, down1 = reduce_rows(down_grad.reshape(chips, size, ff_part, width))
-    down_weight_grad = jnp.concatenate(
-        [down0.reshape(ff_half, width), down1.reshape(ff_half, width)], 0
-    ).astype(f32)
-    up0, up1 = reduce_rows(up_grad.reshape(chips, size, ff_part, width))
-    up_weight_grad = jnp.concatenate(
-        [up0.reshape(ff_half, width).T, up1.reshape(ff_half, width).T], 1
-    ).astype(f32)
-    cross0, cross1 = reduce_rows(cross_grads.reshape(4, size, half, width))
+    skip_rel_grad = rolled(skip_sum.reshape(size, chips, skip_part, width), rank).transpose(1, 0, 2, 3)
+    skip_rows = size * skip_part
+    skip_rows_all = jnp.concatenate([skip_rel_grad.reshape(chips, skip_rows, width), vectors], 1)
+    skip_rows_all, self_parts, down_sum, up_sum = tie(skip_rows_all, self_parts, down_sum, up_sum)
+    parts = lax.psum_scatter(
+        skip_rows_all.reshape(-1, width), "chip", scatter_dimension=0, tiled=True
+    )
+    cross_sum, self_sum = (
+        share_rows(add_line(parts[0], send_line(parts))) for parts in (cross_parts, self_parts)
+    )
+    down0, down1 = by_core(down_sum)
+    down_weight_grad = jnp.concatenate([down0, down1], 0).astype(f32)
+    up0, up1 = by_core(up_sum)
+    up_weight_grad = jnp.concatenate([up0.T, up1.T], 1).astype(f32)
+    cross0, cross1 = (part.reshape(4, half, width) for part in by_core(cross_sum))
 
     def cols_of(first, second):
         return jnp.concatenate([first.T, second.T], 1).astype(f32)
@@ -948,14 +1269,45 @@
     cross_query_weight_grad = cols_of(cross0[0], cross1[0])
     cross_kv_weight_grad = jnp.stack([cols_of(cross0[i], cross1[i]) for i in (1, 2)])
     cross_out_weight_grad = rows_of(cross0[3], cross1[3])
-    self0, self1 = reduce_rows(self_grads.reshape(4, size, half, width))
+    self0, self1 = (part.reshape(4, half, width) for part in by_core(self_sum))
     qkv_weight_grad = jnp.stack([cols_of(self0[i], self1[i]) for i in range(3)])
     out_weight_grad = rows_of(self0[3], self1[3])
-    skip_rel_grad = rolled(skip_sum.reshape(size, chips, skip_part, width), rank).transpose(1, 0, 2, 3)
-    skip0, skip1 = reduce_rows(skip_rel_grad)
+    vector_mine = parts[skip_rows:]
+    skip_total = parts[:skip_part].astype(f32)
+    vector_line = [vector_mine]
+    for step in range(1, size):
+        arrived = from_earlier(
+            jnp.concatenate([parts[step * skip_part : (step + 1) * skip_part], vector_mine], 0), step, size
+        )
+        skip_total = skip_total + arrived[:skip_part].astype(f32)
+        vector_line.append(arrived[skip_part:])
+    vector_line = jnp.stack(vector_line)
+    vector_total = pick(vector_line, rank).astype(f32)
+    for source in range(1, size):
+        vector_total = vector_total + pick(vector_line, (rank - source) % size).astype(f32)
+    total = lax.all_gather(
+        jnp.concatenate([skip_total, vector_total], 0).astype(low), "chip", axis=0, tiled=True
+    ).reshape(chips, skip_part + vector_part, width)
+    total_other = swap_cores(total)
+    skip0 = jnp.where(core == 0, total[:, :skip_part], total_other[:, :skip_part])
+    skip1 = jnp.where(core == 0, total_other[:, :skip_part], total[:, :skip_part])
     skip_weight_grad = jnp.concatenate(
         [skip0.reshape(shard, width).T, skip1.reshape(shard, width).T], 0
     ).astype(f32)
+    summed = (total[:, skip_part:].astype(f32) + total_other[:, skip_part:].astype(f32)).reshape(-1, width)
+    seqs = chips * size
+    own_seq = (chip * 2 + core) * sequences
+    time_back = lax.dynamic_slice_in_dim(summed[:seqs], own_seq, sequences, 0)
+    _, silu_back = jax.vjp(jax.nn.silu, time_emb.astype(f32))
+    time_grad = silu_back(time_back)[0]
+    shift_cols = lax.dynamic_slice_in_dim(summed[seqs : 2 * seqs], rank * shard, shard, 1)
+    condition_all = jax.nn.silu(summed[2 * seqs : 3 * seqs])
+    ada_bias_grad = jnp.sum(shift_cols, axis=0)
+    ada_weight_grad = jnp.dot(condition_all.T, shift_cols, precision=PRECISE)
+    flat = summed[3 * seqs :].reshape(-1)
+    rows_at = [flat[width * i : width * (i + 1)] for i in range(12)]
+    up_bias_sum = flat[12 * width : 12 * width + 2 * size * ff_half]
+    gain_sums = flat[12 * width + 2 * size * ff_half :][: 4 * HD].reshape(2, 2, HD)
     return (
         output_home,
         stats_home,
@@ -963,29 +1315,29 @@
         skip_grad,
         text_grad,
         time_grad,
-        sums[0],
-        sums[1],
+        flat[: 2 * width],
+        flat[2 * width : 4 * width],
         skip_weight_grad,
-        own_cols(sums[2], shard),
+        own_cols(rows_at[4], shard),
         ada_weight_grad,
         ada_bias_grad,
         qkv_weight_grad,
-        sums[3].reshape(2, HD),
+        gain_sums[0],
         out_weight_grad,
-        sums[4],
-        sums[5],
-        sums[6],
+        rows_at[5],
+        rows_at[6],
+        rows_at[7],
         cross_query_weight_grad,
         cross_kv_weight_grad,
-        sums[7].reshape(2, HD),
+        gain_sums[1],
         cross_out_weight_grad,
-        sums[8],
-        sums[9],
-        sums[10],
+        rows_at[8],
+        rows_at[9],
+        rows_at[10],
         up_weight_grad,
-        own_cols(sums[11], 2 * ff_half),
+        own_cols(up_bias_sum, 2 * ff_half),
         down_weight_grad,
-        sums[12],
+        rows_at[11],
     )
 
 

time: 1500 us -> 1270 us (0.85)
  local copies, waits for them, and re-layouts: 301 us -> 146 us
  waiting for transfers between devices: 288 us -> 434 us
  starting transfers between devices: 275 us -> 176 us
  Pallas kernels: 0 us -> 94.9 us
  matrix products: 325 us -> 234 us
  blocking collectives: 81 us -> 0 us
  other arithmetic: 186 us -> 155 us
    ppermute x21 -> x15, waiting for transfers between devices: 68.3 us -> 194 us  [from_later(): return lax.ppermute(values, 'tensor', ring_pairs(size, -step))]
    dynamic_update_slice x8 -> x0, local copies, waits for them, and re-layouts: 121 us -> none  [attend_forward(): results, logsum = lax.map(one_block, query_blocks)]
    dot_general x29 -> x1, matrix products: 108 us -> 0.55 us  [chip_local(): condition_part = jnp.dot(line_cols, ada_weight_f.T, precision=PRECISE)]
    pallas_call x0 -> x4, Pallas kernels: none -> 94.9 us  [the longest x2 64.1 us: attention_back(): pl.pallas_call(functools.partial(attention_back_kernel, turned, min(rows,...]
    all_gather x3 -> x0, blocking collectives: 65 us -> none  [the longest x1 39.1 us: chip_local(): lax.all_gather(shift_own, ('chip', 'tensor'), axis=0, tiled=False)]
    ppermute x21 -> x15, starting transfers between devices: 91.3 us -> 26.9 us  [from_later(): return lax.ppermute(values, 'tensor', ring_pairs(size, -step))]
    ppermute x24 -> x23, starting transfers between devices: 57.7 us -> 21.1 us  [swap_cores(): return lax.ppermute(values, 'core', [(0, 1), (1, 0)])]
    while x69 -> x0, local copies, waits for them, and re-layouts: 29.1 us -> none
  transfers between devices with their start and end apart: 99 -> 88, of which waited for: 30 -> 37; matrix products, arithmetic and copies ran while one was open for 47% -> 32% of each run, Pallas kernels for 0% -> 8%
where the time goes in v2:
time: 1270 us; the launch traced here: 1260 us
  waiting for transfers between devices  434 us (34%)
  matrix products  234 us (18%)
  starting transfers between devices  176 us (14%)
  other arithmetic  155 us (12%)
  local copies, waits for them, and re-layouts  146 us (11%)
  Pallas kernels  94.9 us (7%)
  between operations  17.8 us (1%)
    ppermute x15, waiting for transfers between devices, from_later(): return lax.ppermute(values, 'tensor', ring_pairs(size, -step))  194 us
    ppermute x15, waiting for transfers between devices, from_earlier(): return lax.ppermute(values, 'tensor', ring_pairs(size, step))  127 us
    dot_general x12, matrix products, dot_nn(): lax.dot_general(left, right, (((1,), (0,)), ((), ())), preferred_element_...  81 us
    dot_general x12, matrix products, dot_tn(): lax.dot_general(left, right, (((0,), (0,)), ((), ())), preferred_element_...  74.8 us
    dot_general x9, matrix products, dot_tt(): lax.dot_general(left, right, (((1,), (1,)), ((), ())), preferred_element_...  73.6 us
    unnamed x411, local copies, waits for them, and re-layouts  65.3 us
    pallas_call x2, Pallas kernels, attention_back(): pl.pallas_call(functools.partial(attention_back_kernel, turned, min(rows,...  64.1 us
    ppermute x8, starting transfers between devices, collect(): lax.ppermute(values[turn], ('core', 'tensor'), [(target, source) for sour...  51.5 us
  transfers between devices with their start and end apart: 88, of which 37 were waited for; matrix products, arithmetic and copies ran while one was open for 32% of the time, Pallas kernels for 8%

profile of v2, /device:TPU:0, one launch (start us, length us, event | category | flops | bytes accessed | tf_op | source)
XLA Modules:
  0.0 1257.9 jit_solution(1298387535652613282)
XLA Ops:
  15.6 5.4 collective-permute-done
  21.8 13.9 %collective-permute-done.1 = bf16[88,1408]{1,0:T(8,128)(2,1)S(1)} collective-permute-done((bf16[88,1408]{1,0:T(8,128)(2,1)S(1)}, bf16[88,1408]{1,0:T(8,128)(2,1)S(1)}, u32[]{:S(2)}, u32[]{:S(2)}) %collective-permute-start.1) | collective-permute-done | bytes 247840 | tf_op jit(solution)/shard_map/ppermute | solution.py:723
  53.2 9.1 collective-permute-done.4
  62.3 33.3 %collective-permute-done.5 = bf16[184,1408]{1,0:T(8,128)(2,1)S(1)} collective-permute-done((bf16[184,1408]{1,0:T(8,128)(2,1)S(1)}, bf16[184,1408]{1,0:T(8,128)(2,1)S(1)}, u32[]{:S(2)}, u32[]{:S(2)}) %collective-permute-start.5) | collective-permute-done | bytes 518176 | tf_op jit(solution)/shard_map/ppermute | solution.py:723
  102.8 9.8 collective-permute-done.15
  112.6 31.5 %collective-permute-done.16 = bf16[176,1408]{1,0:T(8,128)(2,1)S(1)} collective-permute-done((bf16[176,1408]{1,0:T(8,128)(2,1)S(1)}, bf16[176,1408]{1,0:T(8,128)(2,1)S(1)}, u32[]{:S(2)}, u32[]{:S(2)}) %collective-permute-start.16) | collective-permute-done | bytes 495648 | tf_op jit(solution)/shard_map/ppermute | solution.py:723
  162.5 21.6 %collective-permute-done.21 = bf16[384,1408]{1,0:T(8,128)(2,1)S(1)} collective-permute-done((bf16[384,1408]{1,0:T(8,128)(2,1)}, bf16[384,1408]{1,0:T(8,128)(2,1)S(1)}, u32[]{:S(2)}, u32[]{:S(2)}) %collective-permute-start.21) | collective-permute-done | bytes 1081376 | tf_op jit(solution)/shard_map/ppermute | solution.py:723
  184.1 69.2 %collective-permute-done.22 = bf16[384,1408]{1,0:T(8,128)(2,1)} collective-permute-done((bf16[384,1408]{1,0:T(8,128)(2,1)}, bf16[384,1408]{1,0:T(8,128)(2,1)}, u32[]{:S(2)}, u32[]{:S(2)}) %collective-permute-start.22) | collective-permute-done | bytes 1081376 | tf_op jit(solution)/shard_map/ppermute | solution.py:723
  267.9 5.5 fusion.53
  287.7 5.3 fusion.139
  309.6 8.9 collective-permute-done.8
  318.5 13.0 %collective-permute-done.9 = bf16[128,1408]{1,0:T(8,128)(2,1)S(1)} collective-permute-done((bf16[128,1408]{1,0:T(8,128)(2,1)}, bf16[128,1408]{1,0:T(8,128)(2,1)S(1)}, u32[]{:S(2)}, u32[]{:S(2)}) %collective-permute-start.9) | collective-permute-done | bytes 360480 | tf_op jit(solution)/shard_map/ppermute | solution.py:816
  338.4 8.4 fusion.19
  346.8 7.6 fusion.157
  357.7 14.4 %fusion.135.refs_0_.refs_1_.refs_2_ = f32[1024,3072]{1,0:T(8,128)} fusion(bf16[3072,1408]{1,0:T(8,128)(2,1)S(1)} %bitcast.482, bf16[512,1408]{1,0:T(8,128)(2,1)} %collective-permute-done.12, bf16[512,1408]{1,0:T(8,128)(2,1)} %fusion.45), kind=kOutput, calls=%fused_computation.470 | convolution fusion | flops 8864137216 | bytes 24117248 | tf_op jit(solution)/shard_map/dot_general | solution.py:752
  372.7 20.3 %attention_turned.1 = (bf16[1024,1024]{1,0:T(8,128)(2,1)S(1)}, f32[1024,1024]{1,0:T(8,128)S(1)}) custom-call(f32[1024,3072]{1,0:T(8,128)} %fusion.135.refs_0_.refs_1_.refs_2_, f32[1024,3072]{1,0:T(8,128)} %fusion.135.refs_0_.refs_1_.refs_2_, f32[1024,3072]{1,0:T(8,128)} %fusion.135.refs_0_.refs_1_.refs_2_, f32[8,128]{1,0:T(8,128)S(1)} %select_maximum_fusion.2.refs_3_, ...), custom_call_target="tpu_custom_call" | custom-call | flops 4294967296 | bytes 18874368 | tf_op jit(solution)/shard_map/attention_turned/pallas_call | solution.py:656
  399.7 6.0 fusion.27
  420.0 7.5 fusion.156
  432.6 10.5 attention_plain.1
  457.3 9.1 collective-permute-done.30
  466.4 13.8 %collective-permute-done.31 = bf16[128,1408]{1,0:T(8,128)(2,1)S(1)} collective-permute-done((bf16[128,1408]{1,0:T(8,128)(2,1)S(1)}, bf16[128,1408]{1,0:T(8,128)(2,1)S(1)}, u32[]{:S(2)}, u32[]{:S(2)}) %collective-permute-start.31) | collective-permute-done | bytes 360480 | tf_op jit(solution)/shard_map/ppermute | solution.py:816
  488.1 7.8 pad_maximum_fusion
  495.8 7.8 pad_maximum_fusion.1
  506.7 13.3 %fusion.59 = f32[1024,3072]{1,0:T(8,128)S(1)} fusion(bf16[3072,1408]{1,0:T(8,128)(2,1)} %bitcast.527, bf16[512,1408]{1,0:T(8,128)(2,1)} %collective-permute-done.20, bf16[512,1408]{1,0:T(8,128)(2,1)} %add_convert_fusion.1), kind=kOutput, calls=%fused_computation.173 | convolution fusion | flops 8864137216 | bytes 24117248 | tf_op jit(solution)/shard_map/dot_general | solution.py:752
  524.7 14.6 %convolution_convert_fusion.1 = bf16[3072,1408]{1,0:T(8,128)(2,1)} fusion(bf16[512,1408]{1,0:T(8,128)(2,1)} %collective-permute-done.33, bf16[512,1408]{1,0:T(8,128)(2,1)S(1)} %bitcast.488, f32[1024,3072]{1,0:T(8,128)S(1)} %fusion.59, f32[3072]{0:T(1024)S(1)} %add.823), kind=kOutput, calls=%fused_computation.37 | convolution fusion | flops 8899919872 | bytes 24129536 | tf_op jit(solution)/shard_map/dot_general | solution.py:760
  539.2 22.8 %fusion.146 = (bf16[3072]{0:T(1024)(128)(2,1)}, bf16[1024,3072]{1,0:T(8,128)(2,1)S(1)}) fusion(f32[1024,3072]{1,0:T(8,128)} %copy-done.184, f32[3072]{0:T(1024)S(1)} %add.823, bf16[1024,1408]{1,0:T(8,128)(2,1)} %pad_maximum_fusion.9, bf16[3072,1408]{1,0:T(8,128)(2,1)} %bitcast.529), kind=kOutput, calls=%fused_computation.477 | convolution fusion | flops 8927572992 | bytes 30427136 | tf_op jit(solution)/shard_map/dot_general | solution.py:752
  564.7 13.9 %convolution_convert_fusion = bf16[3072,1408]{1,0:T(8,128)(2,1)} fusion(bf16[1024,3072]{1,0:T(8,128)(2,1)S(1)} %get-tuple-element.58, bf16[512,1408]{1,0:T(8,128)(2,1)} %collective-permute-done.20, bf16[512,1408]{1,0:T(8,128)(2,1)} %add_convert_fusion.1), kind=kOutput, calls=%fused_computation.36 | convolution fusion | flops 8868462592 | bytes 17825792 | tf_op jit(solution)/shard_map/dot_general | solution.py:760
  579.4 17.4 %fusion.145 = f32[1024,1408]{1,0:T(8,128)S(1)} fusion(bf16[3072,1408]{1,0:T(8,128)(2,1)} %bitcast.530, f32[1024,3072]{1,0:T(8,128)} %copy-done.184, f32[3072]{0:T(1024)S(1)} %add.823), kind=kOutput, calls=%fused_computation.476 | convolution fusion | flops 8889827328 | bytes 27013120 | tf_op jit(solution)/shard_map/dot_general | solution.py:756
  597.7 12.9 %fusion.181 = f32[1024,1408]{1,0:T(8,128)S(1)} fusion(bf16[1024,3072]{1,0:T(8,128)(2,1)} %copy-done.185, bf16[3072,1408]{1,0:T(8,128)(2,1)} %bitcast.528), kind=kOutput, calls=%fused_computation.510 | convolution fusion | flops 8858370048 | bytes 20709376 | tf_op jit(solution)/shard_map/dot_general | solution.py:756
  627.4 19.6 %attention_plain_back.1 = (bf16[1024,1024]{1,0:T(8,128)(2,1)S(1)}, bf16[256,1024]{1,0:T(8,128)(2,1)S(1)}, bf16[256,1024]{1,0:T(8,128)(2,1)S(1)}, f32[8,8,128]{2,1,0:T(8,128)S(1)}) custom-call(f32[1024,1024]{1,0:T(8,128)S(1)} %copy-done.5, f32[256,2048]{1,0:T(8,128)S(1)} %copy-done.3, f32[256,2048]{1,0:T(8,128)S(1)} %copy-done.3, f32[8,128]{1,0:T(8,128)S(1)} %copy-done.15, ...), custom_call_target="tpu_custom_call" | custom-call | flops 2684354560 | bytes 31457280 | tf_op jit(solution)/shard_map/attention_plain_back/pallas_call | solution.py:685
  662.3 5.9 fusion.182
  684.6 44.4 %attention_turned_back.1 = (bf16[1024,1024]{1,0:T(8,128)(2,1)S(1)}, bf16[1024,1024]{1,0:T(8,128)(2,1)S(1)}, bf16[1024,1024]{1,0:T(8,128)(2,1)S(1)}, f32[8,8,128]{2,1,0:T(8,128)S(1)}) custom-call(f32[1024,3072]{1,0:T(8,128)} %fusion.135.refs_0_.refs_1_.refs_2_, f32[1024,3072]{1,0:T(8,128)} %fusion.135.refs_0_.refs_1_.refs_2_, ...), custom_call_target="tpu_custom_call" | custom-call | flops 10737418240 | bytes 31457280 | tf_op jit(solution)/shard_map/attention_turned_back/pallas_call | solution.py:685
  743.9 7.1 fusion.183
  750.9 6.2 collective-permute-done.56
  757.1 22.2 %collective-permute-done.57 = bf16[192,1408]{1,0:T(8,128)(2,1)S(1)} collective-permute-done((bf16[192,1408]{1,0:T(8,128)(2,1)S(1)}, bf16[192,1408]{1,0:T(8,128)(2,1)S(1)}, u32[]{:S(2)}, u32[]{:S(2)}) %collective-permute-start.57) | collective-permute-done | bytes 540704 | tf_op jit(solution)/shard_map/ppermute | solution.py:727
  781.5 9.7 add_add_fusion
  794.5 7.5 convolution_convert_fusion.10
  802.0 6.6 convolution_convert_fusion.9
  810.4 11.2 collective-permute-start.53
  824.1 6.6 convolution_convert_fusion.8
  835.2 22.1 %collective-permute-done.54 = bf16[192,1408]{1,0:T(8,128)(2,1)S(1)} collective-permute-done((bf16[192,1408]{1,0:T(8,128)(2,1)S(1)}, bf16[192,1408]{1,0:T(8,128)(2,1)S(1)}, u32[]{:S(2)}, u32[]{:S(2)}) %collective-permute-start.54) | collective-permute-done | bytes 540704 | tf_op jit(solution)/shard_map/ppermute | solution.py:727
  859.5 6.1 convolution_convert_fusion.7
  885.5 16.6 %collective-permute-start.26 = (bf16[136,1408]{1,0:T(8,128)(2,1)}, bf16[136,1408]{1,0:T(8,128)(2,1)S(1)}, u32[]{:S(2)}, u32[]{:S(2)}) collective-permute-start(bf16[136,1408]{1,0:T(8,128)(2,1)} %get-tuple-element.308), channel_id=1, source_target_pairs={{4,0},{1,1},{5,2},{0,3},{6,4},{3,5},{7,6},{2,7},{12,8},{9,9},{13,1... | collective-permute-start | bytes 1148936 | tf_op jit(solution)/shard_map/ppermute | solution.py:825
  907.9 10.4 collective-permute-start.50
  919.9 6.0 collective-permute-start.40
  932.7 7.7 collective-permute-done.41
  940.5 6.1 collective-permute-done.42
  965.1 10.1 collective-permute-done.67
  975.8 20.7 %collective-permute-done.68 = bf16[176,1408]{1,0:T(8,128)(2,1)S(1)} collective-permute-done((bf16[176,1408]{1,0:T(8,128)(2,1)}, bf16[176,1408]{1,0:T(8,128)(2,1)S(1)}, u32[]{:S(2)}, u32[]{:S(2)}) %collective-permute-start.68) | collective-permute-done | bytes 495648 | tf_op jit(solution)/shard_map/ppermute | solution.py:727
  996.5 22.2 %collective-permute-start.28 = (bf16[136,1408]{1,0:T(8,128)(2,1)}, bf16[136,1408]{1,0:T(8,128)(2,1)}, u32[]{:S(2)}, u32[]{:S(2)}) collective-permute-start(bf16[136,1408]{1,0:T(8,128)(2,1)} %get-tuple-element.306), channel_id=1, source_target_pairs={{5,0},{0,1},{4,2},{1,3},{7,4},{2,5},{6,6},{3,7},{13,8},{8,9},{12,1... | collective-permute-start | bytes 1148936 | tf_op jit(solution)/shard_map/ppermute | solution.py:825
  1021.4 5.3 fusion.185
  1026.8 8.7 multiply_reduce_fusion.3
  1035.9 5.6 fusion.31
  1056.9 6.7 collective-permute-start.45
  1075.1 5.7 collective-permute-done.45
  1089.9 8.0 collective-permute-start.70
  1109.5 6.0 collective-permute-done.63
  1115.5 20.4 %collective-permute-done.64 = bf16[176,1408]{1,0:T(8,128)(2,1)S(1)} collective-permute-done((bf16[176,1408]{1,0:T(8,128)(2,1)S(1)}, bf16[176,1408]{1,0:T(8,128)(2,1)S(1)}, u32[]{:S(2)}, u32[]{:S(2)}) %collective-permute-start.64) | collective-permute-done | bytes 495648 | tf_op jit(solution)/shard_map/ppermute | solution.py:727
  1154.7 10.3 collective-permute-start.60
  1169.7 9.2 copy.104
  1187.2 8.4 collective-permute-done.59
  1195.7 6.5 collective-permute-done.61
  1203.2 6.4 maximum_convert_fusion.1
  1212.5 18.5 %all-gather.20.cloned.1.call-done = bf16[480,1408]{1,0:T(8,128)(2,1)} async-done(((bf16[120,1408]{1,0:T(8,128)(2,1)}), bf16[480,1408]{1,0:T(8,128)(2,1)}) %all-gather.20.cloned.1.call-update) | async-done | bytes 1351696 | tf_op jit(solution)/shard_map/all_gather | solution.py:1288
  (852 shorter events, 404.2 us)
Async XLA Ops:
  7.2 266.2 %all-gather.26.cloned.1.call-start = ((), (), s32[]{:S(2)}) async-start(), calls=%async_computation.15 | async-start | bytes 4956160 | tf_op jit(solution)/shard_map/all_gather | solution.py:854
  14.6 21.1 %collective-permute-start.1 = (bf16[88,1408]{1,0:T(8,128)(2,1)S(1)}, bf16[88,1408]{1,0:T(8,128)(2,1)S(1)}, u32[]{:S(2)}, u32[]{:S(2)}) collective-permute-start(bf16[88,1408]{1,0:T(8,128)(2,1)S(1)} %get-tuple-element.330), channel_id=1, source_target_pairs={{0,2},{1,3},{2,0},{3,1},{4,6},{5,7},{6,4},{7,5},{8,10},{9,11},{10,... | collective-permute-start | bytes 743432 | tf_op jit(solution)/shard_map/ppermute | solution.py:723
  14.6 21.8 %collective-permute-start.2 = (bf16[88,1408]{1,0:T(8,128)(2,1)S(1)}, bf16[88,1408]{1,0:T(8,128)(2,1)S(1)}, u32[]{:S(2)}, u32[]{:S(2)}) collective-permute-start(bf16[88,1408]{1,0:T(8,128)(2,1)S(1)} %get-tuple-element.330), channel_id=1, source_target_pairs={{0,1},{1,2},{2,3},{3,0},{4,5},{5,6},{6,7},{7,4},{8,9},{9,10},{10,1... | collective-permute-start | bytes 743432 | tf_op jit(solution)/shard_map/ppermute | solution.py:723
  42.2 296.2 %all-gather.28.cloned.1.call-start = ((), (), s32[]{:S(2)}) async-start(), calls=%async_computation.16 | async-start | bytes 7434240 | tf_op jit(solution)/shard_map/all_gather | solution.py:854
  49.1 46.6 %collective-permute-start.5 = (bf16[184,1408]{1,0:T(8,128)(2,1)S(1)}, bf16[184,1408]{1,0:T(8,128)(2,1)S(1)}, u32[]{:S(2)}, u32[]{:S(2)}) collective-permute-start(bf16[184,1408]{1,0:T(8,128)(2,1)S(1)} %pad_maximum_fusion.29), channel_id=1, source_target_pairs={{0,2},{1,3},{2,0},{3,1},{4,6},{5,7},{6,4},{7,5},{8,10},{9,11},{10,... | collective-permute-start | bytes 1554440 | tf_op jit(solution)/shard_map/ppermute | solution.py:723
  51.2 44.4 %collective-permute-start.6 = (bf16[184,1408]{1,0:T(8,128)(2,1)S(1)}, bf16[184,1408]{1,0:T(8,128)(2,1)S(1)}, u32[]{:S(2)}, u32[]{:S(2)}) collective-permute-start(bf16[184,1408]{1,0:T(8,128)(2,1)S(1)} %pad_maximum_fusion.29), channel_id=1, source_target_pairs={{0,1},{1,2},{2,3},{3,0},{4,5},{5,6},{6,7},{7,4},{8,9},{9,10},{10,1... | collective-permute-start | bytes 1554440 | tf_op jit(solution)/shard_map/ppermute | solution.py:723
  97.9 301.8 %all-gather.30.cloned.1.call-start = ((), (), s32[]{:S(2)}) async-start(), calls=%async_computation.17 | async-start | bytes 7434240 | tf_op jit(solution)/shard_map/all_gather | solution.py:854
  100.3 43.8 %collective-permute-start.16 = (bf16[176,1408]{1,0:T(8,128)(2,1)S(1)}, bf16[176,1408]{1,0:T(8,128)(2,1)S(1)}, u32[]{:S(2)}, u32[]{:S(2)}) collective-permute-start(bf16[176,1408]{1,0:T(8,128)(2,1)S(1)} %fusion.80), channel_id=1, source_target_pairs={{0,2},{1,3},{2,0},{3,1},{4,6},{5,7},{6,4},{7,5},{8,10},{9,11},{10,... | collective-permute-start | bytes 1486856 | tf_op jit(solution)/shard_map/ppermute | solution.py:723
  100.8 43.3 %collective-permute-start.17 = (bf16[176,1408]{1,0:T(8,128)(2,1)S(1)}, bf16[176,1408]{1,0:T(8,128)(2,1)S(1)}, u32[]{:S(2)}, u32[]{:S(2)}) collective-permute-start(bf16[176,1408]{1,0:T(8,128)(2,1)S(1)} %fusion.80), channel_id=1, source_target_pairs={{0,1},{1,2},{2,3},{3,0},{4,5},{5,6},{6,7},{7,4},{8,9},{9,10},{10,1... | collective-permute-start | bytes 1486856 | tf_op jit(solution)/shard_map/ppermute | solution.py:723
  145.5 342.6 %all-gather.32.cloned.1.call-start = ((), (), s32[]{:S(2)}) async-start(), calls=%async_computation.18 | async-start | bytes 8110080 | tf_op jit(solution)/shard_map/all_gather | solution.py:854
  158.1 25.9 %collective-permute-start.21 = (bf16[384,1408]{1,0:T(8,128)(2,1)}, bf16[384,1408]{1,0:T(8,128)(2,1)S(1)}, u32[]{:S(2)}, u32[]{:S(2)}) collective-permute-start(bf16[384,1408]{1,0:T(8,128)(2,1)} %pad_maximum_fusion.28), channel_id=1, source_target_pairs={{0,3},{1,0},{2,1},{3,2},{4,7},{5,4},{6,5},{7,6},{8,11},{9,8},{10,9... | collective-permute-start | bytes 3244040 | tf_op jit(solution)/shard_map/ppermute | solution.py:723
  158.1 95.1 %collective-permute-start.22 = (bf16[384,1408]{1,0:T(8,128)(2,1)}, bf16[384,1408]{1,0:T(8,128)(2,1)}, u32[]{:S(2)}, u32[]{:S(2)}) collective-permute-start(bf16[384,1408]{1,0:T(8,128)(2,1)} %pad_maximum_fusion.28), channel_id=1, source_target_pairs={{0,2},{1,3},{2,0},{3,1},{4,6},{5,7},{6,4},{7,5},{8,10},{9,11},{10,... | collective-permute-start | bytes 3244040 | tf_op jit(solution)/shard_map/ppermute | solution.py:723
  159.2 94.0 %collective-permute-start.23 = (bf16[384,1408]{1,0:T(8,128)(2,1)}, bf16[384,1408]{1,0:T(8,128)(2,1)}, u32[]{:S(2)}, u32[]{:S(2)}) collective-permute-start(bf16[384,1408]{1,0:T(8,128)(2,1)} %pad_maximum_fusion.28), channel_id=1, source_target_pairs={{0,1},{1,2},{2,3},{3,0},{4,5},{5,6},{6,7},{7,4},{8,9},{9,10},{10,1... | collective-permute-start | bytes 3244040 | tf_op jit(solution)/shard_map/ppermute | solution.py:723
  162.2 146.1 %collective-permute-start.18 = (bf16[256,1408]{1,0:T(8,128)(2,1)}, bf16[256,1408]{1,0:T(8,128)(2,1)}, u32[]{:S(2)}, u32[]{:S(2)}) collective-permute-start(bf16[256,1408]{1,0:T(8,128)(2,1)} %dynamic-slice_bitcast_fusion), channel_id=1, source_target_pairs={{0,4},{4,0},{1,5},{5,1},{2,6},{6,2},{3,7},{7,3},{8,12},{12,8},{9,1... | collective-permute-start | bytes 2162696 | tf_op jit(solution)/shard_map/ppermute | solution.py:719
  257.2 238.7 %all-gather.34.cloned.1.call-start = ((), (), s32[]{:S(2)}) async-start(), calls=%async_computation.19 | async-start | bytes 8110080 | tf_op jit(solution)/shard_map/all_gather | solution.py:854
  300.7 17.8 %collective-permute-start.8 = (bf16[128,1408]{1,0:T(8,128)(2,1)}, bf16[128,1408]{1,0:T(8,128)(2,1)S(1)}, u32[]{:S(2)}, u32[]{:S(2)}) collective-permute-start(bf16[128,1408]{1,0:T(8,128)(2,1)} %get-tuple-element.325), channel_id=1, source_target_pairs={{0,4},{1,1},{2,5},{3,0},{4,6},{5,3},{6,7},{7,2},{8,12},{9,9},{10,1... | collective-permute-start | bytes 1081352 | tf_op jit(solution)/shard_map/ppermute | solution.py:816
  304.6 26.9 %collective-permute-start.9 = (bf16[128,1408]{1,0:T(8,128)(2,1)}, bf16[128,1408]{1,0:T(8,128)(2,1)S(1)}, u32[]{:S(2)}, u32[]{:S(2)}) collective-permute-start(bf16[128,1408]{1,0:T(8,128)(2,1)} %get-tuple-element.324), channel_id=1, source_target_pairs={{0,1},{1,5},{2,0},{3,4},{4,3},{5,7},{6,2},{7,6},{8,9},{9,13},{10,8... | collective-permute-start | bytes 1081352 | tf_op jit(solution)/shard_map/ppermute | solution.py:816
  304.7 26.8 %collective-permute-start.10 = (bf16[128,1408]{1,0:T(8,128)(2,1)}, bf16[128,1408]{1,0:T(8,128)(2,1)S(1)}, u32[]{:S(2)}, u32[]{:S(2)}) collective-permute-start(bf16[128,1408]{1,0:T(8,128)(2,1)} %get-tuple-element.323), channel_id=1, source_target_pairs={{0,5},{1,0},{2,4},{3,1},{4,7},{5,2},{6,6},{7,3},{8,13},{9,8},{10,1... | collective-permute-start | bytes 1081352 | tf_op jit(solution)/shard_map/ppermute | solution.py:816
  309.3 429.0 %reduce-scatter.10.cloned.1.call-start = ((), (), s32[]{:S(2)}) async-start(), calls=%async_computation.8 | async-start | bytes 10813440 | tf_op jit(solution)/shard_map/reduce_scatter | solution.py:877
  334.7 19.7 %collective-permute-start.12 = (bf16[512,1408]{1,0:T(8,128)(2,1)}, bf16[512,1408]{1,0:T(8,128)(2,1)}, u32[]{:S(2)}, u32[]{:S(2)}) collective-permute-start(bf16[512,1408]{1,0:T(8,128)(2,1)} %fusion.45), channel_id=1, source_target_pairs={{0,4},{4,0},{1,5},{5,1},{2,6},{6,2},{3,7},{7,3},{8,12},{12,8},{9,1... | collective-permute-start | bytes 4325384 | tf_op jit(solution)/shard_map/ppermute | solution.py:719
  446.8 37.4 %collective-permute-start.19 = (bf16[512,1408]{1,0:T(8,128)(2,1)S(1)}, bf16[512,1408]{1,0:T(8,128)(2,1)S(1)}, u32[]{:S(2)}, u32[]{:S(2)}) collective-permute-start(bf16[512,1408]{1,0:T(8,128)(2,1)S(1)} %slice.905), channel_id=1, source_target_pairs={{0,4},{4,0},{1,5},{5,1},{2,6},{6,2},{3,7},{7,3},{8,12},{12,8},{9,1... | collective-permute-start | bytes 4325384 | tf_op jit(solution)/shard_map/ppermute | solution.py:719
  448.8 17.7 %collective-permute-start.30 = (bf16[128,1408]{1,0:T(8,128)(2,1)S(1)}, bf16[128,1408]{1,0:T(8,128)(2,1)S(1)}, u32[]{:S(2)}, u32[]{:S(2)}) collective-permute-start(bf16[128,1408]{1,0:T(8,128)(2,1)S(1)} %get-tuple-element.321), channel_id=1, source_target_pairs={{0,4},{1,1},{2,5},{3,0},{4,6},{5,3},{6,7},{7,2},{8,12},{9,9},{10,1... | collective-permute-start | bytes 1081352 | tf_op jit(solution)/shard_map/ppermute | solution.py:816
  453.7 26.5 %collective-permute-start.31 = (bf16[128,1408]{1,0:T(8,128)(2,1)S(1)}, bf16[128,1408]{1,0:T(8,128)(2,1)S(1)}, u32[]{:S(2)}, u32[]{:S(2)}) collective-permute-start(bf16[128,1408]{1,0:T(8,128)(2,1)S(1)} %get-tuple-element.320), channel_id=1, source_target_pairs={{0,1},{1,5},{2,0},{3,4},{4,3},{5,7},{6,2},{7,6},{8,9},{9,13},{10,8... | collective-permute-start | bytes 1081352 | tf_op jit(solution)/shard_map/ppermute | solution.py:816
  453.8 26.5 %collective-permute-start.32 = (bf16[128,1408]{1,0:T(8,128)(2,1)S(1)}, bf16[128,1408]{1,0:T(8,128)(2,1)S(1)}, u32[]{:S(2)}, u32[]{:S(2)}) collective-permute-start(bf16[128,1408]{1,0:T(8,128)(2,1)S(1)} %get-tuple-element.319), channel_id=1, source_target_pairs={{0,5},{1,0},{2,4},{3,1},{4,7},{5,2},{6,6},{7,3},{8,13},{9,8},{10,1... | collective-permute-start | bytes 1081352 | tf_op jit(solution)/shard_map/ppermute | solution.py:816
  480.5 23.1 %collective-permute-start.33 = (bf16[512,1408]{1,0:T(8,128)(2,1)S(1)}, bf16[512,1408]{1,0:T(8,128)(2,1)}, u32[]{:S(2)}, u32[]{:S(2)}) collective-permute-start(bf16[512,1408]{1,0:T(8,128)(2,1)S(1)} %bitcast.486), channel_id=1, source_target_pairs={{0,4},{4,0},{1,5},{5,1},{2,6},{6,2},{3,7},{7,3},{8,12},{12,8},{9,1... | collective-permute-start | bytes 4325384 | tf_op jit(solution)/shard_map/ppermute | solution.py:719
  487.8 19.0 %collective-permute-start.20 = (bf16[512,1408]{1,0:T(8,128)(2,1)}, bf16[512,1408]{1,0:T(8,128)(2,1)}, u32[]{:S(2)}, u32[]{:S(2)}) collective-permute-start(bf16[512,1408]{1,0:T(8,128)(2,1)} %add_convert_fusion.1), channel_id=1, source_target_pairs={{0,4},{4,0},{1,5},{5,1},{2,6},{6,2},{3,7},{7,3},{8,12},{12,8},{9,1... | collective-permute-start | bytes 4325384 | tf_op jit(solution)/shard_map/ppermute | solution.py:719
  578.6 230.1 %reduce-scatter.8.cloned.1.call-start = ((), (), s32[]{:S(2)}) async-start(), calls=%async_computation.6 | async-start | bytes 10813440 | tf_op jit(solution)/shard_map/reduce_scatter | solution.py:877
  579.3 375.1 %reduce-scatter.14.cloned.1.call-start = ((), (), s32[]{:S(2)}) async-start(), calls=%async_computation.13 | async-start | bytes 9912320 | tf_op jit(solution)/shard_map/reduce_scatter | solution.py:877
  662.2 383.6 %all-gather.18.cloned.1.call-start = ((), (), s32[]{:S(2)}) async-start(), calls=%async_computation.9 | async-start | bytes 2703360 | tf_op jit(solution)/shard_map/all_gather | solution.py:891
  740.0 17.1 %collective-permute-start.56 = (bf16[192,1408]{1,0:T(8,128)(2,1)S(1)}, bf16[192,1408]{1,0:T(8,128)(2,1)S(1)}, u32[]{:S(2)}, u32[]{:S(2)}) collective-permute-start(bf16[192,1408]{1,0:T(8,128)(2,1)S(1)} %get-tuple-element.276), channel_id=1, source_target_pairs={{0,1},{1,2},{2,3},{3,0},{4,5},{5,6},{6,7},{7,4},{8,9},{9,10},{10,1... | collective-permute-start | bytes 1622024 | tf_op jit(solution)/shard_map/ppermute | solution.py:727
  740.0 39.3 %collective-permute-start.57 = (bf16[192,1408]{1,0:T(8,128)(2,1)S(1)}, bf16[192,1408]{1,0:T(8,128)(2,1)S(1)}, u32[]{:S(2)}, u32[]{:S(2)}) collective-permute-start(bf16[192,1408]{1,0:T(8,128)(2,1)S(1)} %get-tuple-element.278), channel_id=1, source_target_pairs={{0,2},{1,3},{2,0},{3,1},{4,6},{5,7},{6,4},{7,5},{8,10},{9,11},{10,... | collective-permute-start | bytes 1622024 | tf_op jit(solution)/shard_map/ppermute | solution.py:727
  740.6 38.7 %collective-permute-start.58 = (bf16[192,1408]{1,0:T(8,128)(2,1)S(1)}, bf16[192,1408]{1,0:T(8,128)(2,1)S(1)}, u32[]{:S(2)}, u32[]{:S(2)}) collective-permute-start(bf16[192,1408]{1,0:T(8,128)(2,1)S(1)} %get-tuple-element.277), channel_id=1, source_target_pairs={{0,3},{1,0},{2,1},{3,2},{4,7},{5,4},{6,5},{7,6},{8,11},{9,8},{10,9... | collective-permute-start | bytes 1622024 | tf_op jit(solution)/shard_map/ppermute | solution.py:727
  781.5 264.3 %all-gather.16.cloned.1.call-start = ((), (), s32[]{:S(2)}) async-start(), calls=%async_computation.7 | async-start | bytes 2703360 | tf_op jit(solution)/shard_map/all_gather | solution.py:891
  792.5 80.4 %collective-permute-start.38 = (bf16[512,1408]{1,0:T(8,128)(2,1)}, bf16[512,1408]{1,0:T(8,128)(2,1)S(1)}, u32[]{:S(2)}, u32[]{:S(2)}) collective-permute-start(bf16[512,1408]{1,0:T(8,128)(2,1)} %slice.901), channel_id=1, source_target_pairs={{0,4},{4,0},{1,5},{5,1},{2,6},{6,2},{3,7},{7,3},{8,12},{12,8},{9,1... | collective-permute-start | bytes 4325384 | tf_op jit(solution)/shard_map/ppermute | solution.py:719
  810.4 24.8 %collective-permute-start.53 = (bf16[192,1408]{1,0:T(8,128)(2,1)S(1)}, bf16[192,1408]{1,0:T(8,128)(2,1)S(1)}, u32[]{:S(2)}, u32[]{:S(2)}) collective-permute-start(bf16[192,1408]{1,0:T(8,128)(2,1)S(1)} %get-tuple-element.279), channel_id=1, source_target_pairs={{0,1},{1,2},{2,3},{3,0},{4,5},{5,6},{6,7},{7,4},{8,9},{9,10},{10,1... | collective-permute-start | bytes 1622024 | tf_op jit(solution)/shard_map/ppermute | solution.py:727
  821.6 35.7 %collective-permute-start.54 = (bf16[192,1408]{1,0:T(8,128)(2,1)S(1)}, bf16[192,1408]{1,0:T(8,128)(2,1)S(1)}, u32[]{:S(2)}, u32[]{:S(2)}) collective-permute-start(bf16[192,1408]{1,0:T(8,128)(2,1)S(1)} %get-tuple-element.281), channel_id=1, source_target_pairs={{0,2},{1,3},{2,0},{3,1},{4,6},{5,7},{6,4},{7,5},{8,10},{9,11},{10,... | collective-permute-start | bytes 1622024 | tf_op jit(solution)/shard_map/ppermute | solution.py:727
  822.5 34.8 %collective-permute-start.55 = (bf16[192,1408]{1,0:T(8,128)(2,1)S(1)}, bf16[192,1408]{1,0:T(8,128)(2,1)S(1)}, u32[]{:S(2)}, u32[]{:S(2)}) collective-permute-start(bf16[192,1408]{1,0:T(8,128)(2,1)S(1)} %get-tuple-element.280), channel_id=1, source_target_pairs={{0,3},{1,0},{2,1},{3,2},{4,7},{5,4},{6,5},{7,6},{8,11},{9,8},{10,9... | collective-permute-start | bytes 1622024 | tf_op jit(solution)/shard_map/ppermute | solution.py:727
  859.4 186.4 %reduce-scatter.6.cloned.1.call-start = ((), (), s32[]{:S(2)}) async-start(), calls=%async_computation.5 | async-start | bytes 9912320 | tf_op jit(solution)/shard_map/reduce_scatter | solution.py:877
  878.9 211.0 %all-gather.24.cloned.1.call-start = ((), (), s32[]{:S(2)}) async-start(), calls=%async_computation.14 | async-start | bytes 2478080 | tf_op jit(solution)/shard_map/all_gather | solution.py:891
  884.8 20.1 %collective-permute-start.25 = (bf16[136,1408]{1,0:T(8,128)(2,1)S(1)}, bf16[136,1408]{1,0:T(8,128)(2,1)S(1)}, u32[]{:S(2)}, u32[]{:S(2)}) collective-permute-start(bf16[136,1408]{1,0:T(8,128)(2,1)S(1)} %get-tuple-element.309), channel_id=1, source_target_pairs={{0,0},{4,1},{1,2},{5,3},{2,4},{6,5},{3,6},{7,7},{8,8},{12,9},{9,10... | collective-permute-start | bytes 1148936 | tf_op jit(solution)/shard_map/ppermute | solution.py:825
  885.5 160.4 %collective-permute-start.26 = (bf16[136,1408]{1,0:T(8,128)(2,1)}, bf16[136,1408]{1,0:T(8,128)(2,1)S(1)}, u32[]{:S(2)}, u32[]{:S(2)}) collective-permute-start(bf16[136,1408]{1,0:T(8,128)(2,1)} %get-tuple-element.308), channel_id=1, source_target_pairs={{4,0},{1,1},{5,2},{0,3},{6,4},{3,5},{7,6},{2,7},{12,8},{9,9},{13,1... | collective-permute-start | bytes 1148936 | tf_op jit(solution)/shard_map/ppermute | solution.py:825
  903.3 26.7 %collective-permute-start.39 = (bf16[128,1408]{1,0:T(8,128)(2,1)}, bf16[128,1408]{1,0:T(8,128)(2,1)S(1)}, u32[]{:S(2)}, u32[]{:S(2)}) collective-permute-start(bf16[128,1408]{1,0:T(8,128)(2,1)} %get-tuple-element.317), channel_id=1, source_target_pairs={{0,0},{4,1},{1,2},{5,3},{2,4},{6,5},{3,6},{7,7},{8,8},{12,9},{9,10... | collective-permute-start | bytes 1081352 | tf_op jit(solution)/shard_map/ppermute | solution.py:825
  926.0 20.6 %collective-permute-start.42 = (bf16[128,1408]{1,0:T(8,128)(2,1)}, bf16[128,1408]{1,0:T(8,128)(2,1)S(1)}, u32[]{:S(2)}, u32[]{:S(2)}) collective-permute-start(bf16[128,1408]{1,0:T(8,128)(2,1)} %get-tuple-element.314), channel_id=1, source_target_pairs={{5,0},{0,1},{4,2},{1,3},{7,4},{2,5},{6,6},{3,7},{13,8},{8,9},{12,1... | collective-permute-start | bytes 1081352 | tf_op jit(solution)/shard_map/ppermute | solution.py:825
  953.2 82.7 %collective-permute-start.48 = (bf16[1408,1408]{1,0:T(8,128)(2,1)}, bf16[1408,1408]{1,0:T(8,128)(2,1)}, u32[]{:S(2)}, u32[]{:S(2)}) collective-permute-start(bf16[1408,1408]{1,0:T(8,128)(2,1)} %convolution_convert_fusion.2), channel_id=1, source_target_pairs={{0,4},{4,0},{1,5},{5,1},{2,6},{6,2},{3,7},{7,3},{8,12},{12,8},{9,1... | collective-permute-start | bytes 11894792 | tf_op jit(solution)/shard_map/ppermute | solution.py:719
  957.0 18.2 %collective-permute-start.67 = (bf16[176,1408]{1,0:T(8,128)(2,1)}, bf16[176,1408]{1,0:T(8,128)(2,1)S(1)}, u32[]{:S(2)}, u32[]{:S(2)}) collective-permute-start(bf16[176,1408]{1,0:T(8,128)(2,1)} %get-tuple-element.290), channel_id=1, source_target_pairs={{0,1},{1,2},{2,3},{3,0},{4,5},{5,6},{6,7},{7,4},{8,9},{9,10},{10,1... | collective-permute-start | bytes 1486856 | tf_op jit(solution)/shard_map/ppermute | solution.py:727
  960.5 36.0 %collective-permute-start.68 = (bf16[176,1408]{1,0:T(8,128)(2,1)}, bf16[176,1408]{1,0:T(8,128)(2,1)S(1)}, u32[]{:S(2)}, u32[]{:S(2)}) collective-permute-start(bf16[176,1408]{1,0:T(8,128)(2,1)} %get-tuple-element.292), channel_id=1, source_target_pairs={{0,2},{1,3},{2,0},{3,1},{4,6},{5,7},{6,4},{7,5},{8,10},{9,11},{10,... | collective-permute-start | bytes 1486856 | tf_op jit(solution)/shard_map/ppermute | solution.py:727
  963.3 55.4 %collective-permute-start.69 = (bf16[176,1408]{1,0:T(8,128)(2,1)}, bf16[176,1408]{1,0:T(8,128)(2,1)S(1)}, u32[]{:S(2)}, u32[]{:S(2)}) collective-permute-start(bf16[176,1408]{1,0:T(8,128)(2,1)} %get-tuple-element.291), channel_id=1, source_target_pairs={{0,3},{1,0},{2,1},{3,2},{4,7},{5,4},{6,5},{7,6},{8,11},{9,8},{10,9... | collective-permute-start | bytes 1486856 | tf_op jit(solution)/shard_map/ppermute | solution.py:727
  975.3 71.4 %collective-permute-start.27 = (bf16[136,1408]{1,0:T(8,128)(2,1)}, bf16[136,1408]{1,0:T(8,128)(2,1)}, u32[]{:S(2)}, u32[]{:S(2)}) collective-permute-start(bf16[136,1408]{1,0:T(8,128)(2,1)} %get-tuple-element.307), channel_id=1, source_target_pairs={{1,0},{5,1},{0,2},{4,3},{3,4},{7,5},{2,6},{6,7},{9,8},{13,9},{8,10... | collective-permute-start | bytes 1148936 | tf_op jit(solution)/shard_map/ppermute | solution.py:825
  996.5 52.1 %collective-permute-start.28 = (bf16[136,1408]{1,0:T(8,128)(2,1)}, bf16[136,1408]{1,0:T(8,128)(2,1)}, u32[]{:S(2)}, u32[]{:S(2)}) collective-permute-start(bf16[136,1408]{1,0:T(8,128)(2,1)} %get-tuple-element.306), channel_id=1, source_target_pairs={{5,0},{0,1},{4,2},{1,3},{7,4},{2,5},{6,6},{3,7},{13,8},{8,9},{12,1... | collective-permute-start | bytes 1148936 | tf_op jit(solution)/shard_map/ppermute | solution.py:825
  1020.9 131.8 %reduce-scatter.12.cloned.1.call-start = ((), (), s32[]{:S(2)}) async-start(), calls=%async_computation.10 | async-start | bytes 5406720 | tf_op jit(solution)/shard_map/reduce_scatter | solution.py:1251
  1045.8 137.2 %all-gather.22.cloned.1.call-start = ((), (), s32[]{:S(2)}) async-start(), calls=%async_computation.12 | async-start | bytes 2478080 | tf_op jit(solution)/shard_map/all_gather | solution.py:891
  1056.2 18.9 %collective-permute-start.44 = (bf16[128,1408]{1,0:T(8,128)(2,1)S(1)}, bf16[128,1408]{1,0:T(8,128)(2,1)S(1)}, u32[]{:S(2)}, u32[]{:S(2)}) collective-permute-start(bf16[128,1408]{1,0:T(8,128)(2,1)S(1)} %add_convert_fusion.6), channel_id=1, source_target_pairs={{0,0},{1,2},{2,4},{3,6},{4,1},{5,3},{6,5},{7,7},{8,8},{9,10},{10,1... | collective-permute-start | bytes 1081352 | tf_op jit(solution)/shard_map/ppermute | solution.py:1190
  1056.9 23.9 %collective-permute-start.45 = (bf16[128,1408]{1,0:T(8,128)(2,1)S(1)}, bf16[128,1408]{1,0:T(8,128)(2,1)S(1)}, u32[]{:S(2)}, u32[]{:S(2)}) collective-permute-start(bf16[128,1408]{1,0:T(8,128)(2,1)S(1)} %add_convert_fusion.6), channel_id=1, source_target_pairs={{0,1},{1,3},{2,5},{3,7},{4,2},{5,0},{6,6},{7,4},{8,9},{9,11},{10,1... | collective-permute-start | bytes 1081352 | tf_op jit(solution)/shard_map/ppermute | solution.py:1190
  1063.7 18.4 %collective-permute-start.46 = (bf16[128,1408]{1,0:T(8,128)(2,1)S(1)}, bf16[128,1408]{1,0:T(8,128)(2,1)S(1)}, u32[]{:S(2)}, u32[]{:S(2)}) collective-permute-start(bf16[128,1408]{1,0:T(8,128)(2,1)S(1)} %add_convert_fusion.6), channel_id=1, source_target_pairs={{0,2},{1,0},{2,6},{3,4},{4,3},{5,1},{6,7},{7,5},{8,10},{9,8},{10,1... | collective-permute-start | bytes 1081352 | tf_op jit(solution)/shard_map/ppermute | solution.py:1190
  1065.3 20.2 %collective-permute-start.47 = (bf16[128,1408]{1,0:T(8,128)(2,1)S(1)}, bf16[128,1408]{1,0:T(8,128)(2,1)S(1)}, u32[]{:S(2)}, u32[]{:S(2)}) collective-permute-start(bf16[128,1408]{1,0:T(8,128)(2,1)S(1)} %add_convert_fusion.6), channel_id=1, source_target_pairs={{0,3},{1,1},{2,7},{3,5},{4,0},{5,2},{6,4},{7,6},{8,11},{9,9},{10,1... | collective-permute-start | bytes 1081352 | tf_op jit(solution)/shard_map/ppermute | solution.py:1190
  1089.9 48.2 %collective-permute-start.70 = (bf16[704,1408]{1,0:T(8,128)(2,1)}, bf16[704,1408]{1,0:T(8,128)(2,1)}, u32[]{:S(2)}, u32[]{:S(2)}) collective-permute-start(bf16[704,1408]{1,0:T(8,128)(2,1)} %all-gather.24.cloned.1.call-done), channel_id=1, source_target_pairs={{0,4},{4,0},{1,5},{5,1},{2,6},{6,2},{3,7},{7,3},{8,12},{12,8},{9,1... | collective-permute-start | bytes 5947400 | tf_op jit(solution)/shard_map/ppermute | solution.py:719
  1099.9 36.0 %collective-permute-start.64 = (bf16[176,1408]{1,0:T(8,128)(2,1)S(1)}, bf16[176,1408]{1,0:T(8,128)(2,1)S(1)}, u32[]{:S(2)}, u32[]{:S(2)}) collective-permute-start(bf16[176,1408]{1,0:T(8,128)(2,1)S(1)} %get-tuple-element.303), channel_id=1, source_target_pairs={{0,2},{1,3},{2,0},{3,1},{4,6},{5,7},{6,4},{7,5},{8,10},{9,11},{10,... | collective-permute-start | bytes 1486856 | tf_op jit(solution)/shard_map/ppermute | solution.py:727
  1103.3 32.6 %collective-permute-start.65 = (bf16[176,1408]{1,0:T(8,128)(2,1)S(1)}, bf16[176,1408]{1,0:T(8,128)(2,1)S(1)}, u32[]{:S(2)}, u32[]{:S(2)}) collective-permute-start(bf16[176,1408]{1,0:T(8,128)(2,1)S(1)} %get-tuple-element.302), channel_id=1, source_target_pairs={{0,3},{1,0},{2,1},{3,2},{4,7},{5,4},{6,5},{7,6},{8,11},{9,8},{10,9... | collective-permute-start | bytes 1486856 | tf_op jit(solution)/shard_map/ppermute | solution.py:727
  1109.5 55.6 %collective-permute-start.72 = (bf16[768,1408]{1,0:T(8,128)(2,1)}, bf16[768,1408]{1,0:T(8,128)(2,1)}, u32[]{:S(2)}, u32[]{:S(2)}) collective-permute-start(bf16[768,1408]{1,0:T(8,128)(2,1)} %all-gather.16.cloned.1.call-done), channel_id=1, source_target_pairs={{0,4},{4,0},{1,5},{5,1},{2,6},{6,2},{3,7},{7,3},{8,12},{12,8},{9,1... | collective-permute-start | bytes 6488072 | tf_op jit(solution)/shard_map/ppermute | solution.py:719
  1115.5 30.4 %collective-permute-start.71 = (bf16[768,1408]{1,0:T(8,128)(2,1)}, bf16[768,1408]{1,0:T(8,128)(2,1)}, u32[]{:S(2)}, u32[]{:S(2)}) collective-permute-start(bf16[768,1408]{1,0:T(8,128)(2,1)} %all-gather.18.cloned.1.call-done), channel_id=1, source_target_pairs={{0,4},{4,0},{1,5},{5,1},{2,6},{6,2},{3,7},{7,3},{8,12},{12,8},{9,1... | collective-permute-start | bytes 6488072 | tf_op jit(solution)/shard_map/ppermute | solution.py:719
  1138.1 93.0 %all-gather.20.cloned.1.call-start = ((), (), s32[]{:S(2)}) async-start(), calls=%async_computation.11 | async-start | bytes 1689600 | tf_op jit(solution)/shard_map/all_gather | solution.py:1288
  1154.7 32.5 %collective-permute-start.60 = (bf16[120,1408]{1,0:T(8,128)(2,1)S(1)}, bf16[120,1408]{1,0:T(8,128)(2,1)S(1)}, u32[]{:S(2)}, u32[]{:S(2)}) collective-permute-start(bf16[120,1408]{1,0:T(8,128)(2,1)S(1)} %get-tuple-element.340), channel_id=1, source_target_pairs={{0,2},{1,3},{2,0},{3,1},{4,6},{5,7},{6,4},{7,5},{8,10},{9,11},{10,... | collective-permute-start | bytes 1013768 | tf_op jit(solution)/shard_map/ppermute | solution.py:727
  1183.1 26.6 %collective-permute-start.66 = (bf16[704,1408]{1,0:T(8,128)(2,1)}, bf16[704,1408]{1,0:T(8,128)(2,1)}, u32[]{:S(2)}, u32[]{:S(2)}) collective-permute-start(bf16[704,1408]{1,0:T(8,128)(2,1)} %all-gather.22.cloned.1.call-done), channel_id=1, source_target_pairs={{0,4},{4,0},{1,5},{5,1},{2,6},{6,2},{3,7},{7,3},{8,12},{12,8},{9,1... | collective-permute-start | bytes 5947400 | tf_op jit(solution)/shard_map/ppermute | solution.py:719
  1184.6 17.6 %collective-permute-start.61 = (bf16[120,1408]{1,0:T(8,128)(2,1)S(1)}, bf16[120,1408]{1,0:T(8,128)(2,1)S(1)}, u32[]{:S(2)}, u32[]{:S(2)}) collective-permute-start(bf16[120,1408]{1,0:T(8,128)(2,1)S(1)} %concatenate.249), channel_id=1, source_target_pairs={{0,3},{1,0},{2,1},{3,2},{4,7},{5,4},{6,5},{7,6},{8,11},{9,8},{10,9... | collective-permute-start | bytes 1013768 | tf_op jit(solution)/shard_map/ppermute | solution.py:727
  (215 other events, 2843.5 us)
Sparse Core Ops, SparseCore 0:
  42.4 50.5 all-gather.25
  98.0 65.5 all-gather.27
  166.0 67.2 all-gather.29
  257.3 70.6 all-gather.31
  330.3 71.7 all-gather.33
  578.7 87.8 reduce-scatter.9
  669.8 88.5 reduce-scatter.7
  762.1 82.6 reduce-scatter.13
  846.6 35.8 all-gather.17
  884.2 35.8 all-gather.15
  923.8 82.6 reduce-scatter.5
  1021.0 36.1 all-gather.23
  1060.8 53.8 reduce-scatter.11
  1138.2 44.8 all-gather.21
  1203.3 27.6 all-gather.19

commit v3 on v2

--- a/solution.py
+++ b/solution.py
@@ -537,9 +537,9 @@
 
 def attention_kernel(turned, rows, *refs):
     if turned:
-        q_ref, k_ref, v_ref, gain_ref, count_ref, table_ref, out_ref, inv_ref = refs
+        q_ref, k_ref, v_ref, gain_ref, count_ref, table_ref, out_ref, exact_ref, inv_ref = refs
     else:
-        q_ref, k_ref, v_ref, gain_ref, count_ref, out_ref, inv_ref = refs
+        q_ref, k_ref, v_ref, gain_ref, count_ref, out_ref, exact_ref, inv_ref = refs
     low = jnp.bfloat16
     keys = norm_rows(k_ref[...])[0] * gain_ref[1:2, :]
     if turned:
@@ -561,7 +561,9 @@
         powers = jnp.exp2(matmul_nt(query.astype(low), keys)).astype(low)
         sums = matmul_nn(powers, mixed)
         inverse = 1.0 / sums[:, LANES:]
-        out_ref[part, :] = (sums[:, :LANES] * inverse).astype(low)
+        result = sums[:, :LANES] * inverse
+        out_ref[part, :] = result.astype(low)
+        exact_ref[part, :] = result
         inv_ref[part, :] = inverse
 
 
@@ -596,10 +598,10 @@
             query = turn_rows(query, tables)
         query = query.astype(low)
         grad = grad_ref[part, :].astype(f32) * inv_ref[part, :]
-        delta = row_sums(grad * out_ref[part, :].astype(f32))
+        grad_low = grad.astype(low)
+        delta = row_sums(grad_low.astype(f32) * out_ref[part, :], True)
         delta_high = delta.astype(low).astype(f32)
         lane = lane_index((rows, LANES))
-        grad_low = grad.astype(low)
         grad_more = jnp.where(
             lane == HD, -delta_high, jnp.where(lane == HD + 1, delta_high - delta, grad)
         ).astype(low)
@@ -657,19 +659,17 @@
         functools.partial(attention_kernel, turned, min(rows, length)),
         grid=(heads,),
         in_specs=attention_specs(turned, length, key_length, *at),
-        out_specs=[
-            pl.BlockSpec((length, LANES), lambda h: (0, h)),
-            pl.BlockSpec((length, LANES), lambda h: (0, h)),
-        ],
+        out_specs=[pl.BlockSpec((length, LANES), lambda h: (0, h))] * 3,
         out_shape=[
             jax.ShapeDtypeStruct((length, heads * LANES), jnp.bfloat16),
+            jax.ShapeDtypeStruct((length, heads * LANES), jnp.float32),
             jax.ShapeDtypeStruct((length, heads * LANES), jnp.float32),
         ],
         compiler_params=pltpu.CompilerParams(
             dimension_semantics=("arbitrary",), vmem_limit_bytes=40 * 2**20
         ),
         cost_estimate=pl.CostEstimate(
-            flops=4 * pairs * LANES, transcendentals=pairs, bytes_accessed=18 * heads * length * LANES
+            flops=4 * pairs * LANES, transcendentals=pairs, bytes_accessed=22 * heads * length * LANES
         ),
         name="attention_turned" if turned else "attention_plain",
     )(*operands)
@@ -707,10 +707,12 @@
             dimension_semantics=("arbitrary",), vmem_limit_bytes=40 * 2**20
         ),
         cost_estimate=pl.CostEstimate(
-            flops=10 * pairs * LANES, transcendentals=pairs, bytes_accessed=30 * heads * length * LANES
+            flops=10 * pairs * LANES, transcendentals=pairs, bytes_accessed=32 * heads * length * LANES
         ),
         name="attention_turned_back" if turned else "attention_plain_back",
     )(*operands, grad, mixed, inverse)
+
+
 def ring_pairs(size, step):
     return [(rank, (rank + step) % size) for rank in range(size)]
 
@@ -853,8 +855,8 @@
     def gather_shares(later):
         return lax.all_gather(later, "chip", axis=0, tiled=False)
 
-    def gather_rows(own, later):
-        return jnp.concatenate([own[:, None], gather_shares(later)], 1)
+    def gather_all(part):
+        return lax.all_gather(part, ("chip", "tensor"), axis=0, tiled=True)
 
     def pad_heads(own, rest):
         own = own.reshape(own.shape[0], 1, half // HD, HD, width)
@@ -929,15 +931,23 @@
     small = jnp.pad(small, (0, small_rows * width - small_size)).reshape(1, small_rows, width)
     small = jnp.broadcast_to(small, (chips, small_rows, width))
     self_later, small_later = quarters([self_own, small])
+    self_later, cross_own = tie(self_later, cross_own)
     (cross_later,) = quarters([cross_own])
-    up_later, down_later = quarters([up_own, down_own])
-    self_full = pad_heads(self_own, gather_shares(self_later))
-    cross_full = pad_heads(cross_own, gather_shares(cross_later))
+    cross_later, grad_home = tie(cross_later, out_grad)
+    self_rest = gather_shares(self_later)
+    self_in_w = pad_heads(self_own[:3], self_rest[:3]).reshape(3 * lanes, width)
+    self_out_w = pad_heads(self_own[3:], self_rest[3:])[0]
+    cross_rest = gather_shares(cross_later)
+    cross_query_w = pad_heads(cross_own[:1], cross_rest[:1])[0]
+    cross_text_w = pad_heads(cross_own[1:3], cross_rest[1:3]).reshape(2 * lanes, width)
+    cross_out_w = pad_heads(cross_own[3:], cross_rest[3:])[0]
+    up_full = gather_all(pick(up_own, chip))
+    down_full = gather_all(pick(down_own, chip))
 
     small_rel = jnp.concatenate([small[:1], small_later], 0).reshape(size, -1)[:, :small_size].astype(f32)
     shift_size = sequences * shard
     up_bias_f = (
-        small_rel[:, 2 * shift_size + shard :]
+        rolled(small_rel[:, 2 * shift_size + shard :], (size - rank) % size)
         .reshape(size, chips, ff_part)
         .transpose(1, 0, 2)
         .reshape(size * ff_half)
@@ -1036,22 +1046,20 @@
     stream_low = spread(stream_home.reshape(size, piece_len, width)).reshape(own_len, width)
     stream = stream_low.astype(f32)
 
-    attn_in = both(first_norm(stream, shift_vec).astype(low))
-    projected = dot_tt(attn_in, self_full[:3].reshape(3 * lanes, width))
-    projected, grad_home = tie(projected, out_grad)
     grad_low = spread(grad_home.reshape(size, piece_len, width)).reshape(own_len, width)
+    attn_own, grad_low = tie(first_norm(stream, shift_vec).astype(low), grad_low)
+    attn_in = both(attn_own)
+    projected = dot_tt(attn_in, self_in_w)
     self_inputs = (heads, projected, projected, projected, (0, heads, 2 * heads), self_gains, key_count)
-    attention_combined, self_inverse = attention(*self_inputs, tables, rows=2 * own_len)
-    up_full = gather_rows(up_own, up_later).reshape(size * ff_half, width)
-    down_full = gather_rows(down_own, down_later).reshape(size * ff_half, width)
-    branch_one = halve(dot_nn(attention_combined, self_full[3])) + out_bias.astype(f32)
+    attention_combined, self_exact, self_inverse = attention(*self_inputs, tables, rows=2 * own_len)
+    branch_one = halve(dot_nn(attention_combined, self_out_w)) + out_bias.astype(f32)
     stream_two = stream + branch_one
     cross_in = both(affine_norm(stream_two, norm2_gain_f, norm2_beta_f).astype(low))
-    query_raw = dot_tt(cross_in, cross_full[0])
-    text_raw = dot_tt(text_own, cross_full[1:3].reshape(2 * lanes, width))
+    query_raw = dot_tt(cross_in, cross_query_w)
+    text_raw = dot_tt(text_own, cross_text_w)
     cross_inputs = (heads, query_raw, text_raw, text_raw, (0, 0, heads), cross_gains, key_count)
-    crossed_combined, cross_inverse = attention(*cross_inputs, rows=2 * own_len)
-    branch_two = halve(dot_nn(crossed_combined, cross_full[3])) + cross_out_bias.astype(f32)
+    crossed_combined, cross_exact, cross_inverse = attention(*cross_inputs, rows=2 * own_len)
+    branch_two = halve(dot_nn(crossed_combined, cross_out_w)) + cross_out_bias.astype(f32)
     stream_three = stream_two + branch_two
     mlp_in = both(affine_norm(stream_three, norm3_gain_f, norm3_beta_f).astype(low))
     gelu_fn = partial(jax.nn.gelu, approximate=True)
@@ -1068,29 +1076,20 @@
     )
     stat_rows = stats.reshape(5, size, piece_len).transpose(1, 0, 2).reshape(size, 1, 5 * piece_len)
     stat_rows = jnp.pad(stat_rows.astype(low), ((0, 0), (0, 7), (0, width - 5 * piece_len)))
-    home = collect(jnp.concatenate([output.astype(low).reshape(size, piece_len, width), stat_rows], 1))
-    output_home = home[:, :piece_len].reshape(latent_in.shape)
-    stats_home = (
-        home[:, piece_len, : 5 * piece_len]
-        .reshape(sequences, 2, 5, piece_len)
-        .transpose(0, 2, 1, 3)
-        .reshape(sequences, 5, local_len)
-        .astype(f32)
-    )
+    home_rows = jnp.concatenate([output.astype(low).reshape(size, piece_len, width), stat_rows], 1)
 
     grad_out = grad_low.astype(f32)
     down_bias_part = jnp.sum(grad_out, axis=0)
     grad_all = both(grad_low)
     down_grad = dot_tn(hidden_state, grad_all).astype(low)
     grad_all, down_grad = tie(grad_all, down_grad)
-    down_parts = scatter_rows(down_grad.reshape(chips, size, ff_part, width))
+    down_parts = rolled(scatter_rows(down_grad.reshape(chips, size, ff_part, width)), rank)
     hidden_grad = dot_tt(grad_all, down_full)
     pre_grad = gelu_back(hidden_grad)[0]
     up_bias_part = jnp.sum(pre_grad, axis=0)
     pre_low = pre_grad.astype(low)
     up_grad = dot_tn(pre_low, mlp_in).astype(low)
     pre_low, up_grad = tie(pre_low, up_grad)
-    up_parts = scatter_rows(up_grad.reshape(chips, size, ff_part, width))
     norm3_grad_in = halve(dot_nn(pre_low, up_full))
     _, norm3_back = jax.vjp(affine_norm, stream_three, norm3_gain_f, norm3_beta_f)
     from_three, gain3_part, beta3_part = norm3_back(norm3_grad_in)
@@ -1098,11 +1097,15 @@
     cross_bias_part = jnp.sum(grad_three, axis=0)
     three_all = both(grad_three.astype(low))
     cross_out_grad = dot_tn(crossed_combined, three_all)
-    cross_mixed_grad = dot_tt(three_all, cross_full[3]).astype(low)
+    cross_mixed_grad = dot_tt(three_all, cross_out_w).astype(low)
+    up_grad, down_parts, cross_mixed_grad = tie(up_grad, down_parts, cross_mixed_grad)
+    up_parts = rolled(scatter_rows(up_grad.reshape(chips, size, ff_part, width)), rank)
     query_low, keys_low, values_low, cross_gain_sums = attention_back(
-        *cross_inputs, cross_mixed_grad, crossed_combined, cross_inverse, rows=2 * own_len
-    )
-    norm2_grad_in = halve(dot_nn(query_low, cross_full[0]))
+        *cross_inputs, cross_mixed_grad, cross_exact, cross_inverse, rows=2 * own_len
+    )
+    down_total = add_line(down_parts[0], send_line(down_parts))
+    query_low, keys_low, values_low, down_total = tie(query_low, keys_low, values_low, down_total)
+    norm2_grad_in = halve(dot_nn(query_low, cross_query_w))
     cross_grads = jnp.stack(
         [
             trim_heads(grad.astype(low))
@@ -1114,22 +1117,34 @@
             )
         ],
     )
-    cross_parts = scatter_rows(cross_grads)
-    text_part = dot_nn(keys_low, cross_full[1]) + dot_nn(values_low, cross_full[2])
+    text_part = dot_nn(keys_low, cross_text_w[:lanes]) + dot_nn(values_low, cross_text_w[lanes:])
     _, norm2_back = jax.vjp(affine_norm, stream_two, norm2_gain_f, norm2_beta_f)
     from_two, gain2_part, beta2_part = norm2_back(norm2_grad_in)
     grad_two = grad_three + from_two
     out_bias_part = jnp.sum(grad_two, axis=0)
     two_all = both(grad_two.astype(low))
     out_weight_part = dot_tn(attention_combined, two_all)
-    attn_mixed_grad = dot_tt(two_all, self_full[3]).astype(low)
+    attn_mixed_grad = dot_tt(two_all, self_out_w).astype(low)
+    home = collect(home_rows)
+    cross_grads, up_parts, attn_mixed_grad, home = tie(cross_grads, up_parts, attn_mixed_grad, home)
+    output_home = home[:, :piece_len].reshape(latent_in.shape)
+    stats_home = (
+        home[:, piece_len, : 5 * piece_len]
+        .reshape(sequences, 2, 5, piece_len)
+        .transpose(0, 2, 1, 3)
+        .reshape(sequences, 5, local_len)
+        .astype(f32)
+    )
+    cross_parts = scatter_rows(cross_grads)
     *proj_grads, self_gain_sums = attention_back(
-        *self_inputs, attn_mixed_grad, attention_combined, self_inverse, tables, rows=2 * own_len
-    )
+        *self_inputs, attn_mixed_grad, self_exact, self_inverse, tables, rows=2 * own_len
+    )
+    up_total = add_line(up_parts[0], send_line(up_parts))
+    *proj_grads, up_total = tie(*proj_grads, up_total)
     first_grad_in = halve(
-        dot_nn(proj_grads[0], self_full[0])
-        + dot_nn(proj_grads[1], self_full[1])
-        + dot_nn(proj_grads[2], self_full[2])
+        dot_nn(proj_grads[0], self_in_w[:lanes])
+        + dot_nn(proj_grads[1], self_in_w[lanes : 2 * lanes])
+        + dot_nn(proj_grads[2], self_in_w[2 * lanes :])
     )
     self_grads = jnp.stack(
         [trim_heads(dot_tn(grad, attn_in).astype(low)) for grad in proj_grads]
@@ -1138,16 +1153,20 @@
     _, first_back = jax.vjp(first_norm, stream, shift_vec)
     from_one, shift_own_grad = first_back(first_grad_in)
     grad_one = (grad_two + from_one).astype(low)
-    down_sum = share_rows(add_line(down_parts[0], send_line(down_parts)))
-    up_sum = share_rows(add_line(up_parts[0], send_line(up_parts)))
-    grad_one, self_grads = tie(grad_one, self_grads)
+
+    self_grads, cross_parts = tie(self_grads, cross_parts)
     self_parts = scatter_rows(self_grads)
-
     home_grad = collect(grad_one.reshape(size, piece_len, width)).reshape(own_len, width)
+    home_grad, cross_parts = tie(home_grad, cross_parts)
+    cross_total = add_line(cross_parts[0], send_line(cross_parts))
     skip_bias_part = jnp.sum(home_grad.astype(f32), axis=0)
     skip_own_grad = dot_tn(home_grad, normed_own)
     skip_other_grad = dot_tn(home_grad, normed_other).astype(low)
     skip_sum = (skip_own_grad + swap_cores(skip_other_grad).astype(f32)).astype(low)
+    first_sums = jnp.concatenate([down_total, up_total, cross_total], 0)
+    first_sums, self_parts, skip_sum = tie(first_sums, self_parts, skip_sum)
+    first_sums = share_rows(first_sums)
+    self_total = add_line(self_parts[0], send_line(self_parts))
     own_in = dot_nn(home_grad, skip_own_w)
     other_in = dot_nn(home_grad, skip_other_w)
     latent_in_grad = jnp.where(core == 0, own_in, other_in)
@@ -1180,23 +1199,7 @@
     text_rows = lax.dynamic_slice_in_dim(text_part, core * text_half, text_half, 0)
     text_away = lax.dynamic_slice_in_dim(text_part, (1 - core) * text_half, text_half, 0).astype(low)
     text_rows = (text_rows + swap_cores(text_away).astype(f32)).astype(low)
-    text_pieces = []
-    for turn in range(size):
-        pairs = [
-            (c * size + r, (r // 2) * size + (2 * (r % 2) + c + turn) % size)
-            for c in range(2)
-            for r in range(size)
-        ]
-        text_pieces.append(lax.ppermute(text_rows, ("core", "tensor"), pairs))
-    text_stack = jnp.stack(text_pieces)
-    text_grad = (
-        jnp.stack([pick(text_stack, (rank - k) % size) for k in range(size)])
-        .reshape(sequences, text_size, width)
-        .astype(f32)
-    )
-
-    up_bias_rel = up_bias_part.reshape(chips, size, ff_part).transpose(1, 0, 2).reshape(size, ff_half)
-    up_bias_abs = rolled(up_bias_rel, (size - rank) % size)
+    up_bias_abs = up_bias_part.reshape(chips, size, ff_part).transpose(1, 0, 2).reshape(size, ff_half)
     up_bias_vec = jnp.stack(
         [jnp.where(core == 0, up_bias_abs, 0.0), jnp.where(core == 1, up_bias_abs, 0.0)], 1
     ).reshape(2 * size * ff_half)
@@ -1247,13 +1250,48 @@
     skip_rel_grad = rolled(skip_sum.reshape(size, chips, skip_part, width), rank).transpose(1, 0, 2, 3)
     skip_rows = size * skip_part
     skip_rows_all = jnp.concatenate([skip_rel_grad.reshape(chips, skip_rows, width), vectors], 1)
-    skip_rows_all, self_parts, down_sum, up_sum = tie(skip_rows_all, self_parts, down_sum, up_sum)
+    skip_rows_all, first_sums, self_total, text_rows = tie(
+        skip_rows_all, first_sums, self_total, text_rows
+    )
+    text_pieces = []
+    for turn in range(size):
+        pairs = [
+            (c * size + r, (r // 2) * size + (2 * (r % 2) + c + turn) % size)
+            for c in range(2)
+            for r in range(size)
+        ]
+        text_pieces.append(lax.ppermute(text_rows, ("core", "tensor"), pairs))
+    text_stack = jnp.stack(text_pieces)
+    text_grad = (
+        jnp.stack([pick(text_stack, (rank - k) % size) for k in range(size)])
+        .reshape(sequences, text_size, width)
+        .astype(f32)
+    )
     parts = lax.psum_scatter(
         skip_rows_all.reshape(-1, width), "chip", scatter_dimension=0, tiled=True
     )
-    cross_sum, self_sum = (
-        share_rows(add_line(parts[0], send_line(parts))) for parts in (cross_parts, self_parts)
-    )
+    self_total, parts = tie(self_total, parts)
+    self_sum = share_rows(self_total)
+    vector_mine = parts[skip_rows:]
+    skip_total = parts[:skip_part].astype(f32)
+    vector_line = [vector_mine]
+    for step in range(1, size):
+        arrived = from_earlier(
+            jnp.concatenate([parts[step * skip_part : (step + 1) * skip_part], vector_mine], 0), step, size
+        )
+        skip_total = skip_total + arrived[:skip_part].astype(f32)
+        vector_line.append(arrived[skip_part:])
+    vector_line = jnp.stack(vector_line)
+    vector_total = pick(vector_line, rank).astype(f32)
+    for source in range(1, size):
+        vector_total = vector_total + pick(vector_line, (rank - source) % size).astype(f32)
+    skip_send = jnp.concatenate([skip_total, vector_total], 0).astype(low)
+    skip_send, self_sum = tie(skip_send, self_sum)
+    total = share_rows(skip_send).reshape(chips, skip_part + vector_part, width)
+    first_sums = first_sums.reshape(chips, 2 * ff_part + half, width)
+    down_sum = first_sums[:, :ff_part].reshape(ff_half, width)
+    up_sum = first_sums[:, ff_part : 2 * ff_part].reshape(ff_half, width)
+    cross_sum = first_sums[:, 2 * ff_part :]
     down0, down1 = by_core(down_sum)
     down_weight_grad = jnp.concatenate([down0, down1], 0).astype(f32)
     up0, up1 = by_core(up_sum)
@@ -1272,22 +1310,6 @@
     self0, self1 = (part.reshape(4, half, width) for part in by_core(self_sum))
     qkv_weight_grad = jnp.stack([cols_of(self0[i], self1[i]) for i in range(3)])
     out_weight_grad = rows_of(self0[3], self1[3])
-    vector_mine = parts[skip_rows:]
-    skip_total = parts[:skip_part].astype(f32)
-    vector_line = [vector_mine]
-    for step in range(1, size):
-        arrived = from_earlier(
-            jnp.concatenate([parts[step * skip_part : (step + 1) * skip_part], vector_mine], 0), step, size
-        )
-        skip_total = skip_total + arrived[:skip_part].astype(f32)
-        vector_line.append(arrived[skip_part:])
-    vector_line = jnp.stack(vector_line)
-    vector_total = pick(vector_line, rank).astype(f32)
-    for source in range(1, size):
-        vector_total = vector_total + pick(vector_line, (rank - source) % size).astype(f32)
-    total = lax.all_gather(
-        jnp.concatenate([skip_total, vector_total], 0).astype(low), "chip", axis=0, tiled=True
-    ).reshape(chips, skip_part + vector_part, width)
     total_other = swap_cores(total)
     skip0 = jnp.where(core == 0, total[:, :skip_part], total_other[:, :skip_part])
     skip1 = jnp.where(core == 0, total_other[:, :skip_part], total[:, :skip_part])

time: 1270 us -> 1150 us (0.906)
  waiting for transfers between devices: 434 us -> 369 us
  local copies, waits for them, and re-layouts: 146 us -> 122 us
  other arithmetic: 155 us -> 140 us
  matrix products: 234 us -> 221 us
    ppermute x15 -> x12, waiting for transfers between devices: 194 us -> 106 us  [from_later(): return lax.ppermute(values, 'tensor', ring_pairs(size, -step))]
    all_gather x1 -> x2, waiting for transfers between devices: 18.5 us -> 64.2 us  [gather_all(): return lax.all_gather(part, ('chip', 'tensor'), axis=0, tiled=True)]
    ppermute x15, waiting for transfers between devices: 127 us -> 88.3 us  [from_earlier(): return lax.ppermute(values, 'tensor', ring_pairs(size, step))]
    ppermute x8, starting transfers between devices: 51.5 us -> 21.5 us  [collect(): lax.ppermute(values[turn], ('core', 'tensor'), [(target, source) for sour...]
    ppermute x23, starting transfers between devices: 21.1 us -> 44.7 us  [swap_cores(): return lax.ppermute(values, 'core', [(0, 1), (1, 0)])]
    all_gather x4 -> x3, waiting for transfers between devices: 4.14 us -> 22.6 us  [share_rows(): return lax.all_gather(total, 'chip', axis=0, tiled=True)]
    concatenate x4 -> x2, other arithmetic: 19.4 us -> 2.02 us  [the longest x1 1.26 us: chip_local(): first_sums = jnp.concatenate([down_total, up_total, cross_total], 0)]
    ppermute x8, waiting for transfers between devices: 16.5 us -> 33.6 us  [collect(): lax.ppermute(values[turn], ('core', 'tensor'), [(target, source) for sour...]
  transfers between devices with their start and end apart: 88 -> 83, of which waited for: 37 -> 35; matrix products, arithmetic and copies ran while one was open for 32% -> 36% of each run, Pallas kernels for 8% -> 9%
where the time goes in v3:
time: 1150 us
  waiting for transfers between devices  369 us (32%)
  matrix products  221 us (19%)
  starting transfers between devices  177 us (15%)
  other arithmetic  140 us (12%)
  local copies, waits for them, and re-layouts  122 us (11%)
  Pallas kernels  99.7 us (9%)
  between operations  17.8 us (2%)
    ppermute x12, waiting for transfers between devices, from_later(): return lax.ppermute(values, 'tensor', ring_pairs(size, -step))  106 us
    ppermute x15, waiting for transfers between devices, from_earlier(): return lax.ppermute(values, 'tensor', ring_pairs(size, step))  88.3 us
    dot_general x9, matrix products, dot_tt(): lax.dot_general(left, right, (((1,), (1,)), ((), ())), preferred_element_...  79.1 us
    dot_general x12, matrix products, dot_nn(): lax.dot_general(left, right, (((1,), (0,)), ((), ())), preferred_element_...  68.8 us
    dot_general x12, matrix products, dot_tn(): lax.dot_general(left, right, (((0,), (0,)), ((), ())), preferred_element_...  68.6 us
    pallas_call x2, Pallas kernels, attention_back(): pl.pallas_call(functools.partial(attention_back_kernel, turned, min(rows,...  66.4 us
    all_gather x2, waiting for transfers between devices, gather_all(): return lax.all_gather(part, ('chip', 'tensor'), axis=0, tiled=True)  64.2 us
    unnamed x378, local copies, waits for them, and re-layouts  52.9 us
  transfers between devices with their start and end apart: 83, of which 35 were waited for; matrix products, arithmetic and copies ran while one was open for 36% of the time, Pallas kernels for 9%

profile of v3, /device:TPU:0, one launch (start us, length us, event | category | flops | bytes accessed | tf_op | source)
XLA Modules:
  0.0 1146.4 jit_solution(17311375935029247985)
XLA Ops:
  9.6 5.0 collective-permute-start
  15.6 5.4 collective-permute-done
  21.8 13.9 %collective-permute-done.1 = bf16[88,1408]{1,0:T(8,128)(2,1)S(1)} collective-permute-done((bf16[88,1408]{1,0:T(8,128)(2,1)S(1)}, bf16[88,1408]{1,0:T(8,128)(2,1)S(1)}, u32[]{:S(2)}, u32[]{:S(2)}) %collective-permute-start.1) | collective-permute-done | bytes 247840 | tf_op jit(solution)/shard_map/ppermute | solution.py:725
  53.0 7.5 collective-permute-done.4
  60.5 33.3 %collective-permute-done.5 = bf16[184,1408]{1,0:T(8,128)(2,1)S(1)} collective-permute-done((bf16[184,1408]{1,0:T(8,128)(2,1)S(1)}, bf16[184,1408]{1,0:T(8,128)(2,1)S(1)}, u32[]{:S(2)}, u32[]{:S(2)}) %collective-permute-start.5) | collective-permute-done | bytes 518176 | tf_op jit(solution)/shard_map/ppermute | solution.py:725
  99.7 9.6 collective-permute-done.12
  109.3 31.8 %collective-permute-done.13 = bf16[176,1408]{1,0:T(8,128)(2,1)S(1)} collective-permute-done((bf16[176,1408]{1,0:T(8,128)(2,1)S(1)}, bf16[176,1408]{1,0:T(8,128)(2,1)S(1)}, u32[]{:S(2)}, u32[]{:S(2)}) %collective-permute-start.13) | collective-permute-done | bytes 495648 | tf_op jit(solution)/shard_map/ppermute | solution.py:725
  166.4 5.1 fusion.49
  171.6 5.3 copy.89
  178.3 5.5 collective-permute-done.11
  194.9 4.8 fusion.137
  199.7 4.8 fusion.29
  207.2 5.4 collective-permute-start.8
  214.1 8.7 collective-permute-done.17
  224.9 5.6 collective-permute-start.22
  230.8 19.2 %collective-permute-done.9 = bf16[128,1408]{1,0:T(8,128)(2,1)} collective-permute-done((bf16[128,1408]{1,0:T(8,128)(2,1)}, bf16[128,1408]{1,0:T(8,128)(2,1)}, u32[]{:S(2)}, u32[]{:S(2)}) %collective-permute-start.9) | collective-permute-done | bytes 360480 | tf_op jit(solution)/shard_map/ppermute | solution.py:818
  256.2 14.2 %collective-permute-start.19 = (bf16[512,1408]{1,0:T(8,128)(2,1)S(1)}, bf16[512,1408]{1,0:T(8,128)(2,1)S(1)}, u32[]{:S(2)}, u32[]{:S(2)}) collective-permute-start(bf16[512,1408]{1,0:T(8,128)(2,1)S(1)} %fusion.41), channel_id=1, source_target_pairs={{0,4},{4,0},{1,5},{5,1},{2,6},{6,2},{3,7},{7,3},{8,12},{12,8},{9,1... | collective-permute-start | bytes 4325384 | tf_op jit(solution)/shard_map/ppermute | solution.py:721
  275.3 12.3 %fusion.172.refs_0_.refs_1_.refs_2_ = f32[1024,3072]{1,0:T(8,128)} fusion(bf16[1024,1408]{1,0:T(8,128)(2,1)S(1)} %constant_dynamic-update-slice_fusion, bf16[3072,1408]{1,0:T(8,128)(2,1)S(1)} %bitcast.528), kind=kOutput, calls=%fused_computation.517 | convolution fusion | flops 8858370048 | bytes 24117248 | tf_op jit(solution)/shard_map/dot_general | solution.py:754
  288.4 21.3 %attention_turned.1 = (bf16[1024,1024]{1,0:T(8,128)(2,1)S(1)}, f32[1024,1024]{1,0:T(8,128)S(1)}, f32[1024,1024]{1,0:T(8,128)S(1)}) custom-call(f32[1024,3072]{1,0:T(8,128)} %fusion.172.refs_0_.refs_1_.refs_2_, f32[1024,3072]{1,0:T(8,128)} %fusion.172.refs_0_.refs_1_.refs_2_, f32[1024,3072]{1,0:T(8,128)} %fusion.172.refs_0_.refs_1_.refs_2_, ...), custom_call_target="tpu_custom_call" | custom-call | flops 4294967296 | bytes 23068672 | tf_op jit(solution)/shard_map/attention_turned/pallas_call | solution.py:658
  336.6 7.1 fusion.57.refs_0_
  343.7 11.9 %attention_plain.1 = (bf16[1024,1024]{1,0:T(8,128)(2,1)S(1)}, f32[1024,1024]{1,0:T(8,128)S(1)}, f32[1024,1024]{1,0:T(8,128)S(1)}) custom-call(f32[1024,1024]{1,0:T(8,128)} %fusion.57.refs_0_, f32[256,2048]{1,0:T(8,128)S(1)} %fusion.174.refs_1_.refs_2_, f32[256,2048]{1,0:T(8,128)S(1)} %fusion.174.refs_1_.refs_2_, f32[8,128]{1,0:T(8,128)S(1)} %select_maximum_fusion.refs_3_, ...), custom_call_target="tpu_custom_call" | custom-call | flops 1073741824 | bytes 23068672 | tf_op jit(solution)/shard_map/attention_plain/pallas_call | solution.py:658
  372.4 13.3 %fusion.22 = f32[1024,3072]{1,0:T(8,128)S(1)} fusion(bf16[1,3072,1408]{2,1,0:T(8,128)(2,1)} %all-gather.26.cloned.1.call-done, bf16[512,1408]{1,0:T(8,128)(2,1)} %collective-permute-done.25, bf16[512,1408]{1,0:T(8,128)(2,1)} %add_convert_fusion.2), kind=kOutput, calls=%fused_computation.32 | convolution fusion | flops 8864137216 | bytes 24117248 | tf_op jit(solution)/shard_map/dot_general | solution.py:754
  390.4 14.9 %convolution_convert_fusion.1 = bf16[3072,1408]{1,0:T(8,128)(2,1)} fusion(bf16[1024,1408]{1,0:T(8,128)(2,1)} %constant_dynamic-update-slice_fusion.10, f32[1024,3072]{1,0:T(8,128)S(1)} %fusion.22, f32[3072]{0:T(1024)S(1)} %add.849), kind=kOutput, calls=%fused_computation.16 | convolution fusion | flops 8894152704 | bytes 24129536 | tf_op jit(solution)/shard_map/dot_general | solution.py:762
  405.4 64.2 %all-gather.28.cloned.1.call-done = bf16[1,3072,1408]{2,1,0:T(8,128)(2,1)} async-done(((bf16[1,192,1408]{2,1,0:T(8,128)(2,1)}), bf16[1,3072,1408]{2,1,0:T(8,128)(2,1)}) %all-gather.28.cloned.1.call-update) | async-done | bytes 8650768 | tf_op jit(solution)/shard_map/all_gather | solution.py:859
  469.6 22.8 %fusion.152 = (bf16[3072]{0:T(1024)(128)(2,1)}, bf16[1024,3072]{1,0:T(8,128)(2,1)S(1)}) fusion(f32[1024,3072]{1,0:T(8,128)} %copy-done.165, f32[3072]{0:T(1024)S(1)} %add.849, bf16[1024,1408]{1,0:T(8,128)(2,1)} %constant_dynamic-update-slice_fusion.10, bf16[1,3072,1408]{2,1,0:T(8,128)(2,1)} %all-gather.28.cloned.1.call-done), kind=kOutput, calls=%fused_computation.497 | convolution fusion | flops 8927572992 | bytes 30427136 | tf_op jit(solution)/shard_map/dot_general | solution.py:754
  495.1 14.1 %convolution_convert_fusion = bf16[3072,1408]{1,0:T(8,128)(2,1)} fusion(bf16[1024,3072]{1,0:T(8,128)(2,1)S(1)} %get-tuple-element.94, bf16[512,1408]{1,0:T(8,128)(2,1)} %collective-permute-done.25, bf16[512,1408]{1,0:T(8,128)(2,1)} %add_convert_fusion.2), kind=kOutput, calls=%fused_computation.15 | convolution fusion | flops 8868462592 | bytes 17825792 | tf_op jit(solution)/shard_map/dot_general | solution.py:762
  509.2 13.2 %fusion.20 = f32[1024,1408]{1,0:T(8,128)S(1)} fusion(bf16[1024,3072]{1,0:T(8,128)(2,1)} %copy-done.166, bf16[1,3072,1408]{2,1,0:T(8,128)(2,1)} %all-gather.26.cloned.1.call-done), kind=kOutput, calls=%fused_computation.30 | convolution fusion | flops 8858370048 | bytes 20709376 | tf_op jit(solution)/shard_map/dot_general | solution.py:758
  522.6 17.2 %fusion.16 = f32[1024,1408]{1,0:T(8,128)S(1)} fusion(bf16[1,3072,1408]{2,1,0:T(8,128)(2,1)} %all-gather.28.cloned.1.call-done, f32[1024,3072]{1,0:T(8,128)} %copy-done.165, f32[3072]{0:T(1024)S(1)} %add.849), kind=kOutput, calls=%fused_computation.26 | convolution fusion | flops 8889827328 | bytes 27013120 | tf_op jit(solution)/shard_map/dot_general | solution.py:758
  554.0 7.5 convolution_convert_fusion.12.refs_5_
  567.9 6.0 collective-permute-start.35
  578.0 5.0 collective-permute-done.35
  583.0 8.2 collective-permute-done.36
  595.9 8.6 collective-permute-start.28
  608.7 20.6 %attention_plain_back.1 = (bf16[1024,1024]{1,0:T(8,128)(2,1)S(1)}, bf16[256,1024]{1,0:T(8,128)(2,1)S(1)}, bf16[256,1024]{1,0:T(8,128)(2,1)S(1)}, f32[8,8,128]{2,1,0:T(8,128)S(1)}) custom-call(f32[1024,1024]{1,0:T(8,128)S(1)} %copy-done.4, f32[256,2048]{1,0:T(8,128)S(1)} %copy-done.3, f32[256,2048]{1,0:T(8,128)S(1)} %copy-done.3, f32[8,128]{1,0:T(8,128)S(1)} %copy-done.15, ...), custom_call_target="tpu_custom_call" | custom-call | flops 2684354560 | bytes 33554432 | tf_op jit(solution)/shard_map/attention_plain_back/pallas_call | solution.py:685
  629.4 13.0 %collective-permute-done.29 = bf16[192,1408]{1,0:T(8,128)(2,1)S(1)} collective-permute-done((bf16[192,1408]{1,0:T(8,128)(2,1)S(1)}, bf16[192,1408]{1,0:T(8,128)(2,1)S(1)}, u32[]{:S(2)}, u32[]{:S(2)}) %collective-permute-start.29) | collective-permute-done | bytes 540704 | tf_op jit(solution)/shard_map/ppermute | solution.py:729
  650.5 5.1 convolution_convert_fusion.9
  657.0 5.5 convolution_convert_fusion.10
  684.4 6.8 fusion.153
  696.4 12.2 %collective-permute-start.38 = (bf16[192,1408]{1,0:T(8,128)(2,1)S(1)}, bf16[192,1408]{1,0:T(8,128)(2,1)}, u32[]{:S(2)}, u32[]{:S(2)}) collective-permute-start(bf16[192,1408]{1,0:T(8,128)(2,1)S(1)} %get-tuple-element.333), channel_id=1, source_target_pairs={{0,1},{1,2},{2,3},{3,0},{4,5},{5,6},{6,7},{7,4},{8,9},{9,10},{10,1... | collective-permute-start | bytes 1622024 | tf_op jit(solution)/shard_map/ppermute | solution.py:729
  711.1 45.8 %attention_turned_back.1 = (bf16[1024,1024]{1,0:T(8,128)(2,1)S(1)}, bf16[1024,1024]{1,0:T(8,128)(2,1)S(1)}, bf16[1024,1024]{1,0:T(8,128)(2,1)S(1)}, f32[8,8,128]{2,1,0:T(8,128)S(1)}) custom-call(f32[1024,3072]{1,0:T(8,128)} %fusion.172.refs_0_.refs_1_.refs_2_, f32[1024,3072]{1,0:T(8,128)} %fusion.172.refs_0_.refs_1_.refs_2_, ...), custom_call_target="tpu_custom_call" | custom-call | flops 10737418240 | bytes 33554432 | tf_op jit(solution)/shard_map/attention_turned_back/pallas_call | solution.py:685
  778.2 6.0 fusion.178
  801.2 5.8 collective-permute-start.43
  813.8 7.7 collective-permute-done.44
  821.6 5.8 collective-permute-done.45
  834.2 8.4 collective-permute-start.49
  848.4 10.5 collective-permute-done.46
  858.9 20.4 %collective-permute-done.47 = bf16[176,1408]{1,0:T(8,128)(2,1)S(1)} collective-permute-done((bf16[176,1408]{1,0:T(8,128)(2,1)S(1)}, bf16[176,1408]{1,0:T(8,128)(2,1)S(1)}, u32[]{:S(2)}, u32[]{:S(2)}) %collective-permute-start.47) | collective-permute-done | bytes 495648 | tf_op jit(solution)/shard_map/ppermute | solution.py:729
  880.9 7.6 add_convert_fusion
  898.2 12.9 %collective-permute-start.51 = (f32[1408]{0:T(1024)S(1)}, f32[1408]{0:T(1024)S(1)}, u32[]{:S(2)}, u32[]{:S(2)}) collective-permute-start(f32[1408]{0:T(1024)S(1)} %add.884), channel_id=1, source_target_pairs={{0,3},{1,0},{2,1},{3,2},{4,7},{5,4},{6,5},{7,6},{8,11},{9,8},{10,9... | collective-permute-start | bytes 16904 | tf_op jit(solution)/shard_map/ppermute | solution.py:725
  918.1 5.3 fusion.179
  923.5 8.1 multiply_reduce_fusion.3
  944.0 5.9 collective-permute-done.54
  949.9 18.6 %collective-permute-done.55 = bf16[176,1408]{1,0:T(8,128)(2,1)S(1)} collective-permute-done((bf16[176,1408]{1,0:T(8,128)(2,1)S(1)}, bf16[176,1408]{1,0:T(8,128)(2,1)S(1)}, u32[]{:S(2)}, u32[]{:S(2)}) %collective-permute-start.55) | collective-permute-done | bytes 495648 | tf_op jit(solution)/shard_map/ppermute | solution.py:729
  974.8 5.7 subtract_multiply_fusion
  981.2 14.2 %collective-permute-start.59 = (bf16[128,1408]{1,0:T(8,128)(2,1)S(1)}, bf16[128,1408]{1,0:T(8,128)(2,1)S(1)}, u32[]{:S(2)}, u32[]{:S(2)}) collective-permute-start(bf16[128,1408]{1,0:T(8,128)(2,1)S(1)} %copy-done.109), channel_id=1, source_target_pairs={{0,1},{1,3},{2,5},{3,7},{4,2},{5,0},{6,6},{7,4},{8,9},{9,11},{10,1... | collective-permute-start | bytes 1081352 | tf_op jit(solution)/shard_map/ppermute | solution.py:1263
  1005.3 10.7 collective-permute-start.69
  1025.2 6.8 reduce-scatter.14.cloned.1.call-done
  1037.7 4.8 select_bitcast_fusion.1
  1046.3 14.5 %collective-permute-done.63 = bf16[120,1408]{1,0:T(8,128)(2,1)S(1)} collective-permute-done((bf16[120,1408]{1,0:T(8,128)(2,1)S(1)}, bf16[120,1408]{1,0:T(8,128)(2,1)S(1)}, u32[]{:S(2)}, u32[]{:S(2)}) %collective-permute-start.63) | collective-permute-done | bytes 337952 | tf_op jit(solution)/shard_map/ppermute | solution.py:729
  1060.9 5.4 collective-permute-done.64
  1069.9 6.3 maximum_convert_fusion
  1076.2 9.1 copy.101
  1090.1 6.4 maximum_convert_fusion.1
  1099.5 20.1 %all-gather.18.cloned.1.call-done = bf16[480,1408]{1,0:T(8,128)(2,1)} async-done(((bf16[120,1408]{1,0:T(8,128)(2,1)}), bf16[480,1408]{1,0:T(8,128)(2,1)}) %all-gather.18.cloned.1.call-update) | async-done | bytes 1351696 | tf_op jit(solution)/shard_map/all_gather | solution.py:893
  (821 shorter events, 359.9 us)
Async XLA Ops:
  7.2 164.4 %all-gather.20.cloned.1.call-start = ((), (), s32[]{:S(2)}) async-start(), calls=%async_computation.13 | async-start | bytes 4956160 | tf_op jit(solution)/shard_map/all_gather | solution.py:856
  14.6 21.1 %collective-permute-start.1 = (bf16[88,1408]{1,0:T(8,128)(2,1)S(1)}, bf16[88,1408]{1,0:T(8,128)(2,1)S(1)}, u32[]{:S(2)}, u32[]{:S(2)}) collective-permute-start(bf16[88,1408]{1,0:T(8,128)(2,1)S(1)} %get-tuple-element.392), channel_id=1, source_target_pairs={{0,2},{1,3},{2,0},{3,1},{4,6},{5,7},{6,4},{7,5},{8,10},{9,11},{10,... | collective-permute-start | bytes 743432 | tf_op jit(solution)/shard_map/ppermute | solution.py:725
  14.6 21.8 %collective-permute-start.2 = (bf16[88,1408]{1,0:T(8,128)(2,1)S(1)}, bf16[88,1408]{1,0:T(8,128)(2,1)S(1)}, u32[]{:S(2)}, u32[]{:S(2)}) collective-permute-start(bf16[88,1408]{1,0:T(8,128)(2,1)S(1)} %get-tuple-element.392), channel_id=1, source_target_pairs={{0,1},{1,2},{2,3},{3,0},{4,5},{5,6},{6,7},{7,4},{8,9},{9,10},{10,1... | collective-permute-start | bytes 743432 | tf_op jit(solution)/shard_map/ppermute | solution.py:725
  42.2 188.5 %all-gather.22.cloned.1.call-start = ((), (), s32[]{:S(2)}) async-start(), calls=%async_computation.14 | async-start | bytes 7434240 | tf_op jit(solution)/shard_map/all_gather | solution.py:856
  47.2 13.3 %collective-permute-start.4 = (bf16[184,1408]{1,0:T(8,128)(2,1)S(1)}, bf16[184,1408]{1,0:T(8,128)(2,1)S(1)}, u32[]{:S(2)}, u32[]{:S(2)}) collective-permute-start(bf16[184,1408]{1,0:T(8,128)(2,1)S(1)} %pad_maximum_fusion.25), channel_id=1, source_target_pairs={{0,3},{1,0},{2,1},{3,2},{4,7},{5,4},{6,5},{7,6},{8,11},{9,8},{10,9... | collective-permute-start | bytes 1554440 | tf_op jit(solution)/shard_map/ppermute | solution.py:725
  47.3 46.6 %collective-permute-start.5 = (bf16[184,1408]{1,0:T(8,128)(2,1)S(1)}, bf16[184,1408]{1,0:T(8,128)(2,1)S(1)}, u32[]{:S(2)}, u32[]{:S(2)}) collective-permute-start(bf16[184,1408]{1,0:T(8,128)(2,1)S(1)} %pad_maximum_fusion.25), channel_id=1, source_target_pairs={{0,2},{1,3},{2,0},{3,1},{4,6},{5,7},{6,4},{7,5},{8,10},{9,11},{10,... | collective-permute-start | bytes 1554440 | tf_op jit(solution)/shard_map/ppermute | solution.py:725
  49.4 44.4 %collective-permute-start.6 = (bf16[184,1408]{1,0:T(8,128)(2,1)S(1)}, bf16[184,1408]{1,0:T(8,128)(2,1)S(1)}, u32[]{:S(2)}, u32[]{:S(2)}) collective-permute-start(bf16[184,1408]{1,0:T(8,128)(2,1)S(1)} %pad_maximum_fusion.25), channel_id=1, source_target_pairs={{0,1},{1,2},{2,3},{3,0},{4,5},{5,6},{6,7},{7,4},{8,9},{9,10},{10,1... | collective-permute-start | bytes 1554440 | tf_op jit(solution)/shard_map/ppermute | solution.py:725
  96.1 223.0 %all-gather.24.cloned.1.call-start = ((), (), s32[]{:S(2)}) async-start(), calls=%async_computation.15 | async-start | bytes 7434240 | tf_op jit(solution)/shard_map/all_gather | solution.py:856
  97.2 43.9 %collective-permute-start.13 = (bf16[176,1408]{1,0:T(8,128)(2,1)S(1)}, bf16[176,1408]{1,0:T(8,128)(2,1)S(1)}, u32[]{:S(2)}, u32[]{:S(2)}) collective-permute-start(bf16[176,1408]{1,0:T(8,128)(2,1)S(1)} %get-tuple-element.363), channel_id=1, source_target_pairs={{0,2},{1,3},{2,0},{3,1},{4,6},{5,7},{6,4},{7,5},{8,10},{9,11},{10,... | collective-permute-start | bytes 1486856 | tf_op jit(solution)/shard_map/ppermute | solution.py:725
  97.7 43.5 %collective-permute-start.14 = (bf16[176,1408]{1,0:T(8,128)(2,1)S(1)}, bf16[176,1408]{1,0:T(8,128)(2,1)S(1)}, u32[]{:S(2)}, u32[]{:S(2)}) collective-permute-start(bf16[176,1408]{1,0:T(8,128)(2,1)S(1)} %get-tuple-element.363), channel_id=1, source_target_pairs={{0,1},{1,2},{2,3},{3,0},{4,5},{5,6},{6,7},{7,4},{8,9},{9,10},{10,1... | collective-permute-start | bytes 1486856 | tf_op jit(solution)/shard_map/ppermute | solution.py:725
  142.5 230.0 %all-gather.26.cloned.1.call-start = ((), (), s32[]{:S(2)}) async-start(), calls=%async_computation.16 | async-start | bytes 9191424 | tf_op jit(solution)/shard_map/all_gather | solution.py:859
  151.7 317.9 %all-gather.28.cloned.1.call-start = ((), (), s32[]{:S(2)}) async-start(), calls=%async_computation.17 | async-start | bytes 9191424 | tf_op jit(solution)/shard_map/all_gather | solution.py:859
  154.5 407.1 %reduce-scatter.6.cloned.1.call-start = ((), (), s32[]{:S(2)}) async-start(), calls=%async_computation.5 | async-start | bytes 10813440 | tf_op jit(solution)/shard_map/reduce_scatter | solution.py:879
  177.0 22.7 %collective-permute-start.3 = (bf16[1408,1408]{1,0:T(8,128)(2,1)}, bf16[1408,1408]{1,0:T(8,128)(2,1)}, u32[]{:S(2)}, u32[]{:S(2)}) collective-permute-start(bf16[1408,1408]{1,0:T(8,128)(2,1)} %bitcast.11), channel_id=1, source_target_pairs={{0,4},{4,0},{1,5},{5,1},{2,6},{6,2},{3,7},{7,3},{8,12},{12,8},{9,1... | collective-permute-start | bytes 11894792 | tf_op jit(solution)/shard_map/ppermute | solution.py:721
  186.7 20.5 %collective-permute-start.15 = (bf16[128,1408]{1,0:T(8,128)(2,1)S(1)}, bf16[128,1408]{1,0:T(8,128)(2,1)S(1)}, u32[]{:S(2)}, u32[]{:S(2)}) collective-permute-start(bf16[128,1408]{1,0:T(8,128)(2,1)S(1)} %get-tuple-element.380), channel_id=1, source_target_pairs={{0,0},{1,4},{2,1},{3,5},{4,2},{5,6},{6,3},{7,7},{8,8},{9,12},{10,9... | collective-permute-start | bytes 1081352 | tf_op jit(solution)/shard_map/ppermute | solution.py:818
  187.4 25.2 %collective-permute-start.16 = (bf16[128,1408]{1,0:T(8,128)(2,1)S(1)}, bf16[128,1408]{1,0:T(8,128)(2,1)S(1)}, u32[]{:S(2)}, u32[]{:S(2)}) collective-permute-start(bf16[128,1408]{1,0:T(8,128)(2,1)S(1)} %get-tuple-element.383), channel_id=1, source_target_pairs={{0,4},{1,1},{2,5},{3,0},{4,6},{5,3},{6,7},{7,2},{8,12},{9,9},{10,1... | collective-permute-start | bytes 1081352 | tf_op jit(solution)/shard_map/ppermute | solution.py:818
  191.5 31.3 %collective-permute-start.17 = (bf16[128,1408]{1,0:T(8,128)(2,1)S(1)}, bf16[128,1408]{1,0:T(8,128)(2,1)S(1)}, u32[]{:S(2)}, u32[]{:S(2)}) collective-permute-start(bf16[128,1408]{1,0:T(8,128)(2,1)S(1)} %get-tuple-element.382), channel_id=1, source_target_pairs={{0,1},{1,5},{2,0},{3,4},{4,3},{5,7},{6,2},{7,6},{8,9},{9,13},{10,8... | collective-permute-start | bytes 1081352 | tf_op jit(solution)/shard_map/ppermute | solution.py:818
  191.6 33.3 %collective-permute-start.18 = (bf16[128,1408]{1,0:T(8,128)(2,1)S(1)}, bf16[128,1408]{1,0:T(8,128)(2,1)S(1)}, u32[]{:S(2)}, u32[]{:S(2)}) collective-permute-start(bf16[128,1408]{1,0:T(8,128)(2,1)S(1)} %get-tuple-element.381), channel_id=1, source_target_pairs={{0,5},{1,0},{2,4},{3,1},{4,7},{5,2},{6,6},{7,3},{8,13},{9,8},{10,1... | collective-permute-start | bytes 1081352 | tf_op jit(solution)/shard_map/ppermute | solution.py:818
  205.6 25.2 %collective-permute-start.7 = (bf16[128,1408]{1,0:T(8,128)(2,1)}, bf16[128,1408]{1,0:T(8,128)(2,1)S(1)}, u32[]{:S(2)}, u32[]{:S(2)}) collective-permute-start(bf16[128,1408]{1,0:T(8,128)(2,1)} %get-tuple-element.384), channel_id=1, source_target_pairs={{0,0},{1,4},{2,1},{3,5},{4,2},{5,6},{6,3},{7,7},{8,8},{9,12},{10,9... | collective-permute-start | bytes 1081352 | tf_op jit(solution)/shard_map/ppermute | solution.py:818
  207.2 23.6 %collective-permute-start.8 = (bf16[128,1408]{1,0:T(8,128)(2,1)}, bf16[128,1408]{1,0:T(8,128)(2,1)}, u32[]{:S(2)}, u32[]{:S(2)}) collective-permute-start(bf16[128,1408]{1,0:T(8,128)(2,1)} %get-tuple-element.387), channel_id=1, source_target_pairs={{0,4},{1,1},{2,5},{3,0},{4,6},{5,3},{6,7},{7,2},{8,12},{9,9},{10,1... | collective-permute-start | bytes 1081352 | tf_op jit(solution)/shard_map/ppermute | solution.py:818
  212.6 37.4 %collective-permute-start.9 = (bf16[128,1408]{1,0:T(8,128)(2,1)}, bf16[128,1408]{1,0:T(8,128)(2,1)}, u32[]{:S(2)}, u32[]{:S(2)}) collective-permute-start(bf16[128,1408]{1,0:T(8,128)(2,1)} %get-tuple-element.386), channel_id=1, source_target_pairs={{0,1},{1,5},{2,0},{3,4},{4,3},{5,7},{6,2},{7,6},{8,9},{9,13},{10,8... | collective-permute-start | bytes 1081352 | tf_op jit(solution)/shard_map/ppermute | solution.py:818
  222.8 27.2 %collective-permute-start.10 = (bf16[128,1408]{1,0:T(8,128)(2,1)}, bf16[128,1408]{1,0:T(8,128)(2,1)}, u32[]{:S(2)}, u32[]{:S(2)}) collective-permute-start(bf16[128,1408]{1,0:T(8,128)(2,1)} %get-tuple-element.385), channel_id=1, source_target_pairs={{0,5},{1,0},{2,4},{3,1},{4,7},{5,2},{6,6},{7,3},{8,13},{9,8},{10,1... | collective-permute-start | bytes 1081352 | tf_op jit(solution)/shard_map/ppermute | solution.py:818
  224.9 92.8 %collective-permute-start.22 = (bf16[256,1408]{1,0:T(8,128)(2,1)}, bf16[256,1408]{1,0:T(8,128)(2,1)}, u32[]{:S(2)}, u32[]{:S(2)}) collective-permute-start(bf16[256,1408]{1,0:T(8,128)(2,1)} %dynamic-slice_bitcast_fusion), channel_id=1, source_target_pairs={{0,4},{4,0},{1,5},{5,1},{2,6},{6,2},{3,7},{7,3},{8,12},{12,8},{9,1... | collective-permute-start | bytes 2162696 | tf_op jit(solution)/shard_map/ppermute | solution.py:721
  256.2 18.9 %collective-permute-start.19 = (bf16[512,1408]{1,0:T(8,128)(2,1)S(1)}, bf16[512,1408]{1,0:T(8,128)(2,1)S(1)}, u32[]{:S(2)}, u32[]{:S(2)}) collective-permute-start(bf16[512,1408]{1,0:T(8,128)(2,1)S(1)} %fusion.41), channel_id=1, source_target_pairs={{0,4},{4,0},{1,5},{5,1},{2,6},{6,2},{3,7},{7,3},{8,12},{12,8},{9,1... | collective-permute-start | bytes 4325384 | tf_op jit(solution)/shard_map/ppermute | solution.py:721
  405.4 275.1 %reduce-scatter.8.cloned.1.call-start = ((), (), s32[]{:S(2)}) async-start(), calls=%async_computation.6 | async-start | bytes 10813440 | tf_op jit(solution)/shard_map/reduce_scatter | solution.py:879
  522.5 17.9 %collective-permute-start.26 = (bf16[512,1408]{1,0:T(8,128)(2,1)S(1)}, bf16[512,1408]{1,0:T(8,128)(2,1)S(1)}, u32[]{:S(2)}, u32[]{:S(2)}) collective-permute-start(bf16[512,1408]{1,0:T(8,128)(2,1)S(1)} %slice.931), channel_id=1, source_target_pairs={{0,4},{4,0},{1,5},{5,1},{2,6},{6,2},{3,7},{7,3},{8,12},{12,8},{9,1... | collective-permute-start | bytes 4325384 | tf_op jit(solution)/shard_map/ppermute | solution.py:721
  565.5 212.4 %reduce-scatter.10.cloned.1.call-start = ((), (), s32[]{:S(2)}) async-start(), calls=%async_computation.7 | async-start | bytes 9912320 | tf_op jit(solution)/shard_map/reduce_scatter | solution.py:879
  567.9 15.0 %collective-permute-start.35 = (bf16[136,1408]{1,0:T(8,128)(2,1)S(1)}, bf16[136,1408]{1,0:T(8,128)(2,1)S(1)}, u32[]{:S(2)}, u32[]{:S(2)}) collective-permute-start(bf16[136,1408]{1,0:T(8,128)(2,1)S(1)} %get-tuple-element.368), channel_id=1, source_target_pairs={{4,0},{1,1},{5,2},{0,3},{6,4},{3,5},{7,6},{2,7},{12,8},{9,9},{13,1... | collective-permute-start | bytes 1148936 | tf_op jit(solution)/shard_map/ppermute | solution.py:827
  573.9 17.2 %collective-permute-start.36 = (bf16[136,1408]{1,0:T(8,128)(2,1)S(1)}, bf16[136,1408]{1,0:T(8,128)(2,1)S(1)}, u32[]{:S(2)}, u32[]{:S(2)}) collective-permute-start(bf16[136,1408]{1,0:T(8,128)(2,1)S(1)} %get-tuple-element.367), channel_id=1, source_target_pairs={{1,0},{5,1},{0,2},{4,3},{3,4},{7,5},{2,6},{6,7},{9,8},{13,9},{8,10... | collective-permute-start | bytes 1148936 | tf_op jit(solution)/shard_map/ppermute | solution.py:827
  574.1 21.4 %collective-permute-start.37 = (bf16[136,1408]{1,0:T(8,128)(2,1)S(1)}, bf16[136,1408]{1,0:T(8,128)(2,1)S(1)}, u32[]{:S(2)}, u32[]{:S(2)}) collective-permute-start(bf16[136,1408]{1,0:T(8,128)(2,1)S(1)} %get-tuple-element.366), channel_id=1, source_target_pairs={{5,0},{0,1},{4,2},{1,3},{7,4},{2,5},{6,6},{3,7},{13,8},{8,9},{12,1... | collective-permute-start | bytes 1148936 | tf_op jit(solution)/shard_map/ppermute | solution.py:827
  595.9 33.5 %collective-permute-start.28 = (bf16[192,1408]{1,0:T(8,128)(2,1)S(1)}, bf16[192,1408]{1,0:T(8,128)(2,1)S(1)}, u32[]{:S(2)}, u32[]{:S(2)}) collective-permute-start(bf16[192,1408]{1,0:T(8,128)(2,1)S(1)} %get-tuple-element.336), channel_id=1, source_target_pairs={{0,1},{1,2},{2,3},{3,0},{4,5},{5,6},{6,7},{7,4},{8,9},{9,10},{10,1... | collective-permute-start | bytes 1622024 | tf_op jit(solution)/shard_map/ppermute | solution.py:729
  604.6 37.8 %collective-permute-start.29 = (bf16[192,1408]{1,0:T(8,128)(2,1)S(1)}, bf16[192,1408]{1,0:T(8,128)(2,1)S(1)}, u32[]{:S(2)}, u32[]{:S(2)}) collective-permute-start(bf16[192,1408]{1,0:T(8,128)(2,1)S(1)} %get-tuple-element.338), channel_id=1, source_target_pairs={{0,2},{1,3},{2,0},{3,1},{4,6},{5,7},{6,4},{7,5},{8,10},{9,11},{10,... | collective-permute-start | bytes 1622024 | tf_op jit(solution)/shard_map/ppermute | solution.py:729
  608.0 34.3 %collective-permute-start.30 = (bf16[192,1408]{1,0:T(8,128)(2,1)S(1)}, bf16[192,1408]{1,0:T(8,128)(2,1)}, u32[]{:S(2)}, u32[]{:S(2)}) collective-permute-start(bf16[192,1408]{1,0:T(8,128)(2,1)S(1)} %get-tuple-element.337), channel_id=1, source_target_pairs={{0,3},{1,0},{2,1},{3,2},{4,7},{5,4},{6,5},{7,6},{8,11},{9,8},{10,9... | collective-permute-start | bytes 1622024 | tf_op jit(solution)/shard_map/ppermute | solution.py:729
  648.1 14.4 %collective-permute-start.31 = (bf16[512,1408]{1,0:T(8,128)(2,1)S(1)}, bf16[512,1408]{1,0:T(8,128)(2,1)S(1)}, u32[]{:S(2)}, u32[]{:S(2)}) collective-permute-start(bf16[512,1408]{1,0:T(8,128)(2,1)S(1)} %slice.930), channel_id=1, source_target_pairs={{0,4},{4,0},{1,5},{5,1},{2,6},{6,2},{3,7},{7,3},{8,12},{12,8},{9,1... | collective-permute-start | bytes 4325384 | tf_op jit(solution)/shard_map/ppermute | solution.py:721
  684.3 204.1 %reduce-scatter.12.cloned.1.call-start = ((), (), s32[]{:S(2)}) async-start(), calls=%async_computation.8 | async-start | bytes 9912320 | tf_op jit(solution)/shard_map/reduce_scatter | solution.py:879
  696.4 60.5 %collective-permute-start.38 = (bf16[192,1408]{1,0:T(8,128)(2,1)S(1)}, bf16[192,1408]{1,0:T(8,128)(2,1)}, u32[]{:S(2)}, u32[]{:S(2)}) collective-permute-start(bf16[192,1408]{1,0:T(8,128)(2,1)S(1)} %get-tuple-element.333), channel_id=1, source_target_pairs={{0,1},{1,2},{2,3},{3,0},{4,5},{5,6},{6,7},{7,4},{8,9},{9,10},{10,1... | collective-permute-start | bytes 1622024 | tf_op jit(solution)/shard_map/ppermute | solution.py:729
  708.6 48.3 %collective-permute-start.39 = (bf16[192,1408]{1,0:T(8,128)(2,1)S(1)}, bf16[192,1408]{1,0:T(8,128)(2,1)}, u32[]{:S(2)}, u32[]{:S(2)}) collective-permute-start(bf16[192,1408]{1,0:T(8,128)(2,1)S(1)} %get-tuple-element.335), channel_id=1, source_target_pairs={{0,2},{1,3},{2,0},{3,1},{4,6},{5,7},{6,4},{7,5},{8,10},{9,11},{10,... | collective-permute-start | bytes 1622024 | tf_op jit(solution)/shard_map/ppermute | solution.py:729
  710.3 46.6 %collective-permute-start.40 = (bf16[192,1408]{1,0:T(8,128)(2,1)S(1)}, bf16[192,1408]{1,0:T(8,128)(2,1)}, u32[]{:S(2)}, u32[]{:S(2)}) collective-permute-start(bf16[192,1408]{1,0:T(8,128)(2,1)S(1)} %get-tuple-element.334), channel_id=1, source_target_pairs={{0,3},{1,0},{2,1},{3,2},{4,7},{5,4},{6,5},{7,6},{8,11},{9,8},{10,9... | collective-permute-start | bytes 1622024 | tf_op jit(solution)/shard_map/ppermute | solution.py:729
  777.9 192.7 %all-gather.14.cloned.1.call-start = ((), (), s32[]{:S(2)}) async-start(), calls=%async_computation.9 | async-start | bytes 7884800 | tf_op jit(solution)/shard_map/all_gather | solution.py:893
  801.2 12.7 %collective-permute-start.43 = (bf16[128,1408]{1,0:T(8,128)(2,1)S(1)}, bf16[128,1408]{1,0:T(8,128)(2,1)S(1)}, u32[]{:S(2)}, u32[]{:S(2)}) collective-permute-start(bf16[128,1408]{1,0:T(8,128)(2,1)S(1)} %get-tuple-element.378), channel_id=1, source_target_pairs={{4,0},{1,1},{5,2},{0,3},{6,4},{3,5},{7,6},{2,7},{12,8},{9,9},{13,1... | collective-permute-start | bytes 1081352 | tf_op jit(solution)/shard_map/ppermute | solution.py:827
  807.0 14.6 %collective-permute-start.44 = (bf16[128,1408]{1,0:T(8,128)(2,1)S(1)}, bf16[128,1408]{1,0:T(8,128)(2,1)S(1)}, u32[]{:S(2)}, u32[]{:S(2)}) collective-permute-start(bf16[128,1408]{1,0:T(8,128)(2,1)S(1)} %get-tuple-element.377), channel_id=1, source_target_pairs={{1,0},{5,1},{0,2},{4,3},{3,4},{7,5},{2,6},{6,7},{9,8},{13,9},{8,10... | collective-permute-start | bytes 1081352 | tf_op jit(solution)/shard_map/ppermute | solution.py:827
  807.0 20.3 %collective-permute-start.45 = (bf16[128,1408]{1,0:T(8,128)(2,1)S(1)}, bf16[128,1408]{1,0:T(8,128)(2,1)S(1)}, u32[]{:S(2)}, u32[]{:S(2)}) collective-permute-start(bf16[128,1408]{1,0:T(8,128)(2,1)S(1)} %get-tuple-element.376), channel_id=1, source_target_pairs={{5,0},{0,1},{4,2},{1,3},{7,4},{2,5},{6,6},{3,7},{13,8},{8,9},{12,1... | collective-permute-start | bytes 1081352 | tf_op jit(solution)/shard_map/ppermute | solution.py:827
  834.2 46.6 %collective-permute-start.49 = (bf16[1408,1408]{1,0:T(8,128)(2,1)}, bf16[1408,1408]{1,0:T(8,128)(2,1)}, u32[]{:S(2)}, u32[]{:S(2)}) collective-permute-start(bf16[1408,1408]{1,0:T(8,128)(2,1)} %convolution_convert_fusion.2), channel_id=1, source_target_pairs={{0,4},{4,0},{1,5},{5,1},{2,6},{6,2},{3,7},{7,3},{8,12},{12,8},{9,1... | collective-permute-start | bytes 11894792 | tf_op jit(solution)/shard_map/ppermute | solution.py:721
  842.8 16.2 %collective-permute-start.46 = (bf16[176,1408]{1,0:T(8,128)(2,1)S(1)}, bf16[176,1408]{1,0:T(8,128)(2,1)S(1)}, u32[]{:S(2)}, u32[]{:S(2)}) collective-permute-start(bf16[176,1408]{1,0:T(8,128)(2,1)S(1)} %get-tuple-element.358), channel_id=1, source_target_pairs={{0,1},{1,2},{2,3},{3,0},{4,5},{5,6},{6,7},{7,4},{8,9},{9,10},{10,1... | collective-permute-start | bytes 1486856 | tf_op jit(solution)/shard_map/ppermute | solution.py:729
  844.1 35.2 %collective-permute-start.47 = (bf16[176,1408]{1,0:T(8,128)(2,1)S(1)}, bf16[176,1408]{1,0:T(8,128)(2,1)S(1)}, u32[]{:S(2)}, u32[]{:S(2)}) collective-permute-start(bf16[176,1408]{1,0:T(8,128)(2,1)S(1)} %get-tuple-element.360), channel_id=1, source_target_pairs={{0,2},{1,3},{2,0},{3,1},{4,6},{5,7},{6,4},{7,5},{8,10},{9,11},{10,... | collective-permute-start | bytes 1486856 | tf_op jit(solution)/shard_map/ppermute | solution.py:729
  846.5 32.8 %collective-permute-start.48 = (bf16[176,1408]{1,0:T(8,128)(2,1)S(1)}, bf16[176,1408]{1,0:T(8,128)(2,1)S(1)}, u32[]{:S(2)}, u32[]{:S(2)}) collective-permute-start(bf16[176,1408]{1,0:T(8,128)(2,1)S(1)} %get-tuple-element.359), channel_id=1, source_target_pairs={{0,3},{1,0},{2,1},{3,2},{4,7},{5,4},{6,5},{7,6},{8,11},{9,8},{10,9... | collective-permute-start | bytes 1486856 | tf_op jit(solution)/shard_map/ppermute | solution.py:729
  888.5 143.5 %reduce-scatter.14.cloned.1.call-start = ((), (), s32[]{:S(2)}) async-start(), calls=%async_computation.10 | async-start | bytes 5406720 | tf_op jit(solution)/shard_map/reduce_scatter | solution.py:1270
  898.2 14.2 %collective-permute-start.51 = (f32[1408]{0:T(1024)S(1)}, f32[1408]{0:T(1024)S(1)}, u32[]{:S(2)}, u32[]{:S(2)}) collective-permute-start(f32[1408]{0:T(1024)S(1)} %add.884), channel_id=1, source_target_pairs={{0,3},{1,0},{2,1},{3,2},{4,7},{5,4},{6,5},{7,6},{8,11},{9,8},{10,9... | collective-permute-start | bytes 16904 | tf_op jit(solution)/shard_map/ppermute | solution.py:725
  933.7 16.2 %collective-permute-start.54 = (bf16[176,1408]{1,0:T(8,128)(2,1)S(1)}, bf16[176,1408]{1,0:T(8,128)(2,1)S(1)}, u32[]{:S(2)}, u32[]{:S(2)}) collective-permute-start(bf16[176,1408]{1,0:T(8,128)(2,1)S(1)} %get-tuple-element.355), channel_id=1, source_target_pairs={{0,1},{1,2},{2,3},{3,0},{4,5},{5,6},{6,7},{7,4},{8,9},{9,10},{10,1... | collective-permute-start | bytes 1486856 | tf_op jit(solution)/shard_map/ppermute | solution.py:729
  933.8 34.7 %collective-permute-start.55 = (bf16[176,1408]{1,0:T(8,128)(2,1)S(1)}, bf16[176,1408]{1,0:T(8,128)(2,1)S(1)}, u32[]{:S(2)}, u32[]{:S(2)}) collective-permute-start(bf16[176,1408]{1,0:T(8,128)(2,1)S(1)} %get-tuple-element.357), channel_id=1, source_target_pairs={{0,2},{1,3},{2,0},{3,1},{4,6},{5,7},{6,4},{7,5},{8,10},{9,11},{10,... | collective-permute-start | bytes 1486856 | tf_op jit(solution)/shard_map/ppermute | solution.py:729
  934.6 34.0 %collective-permute-start.56 = (bf16[176,1408]{1,0:T(8,128)(2,1)S(1)}, bf16[176,1408]{1,0:T(8,128)(2,1)S(1)}, u32[]{:S(2)}, u32[]{:S(2)}) collective-permute-start(bf16[176,1408]{1,0:T(8,128)(2,1)S(1)} %get-tuple-element.356), channel_id=1, source_target_pairs={{0,3},{1,0},{2,1},{3,2},{4,7},{5,4},{6,5},{7,6},{8,11},{9,8},{10,9... | collective-permute-start | bytes 1486856 | tf_op jit(solution)/shard_map/ppermute | solution.py:729
  970.6 99.3 %all-gather.16.cloned.1.call-start = ((), (), s32[]{:S(2)}) async-start(), calls=%async_computation.11 | async-start | bytes 2478080 | tf_op jit(solution)/shard_map/all_gather | solution.py:893
  980.5 24.8 %collective-permute-start.58 = (bf16[128,1408]{1,0:T(8,128)(2,1)S(1)}, bf16[128,1408]{1,0:T(8,128)(2,1)S(1)}, u32[]{:S(2)}, u32[]{:S(2)}) collective-permute-start(bf16[128,1408]{1,0:T(8,128)(2,1)S(1)} %copy-done.109), channel_id=1, source_target_pairs={{0,0},{1,2},{2,4},{3,6},{4,1},{5,3},{6,5},{7,7},{8,8},{9,10},{10,1... | collective-permute-start | bytes 1081352 | tf_op jit(solution)/shard_map/ppermute | solution.py:1263
  981.2 34.8 %collective-permute-start.59 = (bf16[128,1408]{1,0:T(8,128)(2,1)S(1)}, bf16[128,1408]{1,0:T(8,128)(2,1)S(1)}, u32[]{:S(2)}, u32[]{:S(2)}) collective-permute-start(bf16[128,1408]{1,0:T(8,128)(2,1)S(1)} %copy-done.109), channel_id=1, source_target_pairs={{0,1},{1,3},{2,5},{3,7},{4,2},{5,0},{6,6},{7,4},{8,9},{9,11},{10,1... | collective-permute-start | bytes 1081352 | tf_op jit(solution)/shard_map/ppermute | solution.py:1263
  995.4 20.6 %collective-permute-start.60 = (bf16[128,1408]{1,0:T(8,128)(2,1)S(1)}, bf16[128,1408]{1,0:T(8,128)(2,1)S(1)}, u32[]{:S(2)}, u32[]{:S(2)}) collective-permute-start(bf16[128,1408]{1,0:T(8,128)(2,1)S(1)} %copy-done.109), channel_id=1, source_target_pairs={{0,2},{1,0},{2,6},{3,4},{4,3},{5,1},{6,7},{7,5},{8,10},{9,8},{10,1... | collective-permute-start | bytes 1081352 | tf_op jit(solution)/shard_map/ppermute | solution.py:1263
  997.3 19.9 %collective-permute-start.61 = (bf16[128,1408]{1,0:T(8,128)(2,1)S(1)}, bf16[128,1408]{1,0:T(8,128)(2,1)S(1)}, u32[]{:S(2)}, u32[]{:S(2)}) collective-permute-start(bf16[128,1408]{1,0:T(8,128)(2,1)S(1)} %copy-done.109), channel_id=1, source_target_pairs={{0,3},{1,1},{2,7},{3,5},{4,0},{5,2},{6,4},{7,6},{8,11},{9,9},{10,1... | collective-permute-start | bytes 1081352 | tf_op jit(solution)/shard_map/ppermute | solution.py:1263
  1002.8 16.7 %collective-permute-start.67 = (bf16[4,176,1408]{2,1,0:T(8,128)(2,1)S(1)}, bf16[4,176,1408]{2,1,0:T(8,128)(2,1)S(1)}, u32[]{:S(2)}, u32[]{:S(2)}) collective-permute-start(bf16[4,176,1408]{2,1,0:T(8,128)(2,1)S(1)} %slice.773), channel_id=1, source_target_pairs={{0,4},{4,0},{1,5},{5,1},{2,6},{6,2},{3,7},{7,3},{8,12},{12,8},{9,1... | collective-permute-start | bytes 5947400 | tf_op jit(solution)/shard_map/ppermute | solution.py:721
  1005.3 80.0 %collective-permute-start.69 = (bf16[768,1408]{1,0:T(8,128)(2,1)}, bf16[768,1408]{1,0:T(8,128)(2,1)}, u32[]{:S(2)}, u32[]{:S(2)}) collective-permute-start(bf16[768,1408]{1,0:T(8,128)(2,1)} %bitcast.233), channel_id=1, source_target_pairs={{0,4},{4,0},{1,5},{5,1},{2,6},{6,2},{3,7},{7,3},{8,12},{12,8},{9,1... | collective-permute-start | bytes 6488072 | tf_op jit(solution)/shard_map/ppermute | solution.py:721
  1016.0 21.6 %collective-permute-start.68 = (bf16[768,1408]{1,0:T(8,128)(2,1)}, bf16[768,1408]{1,0:T(8,128)(2,1)}, u32[]{:S(2)}, u32[]{:S(2)}) collective-permute-start(bf16[768,1408]{1,0:T(8,128)(2,1)} %bitcast.230), channel_id=1, source_target_pairs={{0,4},{4,0},{1,5},{5,1},{2,6},{6,2},{3,7},{7,3},{8,12},{12,8},{9,1... | collective-permute-start | bytes 6488072 | tf_op jit(solution)/shard_map/ppermute | solution.py:721
  1034.1 26.8 %collective-permute-start.63 = (bf16[120,1408]{1,0:T(8,128)(2,1)S(1)}, bf16[120,1408]{1,0:T(8,128)(2,1)S(1)}, u32[]{:S(2)}, u32[]{:S(2)}) collective-permute-start(bf16[120,1408]{1,0:T(8,128)(2,1)S(1)} %get-tuple-element.402), channel_id=1, source_target_pairs={{0,2},{1,3},{2,0},{3,1},{4,6},{5,7},{6,4},{7,5},{8,10},{9,11},{10,... | collective-permute-start | bytes 1013768 | tf_op jit(solution)/shard_map/ppermute | solution.py:729
  1037.6 81.9 %all-gather.18.cloned.1.call-start = ((), (), s32[]{:S(2)}) async-start(), calls=%async_computation.12 | async-start | bytes 1689600 | tf_op jit(solution)/shard_map/all_gather | solution.py:893
  1042.5 18.4 %collective-permute-start.62 = (bf16[120,1408]{1,0:T(8,128)(2,1)S(1)}, bf16[120,1408]{1,0:T(8,128)(2,1)S(1)}, u32[]{:S(2)}, u32[]{:S(2)}) collective-permute-start(bf16[120,1408]{1,0:T(8,128)(2,1)S(1)} %get-tuple-element.401), channel_id=1, source_target_pairs={{0,1},{1,2},{2,3},{3,0},{4,5},{5,6},{6,7},{7,4},{8,9},{9,10},{10,1... | collective-permute-start | bytes 1013768 | tf_op jit(solution)/shard_map/ppermute | solution.py:729
  1043.9 22.4 %collective-permute-start.64 = (bf16[120,1408]{1,0:T(8,128)(2,1)S(1)}, bf16[120,1408]{1,0:T(8,128)(2,1)S(1)}, u32[]{:S(2)}, u32[]{:S(2)}) collective-permute-start(bf16[120,1408]{1,0:T(8,128)(2,1)S(1)} %concatenate.225), channel_id=1, source_target_pairs={{0,3},{1,0},{2,1},{3,2},{4,7},{5,4},{6,5},{7,6},{8,11},{9,8},{10,9... | collective-permute-start | bytes 1013768 | tf_op jit(solution)/shard_map/ppermute | solution.py:729
  1069.9 26.6 %collective-permute-start.66 = (bf16[704,1408]{1,0:T(8,128)(2,1)}, bf16[704,1408]{1,0:T(8,128)(2,1)}, u32[]{:S(2)}, u32[]{:S(2)}) collective-permute-start(bf16[704,1408]{1,0:T(8,128)(2,1)} %all-gather.16.cloned.1.call-done), channel_id=1, source_target_pairs={{0,4},{4,0},{1,5},{5,1},{2,6},{6,2},{3,7},{7,3},{8,12},{12,8},{9,1... | collective-permute-start | bytes 5947400 | tf_op jit(solution)/shard_map/ppermute | solution.py:721
  (193 other events, 2405.4 us)
Sparse Core Ops, SparseCore 0:
  42.4 50.5 all-gather.19
  96.2 66.4 all-gather.21
  165.1 67.2 all-gather.23
  235.6 117.8 all-gather.25
  356.2 113.4 all-gather.27
  472.6 86.7 reduce-scatter.5
  565.6 86.8 reduce-scatter.7
  684.4 92.4 reduce-scatter.9
  780.7 82.6 reduce-scatter.11
  888.6 79.6 all-gather.13
  971.9 60.0 reduce-scatter.13
  1037.7 32.1 all-gather.15
  1090.2 29.2 all-gather.17
